TPU v7x, 128 devices: a whole 4x4x4 slice. The times are simulated.
128 devices in a mesh: rep: 32 (over y, z, core), shard: 4 (over x).
Axes of the slice: x: 4, y: 4, z: 4, core: 2. Of those that a mesh axis runs over, the one named last changes fastest.
Arguments:
- hidden: bfloat16 [128, 256, 768], P('rep', 'shard'), may hold values from -6 to 6
- grad_out: bfloat16 [128, 256, 768], P('rep', 'shard'), may hold values from -6 to 6
- lengths: int32 [128], P('rep'), may hold values from 1 to 256, 20480 in all
- bucket: int32 [511], replicated, may hold values from 1 to 511, as said below
- w_query: bfloat16 [768, 768], P('shard'), may hold values from -0.21875 to 0.21875
- w_key: bfloat16 [768, 768], P('shard'), may hold values from -0.21875 to 0.21875
- w_value: bfloat16 [768, 768], P('shard'), may hold values from -0.21875 to 0.21875
- w_out: bfloat16 [768, 768], P('shard'), may hold values from -1.25 to 1.25
- w_inner: bfloat16 [768, 3072], P('shard'), may hold values from -0.21875 to 0.21875
- w_outer: bfloat16 [3072, 768], P('shard'), may hold values from -0.109375 to 0.109375
- rel_table: bfloat16 [512, 768], P('shard'), may hold values from -6 to 6
- ln1_gain: bfloat16 [768], P('shard'), may hold values from 0.5 to 1.5
- ln1_bias: bfloat16 [768], P('shard'), may hold values from -1.5 to 1.5
- ln2_gain: bfloat16 [768], P('shard'), may hold values from 0.5 to 1.5
- ln2_bias: bfloat16 [768], P('shard'), may hold values from -1.5 to 1.5
Outputs:
- layer_output: bfloat16 [128, 256, 768], P('rep', 'shard')
- grad_hidden: bfloat16 [128, 256, 768], P('rep', 'shard')
- grad_w_query: float32 [768, 768], P('shard')
- grad_w_key: float32 [768, 768], P('shard')
- grad_w_value: float32 [768, 768], P('shard')
- grad_w_out: float32 [768, 768], P('shard')
- grad_w_inner: float32 [768, 3072], P('shard')
- grad_w_outer: float32 [3072, 768], P('shard')
- grad_rel_table: float32 [512, 768], P('shard')
- grad_ln1_gain: float32 [768], P('shard')
- grad_ln1_bias: float32 [768], P('shard')
- grad_ln2_gain: float32 [768], P('shard')
- grad_ln2_bias: float32 [768], P('shard')
- rms_values: float32 [4], replicated
Inputs may be any that keep to these rules, and one draw needn't show every extreme that they name: bucket[255 + d] = 256 + d for |d| < 128; beyond that it moves away from 256 monotonically with |d|, symmetric in the sign of d, several offsets sharing a row.
All inputs are finite; a program needn't handle non-finite values. No bound on the sum of `lengths` on one device may be relied on, other than what follows from the above.
Results may differ from a plain program's by a relative error of at most 0.028.
Values may be sent and summed in bfloat16 or wider, within the bound.
No kernel may reach another device: no remote copies, remote signals or barrier semaphores. Data moves between devices by JAX's collectives and lax.ppermute only.
A program may use at most 192 MiB of HBM per device.

v0:
```python
import jax
import jax.numpy as jnp
from jax import lax
from jax.experimental import pallas as pl
from jax.experimental.pallas import tpu as pltpu
from jax.sharding import Mesh
from jax.sharding import PartitionSpec as P

D = 768
HEADS = 12
HEAD_DIM = 64
PAIRS = HEADS // 2
ROWS = 256
OFFS = 512
TOKENS = 20480
GROUP = 4
PIECE = D // GROUP
HALF = PIECE // 2
WIDE = GROUP * D
REL_HALF = OFFS // GROUP // 2
REL_AT = 3 * HALF
FIRST = 3 * HALF + REL_HALF
OUT_AT = D // 2
NORM_AT = D // 2 + HALF
QUARTER = 128
SECOND = GROUP * QUARTER
SPAN = QUARTER + HALF
PART = ROWS // GROUP
X, Y, Z, CORE, LENGTH, SEQ = 0, 1, 2, 3, 4, 5
META = 16
EPSILON = 1e-07
MASKED = -1e30
SCALING = (3.0 * HEAD_DIM) ** (-0.5)
F32 = jnp.float32
LOW = jnp.bfloat16
MIB = 1024 * 1024


def mm(a, b):
    return lax.dot_general(a, b, (((1,), (0,)), ((), ())), preferred_element_type=F32)


def mm_nt(a, b):
    return lax.dot_general(a, b, (((1,), (1,)), ((), ())), preferred_element_type=F32)


def mm_tn(a, b):
    return lax.dot_general(a, b, (((0,), (0,)), ((), ())), preferred_element_type=F32)


def iota(shape, dim):
    return lax.broadcasted_iota(jnp.int32, shape, dim)


def whole(ref, start, size):
    piece = ref[:, :, start : start + size, :]
    return piece.reshape(GROUP * 2 * size, piece.shape[3])


def run_copies(copies):
    for copy in copies:
        copy.start()
    for copy in copies:
        copy.wait()


class Copies:
    def __init__(self, sem):
        self.sem, self.made = sem, []

    def add(self, source, target):
        self.made.append(pltpu.make_async_copy(source, target, self.sem.at[len(self.made)]))

    def start(self):
        for copy in self.made:
            copy.start()

    def wait(self):
        for copy in self.made:
            copy.wait()


def near_of(core):
    return 1 + 2 * core


def far_of(core):
    return 3 - 2 * core


def assist_of(meta_ref, core):
    return jnp.where(core == 0, meta_ref[Y], meta_ref[Z])


def position(distance, near):
    far = 4 - near
    place = jnp.where(distance == near, 1, jnp.where(distance == far, 2, 0))
    return jnp.where(distance == 0, 3, place)


def pack_body(
    coord_ref, length_ref, hidden_ref, grad_ref, own_q, own_k, own_v, own_rel, own_outer, own_out, own_inner, norm_ref,
    meta_ref, first_ref, second_ref, *rest,
):
    rows_out, sem, tail_sem = rest
    x, y, z, core = (coord_ref[i] for i in range(4))
    for i in range(4):
        meta_ref[i] = coord_ref[i]
    lengths = [length_ref[i] for i in range(GROUP)]
    dealing = []
    for i in range(GROUP):
        rank = jnp.int32(0)
        for j in range(GROUP):
            if j != i:
                ahead = lengths[j] >= lengths[i] if j < i else lengths[j] > lengths[i]
                rank = rank + ahead.astype(jnp.int32)
        dealing.append(rank)
    length = jnp.int32(0)
    for i in range(GROUP):
        length = length + jnp.where(dealing[i] == x, lengths[i], 0)
    meta_ref[LENGTH] = length
    copies = Copies(sem)
    for k in range(GROUP):
        source = jnp.int32(0)
        for i in range(GROUP):
            source = source + jnp.where(dealing[i] == (x ^ k), i, 0)
        meta_ref[SEQ + k] = source
        copies.add(hidden_ref.at[source], rows_out.at[x ^ k, 0])
        copies.add(grad_ref.at[source], rows_out.at[x ^ k, 1])
    for i in range(SEQ + GROUP, META):
        meta_ref[i] = jnp.int32(0)
    for i, ref in enumerate((own_q, own_k, own_v, own_rel)):
        size = REL_HALF if i == 3 else HALF
        copies.add(ref.at[pl.ds(core * size, size)], first_ref.at[pl.ds(i * HALF, size)])
    quarter = jnp.where(core == 0, y, z)
    copies.add(
        own_inner.at[pl.ds(core * HALF, HALF), pl.ds(pl.multiple_of(quarter * D, D), D)],
        second_ref.at[pl.ds(QUARTER, HALF)],
    )
    copies.start()
    tail = Copies(tail_sem)

    @pl.when(quarter < 3)
    def _():
        copy = pltpu.make_async_copy(
            own_outer.at[pl.ds(core * 3 * QUARTER + quarter * QUARTER, QUARTER)], second_ref.at[pl.ds(0, QUARTER)],
            tail_sem.at[0],
        )
        copy.start()
        copy.wait()

    @pl.when(quarter == 3)
    def _():
        tail.add(own_out.at[pl.ds(core * HALF, HALF)], second_ref.at[pl.ds(0, HALF)])
        tail.add(norm_ref, second_ref.at[pl.ds(HALF, QUARTER - HALF)])
        tail.start()
        tail.wait()

    copies.wait()


def pack(coords, lengths, hidden, grad_out, own_first, own_second, norm_block):
    shape = jax.ShapeDtypeStruct
    scalars, anywhere = pl.BlockSpec(memory_space=pltpu.SMEM), pl.BlockSpec(memory_space=pltpu.HBM)
    full = pl.BlockSpec(memory_space=pltpu.VMEM)
    return pl.pallas_call(
        pack_body,
        out_shape=(
            shape((META,), jnp.int32), shape((FIRST, D), LOW), shape((SPAN, D), LOW), shape((GROUP, 2, PART, D), LOW),
        ),
        in_specs=[scalars, scalars] + [anywhere] * 10,
        out_specs=(scalars, full, full, full),
        scratch_shapes=[pltpu.SemaphoreType.DMA((13,)), pltpu.SemaphoreType.DMA((2,))],
        compiler_params=pltpu.CompilerParams(vmem_limit_bytes=60 * MIB),
        name="pack",
    )(coords, lengths, hidden, grad_out, *own_first, *own_second, norm_block)


def load_first(meta_ref, copies, own, pieces, w_ref):
    x, core = meta_ref[X], meta_ref[CORE]
    near, far = x ^ near_of(core), x ^ far_of(core)
    slots = ((near, core), (far, core), (x ^ 2, core), (far, 1 - core), (near, 1 - core), (x ^ 2, 1 - core))
    for piece, (slot, half) in zip(pieces, slots):
        copies.add(piece, w_ref.at[slot, half])
    for i, ref in enumerate(own):
        size = REL_HALF if i == 3 else HALF
        copies.add(ref, w_ref.at[x, :, pl.ds(i * HALF, size)])


def load_second(meta_ref, copies, own, pieces, w_ref, in_ref):
    own_outer, own_out, own_norm, own_inner = own
    for side in range(2):
        assist = assist_of(meta_ref, meta_ref[CORE] if side == 0 else 1 - meta_ref[CORE])
        base, near, far, across_outer, across_inner = pieces[5 * side : 5 * side + 5]
        for distance, outer, inner in (
            (0, base.at[:, pl.ds(0, QUARTER)], base.at[:, pl.ds(QUARTER, HALF)]),
            (1, near.at[:, pl.ds(0, QUARTER)], near.at[:, pl.ds(QUARTER, HALF)]),
            (3, far.at[:, pl.ds(0, QUARTER)], far.at[:, pl.ds(QUARTER, HALF)]),
            (2, across_outer, across_inner),
        ):
            quarter = assist ^ distance
            copies.add(outer, w_ref.at[side, pl.ds(0, 3), pl.ds(quarter * QUARTER, QUARTER)])
            copies.add(inner, in_ref.at[side, pl.ds(0, 3), :, pl.ds(pl.multiple_of(quarter * D, D), D)])
    for half in range(2):
        side = half ^ meta_ref[CORE]
        copies.add(own_outer.at[pl.ds(half * 3 * QUARTER, 3 * QUARTER)], w_ref.at[side, 3, pl.ds(0, 3 * QUARTER)])
        copies.add(own_out.at[pl.ds(half * HALF, HALF)], w_ref.at[side, 3, pl.ds(OUT_AT, HALF)])
        copies.add(own_inner.at[pl.ds(half * HALF, HALF)], in_ref.at[side, 3])
    copies.add(own_norm, w_ref.at[meta_ref[CORE], 3, pl.ds(NORM_AT, QUARTER - HALF)])


def second_block(meta_ref, shard, half):
    apart = meta_ref[X] ^ shard
    place = jnp.where(apart == near_of(half), 0, jnp.where(apart == far_of(half), 1, 2))
    return half ^ meta_ref[CORE], jnp.where(apart == 0, 3, place)


def select_halves(meta_ref, value):
    half = value.shape[0] // 2
    low, high = value[:half].astype(LOW), value[half:].astype(LOW)
    first_core = meta_ref[CORE] == 0
    return jnp.where(first_core, low, high), jnp.where(first_core, high, low)


def heads_forward(meta_ref, first_pair, refs, probs_ref, ctx_ref):
    q_ref, k_ref, v_ref, pk_ref, pq_ref = refs
    length = meta_ref[LENGTH]
    valid = iota((ROWS, ROWS), 1) < length
    side = iota((ROWS, 2 * HEAD_DIM), 1) // HEAD_DIM

    def pair_step(pair, carry):
        out_cols = pl.ds(pl.multiple_of((pair - first_pair) * 2 * HEAD_DIM, 2 * HEAD_DIM), 2 * HEAD_DIM)
        cols = pl.ds(pl.multiple_of(pair * 2 * HEAD_DIM, 2 * HEAD_DIM), 2 * HEAD_DIM)
        q_pair, k_pair, v_pair = q_ref[:, cols], k_ref[:, cols], v_ref[:, cols]
        pk_pair, pq_pair = pk_ref[:, cols], pq_ref[:, cols]
        zero = jnp.zeros_like(q_pair)
        contexts = []
        for h in range(2):
            mine = side == h
            q_head = jnp.where(mine, q_pair, zero)
            k_head = jnp.where(mine, k_pair, zero)
            content = mm_nt(q_head, k_pair)
            to_off = mm_nt(q_head, pk_pair)
            from_off = mm_nt(k_head, pq_pair)
            to_rel = pltpu.roll(to_off, ROWS + 1, 1, stride=1, stride_axis=0)[:, :ROWS]
            from_rel = pltpu.roll(from_off, ROWS + 1, 1, stride=1, stride_axis=0)[:, :ROWS]
            scores = (content + to_rel + from_rel.T) * SCALING
            scores = jnp.where(valid, scores, MASKED)
            top = jnp.max(scores, axis=1, keepdims=True)
            shifted = jnp.exp(scores - top)
            summed = jnp.sum(shifted, axis=1, keepdims=True)
            probs = (shifted * (1.0 / summed)).astype(LOW)
            probs_ref[2 * (pair - first_pair) + h] = probs
            contexts.append(mm(probs, v_pair))
        ctx_ref[:, out_cols] = jnp.where(side == 0, contexts[0], contexts[1]).astype(LOW)
        return carry

    lax.fori_loop(first_pair, first_pair + PAIRS // 2, pair_step, 0)


def attend_forward_body(
    meta_ref, bucket_ref, rows_ref, own_q, own_k, own_v, own_rel, p0, p1, p2, p3, p4, p5,
    tok_ref, q_ref, k_ref, v_ref, pk_ref, pq_ref, relw_ref, probs_ref, ctx_ref,
    w_ref, rows_in, sem,
):
    copies = Copies(sem)
    copies.add(rows_ref.at[:, 0], rows_in)
    load_first(meta_ref, copies, (own_q, own_k, own_v, own_rel), (p0, p1, p2, p3, p4, p5), w_ref)
    copies.start()
    copies.wait()
    tok = rows_in[...].reshape(ROWS, D)
    tok_ref[...] = tok
    rel = whole(w_ref, REL_AT, REL_HALF)
    pick = (bucket_ref[...] == iota((OFFS, OFFS), 1)).astype(LOW)
    relw = mm(pick, rel).astype(LOW)
    relw_ref[...] = relw
    w_query = whole(w_ref, 0, HALF)
    q_ref[...] = mm(tok, w_query).astype(LOW)
    pq_ref[...] = mm(relw, w_query).astype(LOW)
    w_key = whole(w_ref, HALF, HALF)
    k_ref[...] = mm(tok, w_key).astype(LOW)
    pk_ref[...] = mm(relw, w_key).astype(LOW)
    v_ref[...] = mm(tok, whole(w_ref, 2 * HALF, HALF)).astype(LOW)
    heads_forward(meta_ref, 0, (q_ref, k_ref, v_ref, pk_ref, pq_ref), probs_ref, ctx_ref)


def attend_forward_two_body(meta_ref, q_ref, k_ref, v_ref, pk_ref, pq_ref, probs_ref, ctx_ref):
    heads_forward(meta_ref, PAIRS // 2, (q_ref, k_ref, v_ref, pk_ref, pq_ref), probs_ref, ctx_ref)


def attend_forward(meta, bucket_column, rows, own, pieces):
    shape = jax.ShapeDtypeStruct
    full, anywhere = pl.BlockSpec(memory_space=pltpu.VMEM), pl.BlockSpec(memory_space=pltpu.HBM)
    return pl.pallas_call(
        attend_forward_body,
        out_shape=(
            *(shape((ROWS, D), LOW),) * 4,
            shape((OFFS, D), LOW), shape((OFFS, D), LOW), shape((OFFS, D), LOW),
            shape((HEADS // 2, ROWS, ROWS), LOW), shape((ROWS, D // 2), LOW),
        ),
        in_specs=[pl.BlockSpec(memory_space=pltpu.SMEM), full] + [anywhere] * 11,
        out_specs=(full,) * 9,
        scratch_shapes=[
            pltpu.VMEM((GROUP, 2, FIRST, D), LOW), pltpu.VMEM((GROUP, PART, D), LOW), pltpu.SemaphoreType.DMA((11,)),
        ],
        compiler_params=pltpu.CompilerParams(vmem_limit_bytes=28 * MIB),
        cost_estimate=pl.CostEstimate(flops=12_000_000_000, bytes_accessed=40_000_000, transcendentals=800_000),
        name="attend_forward",
    )(meta, bucket_column, rows, *own, *pieces)


def attend_forward_two(meta, saved):
    shape = jax.ShapeDtypeStruct
    full = pl.BlockSpec(memory_space=pltpu.VMEM)
    return pl.pallas_call(
        attend_forward_two_body,
        out_shape=(shape((HEADS // 2, ROWS, ROWS), LOW), shape((ROWS, D // 2), LOW)),
        in_specs=[pl.BlockSpec(memory_space=pltpu.SMEM)] + [full] * 5,
        out_specs=(full,) * 2,
        compiler_params=pltpu.CompilerParams(vmem_limit_bytes=24 * MIB),
        cost_estimate=pl.CostEstimate(flops=8_000_000_000, bytes_accessed=20_000_000, transcendentals=400_000),
        name="attend_forward_two",
    )(meta, *saved)


def heads_back(first_pair, count, refs, outs):
    q_ref, k_ref, v_ref, pk_ref, pq_ref, probs_ref, gctx_ref = refs
    gq_ref, gk_ref, gv_ref, gpk_ref, gpq_ref, qr_ref, kr_ref = outs
    flip = (iota((ROWS, ROWS), 0) + iota((ROWS, ROWS), 1) == ROWS - 1).astype(LOW)
    qr_ref[...] = mm(flip, q_ref[...]).astype(LOW)
    kr_ref[...] = mm(flip, k_ref[...]).astype(LOW)
    side = iota((ROWS, 2 * HEAD_DIM), 1) // HEAD_DIM
    side_off = iota((OFFS, 2 * HEAD_DIM), 1) // HEAD_DIM
    blank = jnp.zeros((ROWS, OFFS - ROWS), F32)

    def pair_step(pair, carry):
        cols = pl.ds(pl.multiple_of(pair * 2 * HEAD_DIM, 2 * HEAD_DIM), 2 * HEAD_DIM)
        q_pair, k_pair, v_pair = q_ref[:, cols], k_ref[:, cols], v_ref[:, cols]
        pk_pair, pq_pair, gctx_pair = pk_ref[:, cols], pq_ref[:, cols], gctx_ref[:, cols]
        qr_pair, kr_pair = qr_ref[:, cols], kr_ref[:, cols]
        zero = jnp.zeros_like(q_pair)
        parts = []
        for h in range(2):
            gctx_head = jnp.where(side == h, gctx_pair, zero)
            grad_probs = mm_nt(gctx_head, v_pair)
            probs_low = probs_ref[2 * (pair - first_pair) + h]
            probs = probs_low.astype(F32)
            inner = jnp.sum(probs * grad_probs, axis=1, keepdims=True)
            grad_scores = (probs * (grad_probs - inner)).astype(LOW)
            g_value = mm_tn(probs_low, gctx_pair)
            rows_back = mm(flip, grad_scores)
            cols_back = mm_nt(flip, grad_scores)
            to_off = pltpu.roll(jnp.concatenate([rows_back, blank], axis=1), 0, 1, stride=1, stride_axis=0).astype(LOW)
            from_off = pltpu.roll(jnp.concatenate([cols_back, blank], axis=1), 0, 1, stride=1, stride_axis=0).astype(LOW)
            g_query = mm(rows_back.astype(LOW), k_pair) + mm(to_off, pk_pair)
            g_key = mm(cols_back.astype(LOW), q_pair) + mm(from_off, pq_pair)
            g_pk = mm_tn(to_off, qr_pair)
            g_pq = mm_tn(from_off, kr_pair)
            parts.append((g_value, g_query, g_key, g_pk, g_pq))
        first, second = parts
        gv_ref[:, cols] = jnp.where(side == 0, first[0], second[0]).astype(LOW)
        gq_ref[:, cols] = (jnp.where(side == 0, first[1], second[1]) * SCALING).astype(LOW)
        gk_ref[:, cols] = (jnp.where(side == 0, first[2], second[2]) * SCALING).astype(LOW)
        gpk_ref[:, cols] = (jnp.where(side_off == 0, first[3], second[3]) * SCALING).astype(LOW)
        gpq_ref[:, cols] = (jnp.where(side_off == 0, first[4], second[4]) * SCALING).astype(LOW)
        return carry

    lax.fori_loop(first_pair, first_pair + count, pair_step, 0)
    return flip


def attend_back_one_body(
    q_ref, k_ref, v_ref, pk_ref, pq_ref, probs_ref, gctx_ref,
    gq_ref, gk_ref, gv_ref, gpk_ref, gpq_ref, qr_ref, kr_ref,
):
    heads_back(
        0, PAIRS // 2, (q_ref, k_ref, v_ref, pk_ref, pq_ref, probs_ref, gctx_ref),
        (gq_ref, gk_ref, gv_ref, gpk_ref, gpq_ref, qr_ref, kr_ref),
    )


def attend_back_two_body(
    meta_ref, q_ref, k_ref, v_ref, pk_ref, pq_ref, probs_ref, gctx_ref, hq, hk, hv, hpk, hpq,
    tok_ref, relw_ref, gres_ref, bucket_ref,
    own_q, own_k, own_v, own_rel, p0, p1, p2, p3, p4, p5,
    out_ref,
    home_ref, keep_ref, send_ref,
    grad_ref, gv_ref, pos_ref, qr_ref, kr_ref, gtok_ref, w_ref, sem,
):
    gq_ref, gk_ref, gpq_ref, gpk_ref = grad_ref.at[0], grad_ref.at[1], pos_ref.at[0], pos_ref.at[1]
    copies = Copies(sem)
    load_first(meta_ref, copies, (own_q, own_k, own_v, own_rel), (p0, p1, p2, p3, p4, p5), w_ref)
    copies.start()
    for target, done in ((gq_ref, hq), (gk_ref, hk), (gv_ref, hv), (gpk_ref, hpk), (gpq_ref, hpq)):
        target[:, : D // 2] = done[...]
    flip = heads_back(
        PAIRS // 2, PAIRS // 2, (q_ref, k_ref, v_ref, pk_ref, pq_ref, probs_ref, gctx_ref),
        (gq_ref, gk_ref, gv_ref, gpk_ref, gpq_ref, qr_ref, kr_ref),
    )
    copies.wait()
    tok, relw = tok_ref[...], relw_ref[...]
    x, core = meta_ref[X], meta_ref[CORE]

    def put(start, size, value):
        for shard in range(GROUP):
            keep, send = select_halves(meta_ref, value[shard * 2 * size : (shard + 1) * 2 * size])
            keep_ref[position(x ^ shard, near_of(core)), pl.ds(start, size)] = keep
            send_ref[position(x ^ shard, far_of(core)), pl.ds(start, size)] = send

    def weight_step(i, carry):
        g_tok, g_rel = carry
        start = pl.multiple_of(i * HALF, HALF)
        grads = mm(flip, grad_ref[i]).astype(LOW)
        weight = w_ref[:, :, pl.ds(start, HALF), :].reshape(D, D)
        put(start, HALF, mm_tn(tok, grads) + mm_tn(relw, pos_ref[i]))
        return g_tok + mm_nt(grads, weight), g_rel + mm_nt(pos_ref[i], weight)

    g_tok, g_rel = lax.fori_loop(0, 2, weight_step, (gres_ref[...], jnp.zeros((OFFS, D), F32)))
    g_value = gv_ref[...]
    gtok_ref[...] = (g_tok + mm_nt(g_value, whole(w_ref, 2 * HALF, HALF))).astype(LOW)
    put(2 * HALF, HALF, mm_tn(tok, g_value))
    pick = (bucket_ref[...] == iota((OFFS, OFFS), 1)).astype(LOW)
    put(REL_AT, REL_HALF, mm_tn(pick, g_rel.astype(LOW)))
    for member in range(GROUP):
        home_ref[member, 0] = out_ref[member * PART : (member + 1) * PART, :]
        home_ref[member, 1] = gtok_ref[member * PART : (member + 1) * PART, :]


def attend_back_one(saved, gctx):
    shape = jax.ShapeDtypeStruct
    full = pl.BlockSpec(memory_space=pltpu.VMEM)
    return pl.pallas_call(
        attend_back_one_body,
        out_shape=(*(shape((ROWS, D // 2), LOW),) * 3, *(shape((OFFS, D // 2), LOW),) * 2),
        in_specs=[full] * 7,
        out_specs=(full,) * 5,
        scratch_shapes=[pltpu.VMEM((ROWS, D), LOW), pltpu.VMEM((ROWS, D), LOW)],
        compiler_params=pltpu.CompilerParams(vmem_limit_bytes=24 * MIB),
        cost_estimate=pl.CostEstimate(flops=8_000_000_000, bytes_accessed=20_000_000, transcendentals=0),
        name="attend_back_one",
    )(*saved, gctx)


def attend_back_two(meta, saved, gctx, half_done, tok, relw, gres, bucket_column, own, pieces, out):
    shape = jax.ShapeDtypeStruct
    full, anywhere = pl.BlockSpec(memory_space=pltpu.VMEM), pl.BlockSpec(memory_space=pltpu.HBM)
    return pl.pallas_call(
        attend_back_two_body,
        out_shape=(shape((GROUP, 2, PART, D), LOW), shape((GROUP, FIRST, D), LOW), shape((GROUP, FIRST, D), LOW)),
        in_specs=[pl.BlockSpec(memory_space=pltpu.SMEM)] + [full] * 16 + [anywhere] * 10 + [full],
        out_specs=(full,) * 3,
        scratch_shapes=[
            pltpu.VMEM((2, ROWS, D), LOW), pltpu.VMEM((ROWS, D), LOW), pltpu.VMEM((2, OFFS, D), LOW),
            *(pltpu.VMEM((ROWS, D), LOW),) * 3,
            pltpu.VMEM((GROUP, 2, FIRST, D), LOW), pltpu.SemaphoreType.DMA((10,)),
        ],
        compiler_params=pltpu.CompilerParams(vmem_limit_bytes=22 * MIB),
        cost_estimate=pl.CostEstimate(flops=14_000_000_000, bytes_accessed=40_000_000, transcendentals=0),
        name="attend_back_two",
    )(meta, *saved, gctx, *half_done, tok, relw, gres, bucket_column, *own, *pieces, out)


def feed_body(
    meta_ref, tok_ref, ctx_one_ref, ctx_two_ref, rows_ref, own_outer, own_out, own_norm, own_inner, *rest,
):
    pieces, rest = rest[:10], rest[10:]
    out_ref, gctx_ref, gres_ref, keep_ref, send_ref, keep_in_ref, send_in_ref = rest[:7]
    up_ref, low_ref, act_ref, slope_ref, w_ref, in_ref, sem = rest[7:]
    copies = Copies(sem)
    copies.add(rows_ref.at[:, 1], up_ref)
    load_second(meta_ref, copies, (own_outer, own_out, own_norm, own_inner), pieces, w_ref, in_ref)
    copies.start()
    copies.wait()
    x, core = meta_ref[X], meta_ref[CORE]
    assist, assist_peer = assist_of(meta_ref, core), assist_of(meta_ref, 1 - core)

    def put_outer(shard, quarter, keep, send, start):
        rows = slice(start, start + keep.shape[0])
        keep_ref[position(assist ^ quarter, 1), position(x ^ shard, near_of(core)), rows] = keep
        send_ref[position(assist_peer ^ quarter, 1), position(x ^ shard, far_of(core)), rows] = send

    def put_inner(shard, quarter, keep, send):
        keep_in_ref[position(assist ^ quarter, 3), position(x ^ shard, near_of(core))] = keep
        send_in_ref[position(assist_peer ^ quarter, 3), position(x ^ shard, far_of(core))] = send

    length = meta_ref[LENGTH]
    mask = (iota((ROWS, 1), 0) < length).astype(F32)
    norm_rows = []
    for s in range(GROUP):
        side, place = second_block(meta_ref, s, 0)
        norm_rows.append(w_ref[side, place, NORM_AT : NORM_AT + QUARTER - HALF, :].astype(F32)[:1])
    gain_one, bias_one, gain_two, bias_two = (
        jnp.concatenate([row[:, i * PIECE : (i + 1) * PIECE] for row in norm_rows], axis=1) for i in range(4)
    )
    token = tok_ref[...].astype(F32)
    ctx = jnp.concatenate([ctx_one_ref[...], ctx_two_ref[...]], axis=1)
    blocks = [second_block(meta_ref, shard, half) for shard in range(GROUP) for half in range(2)]
    w_out = jnp.concatenate([w_ref[side, place, OUT_AT : OUT_AT + HALF, :] for side, place in blocks], axis=0)
    attn = mm(ctx, w_out)

    def norm(values):
        center = values - jnp.mean(values, axis=1, keepdims=True)
        inverse = lax.rsqrt(jnp.mean(center * center, axis=1, keepdims=True) + EPSILON)
        return center * inverse, inverse

    def norm_back(upstream, normed, inverse, gain):
        scaled = upstream * gain
        plain = jnp.mean(scaled, axis=1, keepdims=True)
        cross = jnp.mean(scaled * normed, axis=1, keepdims=True)
        return inverse * (scaled - plain - normed * cross)

    def total(values):
        return jnp.sum(values, axis=0, keepdims=True)

    normed_one, inverse_one = norm(token + attn)
    hidden_one = normed_one * gain_one + bias_one
    low_ref[...] = hidden_one.astype(LOW)

    def columns(c):
        return pl.ds(pl.multiple_of(c * D, D), D)

    def outer_rows(c):
        halves = [second_block(meta_ref, c, half) for half in range(2)]
        return jnp.concatenate([w_ref[side, place, 0 : D // 2, :] for side, place in halves], axis=0)

    def inner_columns(c):
        return jnp.concatenate([in_ref[side, place, :, columns(c)] for side, place in blocks], axis=0)

    def forward_step(c, ffn):
        inner = mm(low_ref[...], inner_columns(c))
        cumulative = 0.5 * (1.0 + lax.erf(inner * 0.5**0.5))
        density = jnp.exp(-0.5 * inner * inner) * 0.3989422804014327
        act = (inner * cumulative).astype(LOW)
        act_ref[c] = act
        slope_ref[c] = cumulative + inner * density
        return ffn + mm(act, outer_rows(c))

    ffn = lax.fori_loop(0, GROUP, forward_step, jnp.zeros((ROWS, D), F32))
    normed_two, inverse_two = norm(hidden_one + ffn)
    layer = (normed_two * gain_two + bias_two) * mask
    out_ref[...] = layer.astype(LOW)
    squares = [token * token * mask, attn * attn * mask, ffn * ffn * mask, layer * layer]
    sums = [jnp.sum(total(s), axis=1, keepdims=True) for s in squares]
    grad_y = up_ref[...].reshape(ROWS, D).astype(F32) * mask
    grad_gain_two = total(grad_y * normed_two)
    grad_bias_two = total(grad_y)
    grad_two = norm_back(grad_y, normed_two, inverse_two, gain_two)
    grad_ffn = grad_two.astype(LOW)

    def back_step(c, grad_hidden):
        grad_act = mm_nt(grad_ffn, outer_rows(c))
        grad_inner = (grad_act * slope_ref[c]).astype(LOW)
        keep, send = select_halves(meta_ref, mm_tn(act_ref[c], grad_ffn))
        for quarter in range(3):
            rows = slice(quarter * QUARTER, (quarter + 1) * QUARTER)
            put_outer(c, quarter, keep[rows], send[rows], 0)
        grad_w = mm_tn(low_ref[...], grad_inner)
        for s in range(GROUP):
            put_inner(s, c, *select_halves(meta_ref, grad_w[s * PIECE : (s + 1) * PIECE]))
        return grad_hidden + mm_nt(grad_inner, inner_columns(c))

    grad_hidden = lax.fori_loop(0, GROUP, back_step, grad_two)
    grad_gain_one = total(grad_hidden * normed_one)
    grad_bias_one = total(grad_hidden)
    grad_one = norm_back(grad_hidden, normed_one, inverse_one, gain_one)
    gres_ref[...] = grad_one
    grad_attn = grad_one.astype(LOW)
    grad_out = mm_tn(ctx, grad_attn)
    for s in range(GROUP):
        put_outer(s, 3, *select_halves(meta_ref, grad_out[s * PIECE : (s + 1) * PIECE]), 0)
    gctx_ref[...] = mm_nt(grad_attn, w_out).astype(LOW)
    lane = iota((1, D), 1)
    stats = jnp.zeros((1, D), F32)
    for i, value in enumerate(sums):
        stats = jnp.where(lane == i, value, stats)
    low = stats - stats.astype(LOW).astype(F32)
    zeros = jnp.zeros((1, D), F32)
    norm_rows = (grad_gain_one, grad_bias_one, grad_gain_two, grad_bias_two)
    for s in range(GROUP):
        row = jnp.concatenate([r[:, s * PIECE : (s + 1) * PIECE] for r in norm_rows], axis=1)
        block = jnp.concatenate([row] + [zeros] * 31 + [stats, low] + [zeros] * 30, axis=0)
        put_outer(s, 3, *select_halves(meta_ref, block), HALF)


def feed(meta, tok, ctx_one, ctx_two, rows, own, pieces):
    shape = jax.ShapeDtypeStruct
    full, anywhere = pl.BlockSpec(memory_space=pltpu.VMEM), pl.BlockSpec(memory_space=pltpu.HBM)
    block, wide = shape((GROUP, GROUP, QUARTER, D), LOW), shape((GROUP, GROUP, HALF, D), LOW)
    return pl.pallas_call(
        feed_body,
        out_shape=(
            shape((ROWS, D), LOW), shape((ROWS, D), LOW), shape((ROWS, D), F32), block, block, wide, wide
        ),
        in_specs=[pl.BlockSpec(memory_space=pltpu.SMEM)] + [full] * 3 + [anywhere] * 15,
        out_specs=(full,) * 7,
        scratch_shapes=[
            pltpu.VMEM((GROUP, PART, D), LOW), pltpu.VMEM((ROWS, D), LOW), pltpu.VMEM((GROUP, ROWS, D), LOW),
            pltpu.VMEM((GROUP, ROWS, D), F32), pltpu.VMEM((2, GROUP, SECOND, D), LOW),
            pltpu.VMEM((2, GROUP, HALF, WIDE), LOW), pltpu.SemaphoreType.DMA((24,)),
        ],
        compiler_params=pltpu.CompilerParams(vmem_limit_bytes=48 * MIB),
        cost_estimate=pl.CostEstimate(flops=16_000_000_000, bytes_accessed=60_000_000, transcendentals=1_600_000),
        name="feed",
    )(meta, tok, ctx_one, ctx_two, rows, *own, *pieces)


def finish_body(
    meta_ref, mine, other, rows_ref,
    q_ref, k_ref, v_ref, rel_ref, outer_ref, wout_ref, inner_ref, extra_ref, out_ref, gtok_ref,
):
    for piece, side in ((mine, 0), (other, 1)):
        core = meta_ref[CORE] if side == 0 else 1 - meta_ref[CORE]
        assist = assist_of(meta_ref, core)
        for i, ref in enumerate((q_ref, k_ref, v_ref, rel_ref)):
            size = REL_HALF if i == 3 else HALF
            ref[pl.ds(pl.multiple_of(core * size, size), size), :] = piece[i * HALF : i * HALF + size, :].astype(F32)

        def piece_step(distance, carry):
            quarter = assist ^ distance
            at = pl.multiple_of(FIRST + distance * SPAN, HALF // 3)
            block = piece[pl.ds(at, QUARTER), :].astype(F32)

            @pl.when(quarter < 3)
            def _():
                outer_ref[pl.ds(pl.multiple_of(core * 3 * QUARTER + quarter * QUARTER, QUARTER), QUARTER), :] = block

            @pl.when(quarter == 3)
            def _():
                wout_ref[pl.ds(pl.multiple_of(core * HALF, HALF), HALF), :] = block[:HALF]
                extra_ref[core] = block[HALF:]

            inner_ref[
                pl.ds(pl.multiple_of(core * HALF, HALF), HALF), pl.ds(pl.multiple_of(quarter * D, D), D)
            ] = piece[pl.ds(at + QUARTER, HALF), :].astype(F32)
            return carry

        lax.fori_loop(0, GROUP, piece_step, 0)
    for k in range(GROUP):
        member = meta_ref[X] ^ k
        out_ref[meta_ref[SEQ + k]] = rows_ref[member, 0]
        gtok_ref[meta_ref[SEQ + k]] = rows_ref[member, 1]


def finish(meta, mine, other, rows):
    shape = jax.ShapeDtypeStruct
    full = pl.BlockSpec(memory_space=pltpu.VMEM)
    return pl.pallas_call(
        finish_body,
        out_shape=(
            *(shape((PIECE, D), F32),) * 3, shape((OFFS // GROUP, D), F32),
            shape((D, D), F32), shape((PIECE, D), F32), shape((PIECE, WIDE), F32), shape((2, QUARTER - HALF, D), F32),
            *(shape((GROUP, PART, D), LOW),) * 2,
        ),
        in_specs=[pl.BlockSpec(memory_space=pltpu.SMEM)] + [full] * 3,
        out_specs=(full,) * 10,
        compiler_params=pltpu.CompilerParams(vmem_limit_bytes=24 * MIB),
        name="finish",
    )(meta, mine, other, rows)


NEAR, FAR = (1, 3), (3, 1)


def hop_x(value, flips):
    pairs = [(c * 4 + i, c * 4 + (i ^ flips[c])) for c in range(2) for i in range(4)]
    return lax.ppermute(value, ("core", "shard"), pairs)


def hop_yz(value, flip, swapped=False):
    pairs = []
    for y in range(4):
        for z in range(4):
            for c in range(2):
                along_y = (c == 0) != swapped
                ty, tz = (y ^ flip, z) if along_y else (y, z ^ flip)
                pairs.append(((y * 4 + z) * 2 + c, (ty * 4 + tz) * 2 + c))
    return lax.ppermute(value, ("y", "z", "core"), pairs)


def swap(value):
    return lax.ppermute(value, "core", [(0, 1), (1, 0)])


def after(value, *others):
    return lax.optimization_barrier((value, *others))[0]


def add(*values):
    total = values[0].astype(F32)
    for value in values[1:]:
        total = total + value.astype(F32)
    return total.astype(LOW)


def exchange_rows(rows):
    return lax.all_to_all(rows, "shard", split_axis=0, concat_axis=0, tiled=True)


def shards(
    hidden, grad_out, lengths, bucket, w_query, w_key, w_value, w_out, w_inner, w_outer, rel_table,
    ln1_gain, ln1_bias, ln2_gain, ln2_bias,
):
    coords = jnp.stack([lax.axis_index(name) for name in ("shard", "y", "z", "core")]).astype(jnp.int32)
    norm_block = jnp.concatenate(
        [jnp.concatenate([ln1_gain, ln1_bias, ln2_gain, ln2_bias])[None], jnp.zeros((31, D), LOW)], axis=0
    )
    bucket_column = jnp.concatenate([bucket[::-1], jnp.full((1,), -1, jnp.int32)])[:, None]
    own_first = (w_query, w_key, w_value, rel_table)
    own_halves = tuple(ref.reshape(2, ref.shape[0] // 2, D) for ref in own_first)
    meta, first, second, rows = pack(
        coords, lengths, hidden, grad_out, own_first, (w_outer, w_out, w_inner), norm_block
    )
    near_two, far_two = hop_x(second, NEAR), hop_x(second, FAR)
    near, far = hop_x(first, NEAR), hop_x(first, FAR)
    rows = exchange_rows(rows)
    across_two = hop_x(near_two, FAR)
    base = after(jnp.stack([near_two, far_two, across_two]), near, far)
    base_near, base_far = hop_yz(base, 1), hop_yz(base, 3)
    across = hop_x(near, FAR)
    pieces = (near, far, across, swap(near), swap(far), swap(across))
    part_outer, part_inner = base_near[:, :QUARTER], base_far[:, QUARTER:]
    rows = after(rows, part_outer, part_inner)
    across_outer, across_inner = hop_yz(part_outer, 3), hop_yz(part_inner, 1)
    tok, *saved, relw, probs, ctx = attend_forward(meta, bucket_column, rows, own_halves, pieces)
    across_outer, across_inner, base, base_near, base_far, _ = lax.optimization_barrier(
        (across_outer, across_inner, base, base_near, base_far, ctx)
    )
    arrived = (base, base_near, base_far, across_outer, across_inner)
    swapped = tuple(swap(piece) for piece in arrived)
    probs_two, ctx_two = attend_forward_two(meta, saved)
    swapped = after(swapped, ctx_two)
    out, gctx, gres, keep, send, keep_in, send_in = feed(
        meta, tok, ctx, ctx_two, rows, (w_outer, w_out, norm_block, w_inner), (*arrived, *swapped)
    )
    other, other_in = swap(send), swap(send_in)
    half_done = attend_back_one((*saved, probs), gctx)
    leave = add(keep[:2], other[:2])
    leave_in = add(keep_in[:2], other_in[:2])
    came, came_in = hop_yz(leave, 1), hop_yz(leave_in, 3)
    half_done = after(tuple(half_done), leave, leave_in)
    leaving, keep_one, send_one = attend_back_two(
        meta, (*saved, probs_two), gctx, half_done, tok, relw, gres, bucket_column, own_halves, pieces, out
    )
    other_one = swap(after(send_one, came, came_in))
    leave_one = add(keep_one[:2], other_one[:2])
    came, came_in = after((came, came_in), leave_one)
    last = hop_yz(add(keep[2], other[2], came[0]), 3)
    last_in = hop_yz(add(keep_in[2], other_in[2], came_in[0]), 1)
    came_one = hop_x(leave_one, NEAR)
    came_one = after(came_one, last, last_in)
    leave_two = add(keep_one[2], other_one[2], came_one[0])
    last_one = hop_x(leave_two, FAR)
    last, last_in, _ = lax.optimization_barrier((last, last_in, leave_two))
    mine = add(keep[3], other[3], came[1], last)
    mine_in = add(keep_in[3], other_in[3], came_in[1], last_in)
    both = jnp.concatenate([mine, mine_in], axis=1)
    came_x = hop_x(both[:2], NEAR)
    home = exchange_rows(leaving)
    last_one = after(last_one, came_x)
    mine_one = add(keep_one[3], other_one[3], came_one[1], last_one)
    come_one = hop_yz(mine_one, 1, swapped=True)
    last_x = hop_x(after(add(both[2], came_x[0]), mine_one), FAR)
    mine_one = add(mine_one, after(come_one, last_x))
    come_one = hop_yz(mine_one, 3, swapped=True)
    both = after(add(both[3], came_x[1], last_x), mine_one)
    step = hop_yz(both, 1, swapped=True)
    mine_one = add(mine_one, after(come_one, step))
    come_one = hop_yz(mine_one, 1)
    both = after(add(both, step), mine_one)
    step = hop_yz(both, 3, swapped=True)
    mine_one = add(mine_one, after(come_one, step))
    come_one = hop_yz(mine_one, 3)
    both = after(add(both, step), mine_one)
    both = [both, *(hop_yz(both, flip) for flip in (1, 3, 2))]
    both[1], both[2], both[3] = both[1], both[3], both[2]
    mine_one = add(mine_one, come_one)
    packed = after(jnp.concatenate([mine_one, *both], axis=0), home)
    q_grad, k_grad, v_grad, rel_grad, outer_grad, out_grad, inner_grad, extra, layer_output, grad_hidden = finish(
        meta, packed, swap(packed), home
    )
    norm_sums = extra[0, 0].reshape(GROUP, PIECE)
    stats = extra[1, 0, :GROUP] + extra[1, 1, :GROUP]
    return (
        layer_output, grad_hidden, q_grad, k_grad, v_grad, out_grad, inner_grad, outer_grad, rel_grad,
        norm_sums[0], norm_sums[1], norm_sums[2], norm_sums[3],
        jnp.sqrt(stats / (TOKENS * D)),
    )


def solution(mesh):
    split = Mesh(mesh.devices.reshape(4, 4, 2, 4), ("y", "z", "core", "shard"))
    rep = ("y", "z", "core")
    rows, vector = P("shard", None), P("shard")
    batch = P(rep, "shard", None)
    return jax.shard_map(
        shards,
        mesh=split,
        in_specs=(batch, batch, P(rep), P(), *(rows,) * 7, *(vector,) * 4),
        out_specs=(batch, batch, *(rows,) * 7, *(vector,) * 4, P()),
        check_vma=False,
    )
```

profile of v0, /device:TPU:17, one launch (start us, length us, event | category | flops | bytes accessed | tf_op | source)
XLA Modules:
  0.0 222.5 jit_solution(2221310899923034209)
XLA Ops:
  2.7 3.5 %pack.1 = (s32[16]{0:T(128)}, bf16[352,768]{1,0:T(8,128)(2,1)}, bf16[224,768]{1,0:T(8,128)(2,1)}, bf16[4,2,64,768]{3,2,1,0:T(8,128)(2,1)}) custom-call(s32[4]{0:T(128)} %pad_add_fusion.1.coord_ref, s32[4]{0:T(128)} %length_ref.1, bf16[4,64,768]{2,1,0:T(8,128)(2,1)} %hidden_ref.1, bf16[4,64,768]{2,1,0:T(8,128)(2,1)} %grad_ref.1, bf16[192,768]{1,0:T(8,128)(2,1)} %own_q.1, ...), custom_call_target="tpu_custom_call" | custom-call | tf_op jit(solution)/shard_map/pack/pallas_call | solution.py:166
  10.4 4.2 %collective-permute-done = bf16[224,768]{1,0:T(8,128)(2,1)S(1)} collective-permute-done((bf16[224,768]{1,0:T(8,128)(2,1)}, bf16[224,768]{1,0:T(8,128)(2,1)S(1)}, u32[]{:S(2)}, u32[]{:S(2)}) %collective-permute-start) | collective-permute-done | bytes 344096 | tf_op jit(solution)/shard_map/ppermute | solution.py:666
  14.6 11.5 %collective-permute-done.3.p0 = bf16[352,768]{1,0:T(8,128)(2,1)S(1)} collective-permute-done((bf16[352,768]{1,0:T(8,128)(2,1)}, bf16[352,768]{1,0:T(8,128)(2,1)S(1)}, u32[]{:S(2)}, u32[]{:S(2)}) %collective-permute-start.3) | collective-permute-done | bytes 540704 | tf_op jit(solution)/shard_map/ppermute | solution.py:666
  26.1 3.2 %collective-permute-done.1 = bf16[224,768]{1,0:T(8,128)(2,1)S(1)} collective-permute-done((bf16[224,768]{1,0:T(8,128)(2,1)}, bf16[224,768]{1,0:T(8,128)(2,1)S(1)}, u32[]{:S(2)}, u32[]{:S(2)}) %collective-permute-start.1) | collective-permute-done | bytes 344096 | tf_op jit(solution)/shard_map/ppermute | solution.py:666
  29.3 3.7 %collective-permute-done.2 = bf16[224,768]{1,0:T(8,128)(2,1)S(1)} collective-permute-done((bf16[224,768]{1,0:T(8,128)(2,1)S(1)}, bf16[224,768]{1,0:T(8,128)(2,1)S(1)}, u32[]{:S(2)}, u32[]{:S(2)}) %collective-permute-start.2) | collective-permute-done | bytes 344096 | tf_op jit(solution)/shard_map/ppermute | solution.py:666
  34.1 3.8 %collective-permute-start.6 = (bf16[3,224,768]{2,1,0:T(8,128)(2,1)}, bf16[3,224,768]{2,1,0:T(8,128)(2,1)}, u32[]{:S(2)}, u32[]{:S(2)}) collective-permute-start(bf16[3,224,768]{2,1,0:T(8,128)(2,1)} %pad_maximum_fusion.rest_0_), channel_id=1, source_target_pairs={{0,96},{4,28},{8,104},{12,20},{16,112},{20,12},{24,120},{28,4},{32... | collective-permute-start | bytes 3096584 | tf_op jit(solution)/shard_map/ppermute | solution.py:677
  37.8 4.3 %all-to-all-start = ((bf16[4,2,64,768]{3,2,1,0:T(8,128)(2,1)}), bf16[4,2,64,768]{3,2,1,0:T(8,128)(2,1)S(1)}, u32[]{:S(2)}, u32[]{:S(2)}) async-start(bf16[4,2,64,768]{3,2,1,0:T(8,128)(2,1)} %get-tuple-element.87), calls=%async_computation | async-start | bytes 1572864 | tf_op jit(solution)/shard_map/all_to_all | solution.py:696
  43.0 7.3 %collective-permute-done.6.rest_2_ = bf16[3,224,768]{2,1,0:T(8,128)(2,1)} collective-permute-done((bf16[3,224,768]{2,1,0:T(8,128)(2,1)}, bf16[3,224,768]{2,1,0:T(8,128)(2,1)}, u32[]{:S(2)}, u32[]{:S(2)}) %collective-permute-start.6) | collective-permute-done | bytes 1032224 | tf_op jit(solution)/shard_map/ppermute | solution.py:677
  56.8 10.2 %attend_forward.1 = (bf16[256,768]{1,0:T(8,128)(2,1)S(1)}, bf16[256,768]{1,0:T(8,128)(2,1)S(1)}, bf16[256,768]{1,0:T(8,128)(2,1)S(1)}, bf16[256,768]{1,0:T(8,128...) custom-call(s32[16]{0:T(128)S(1)} %copy-done.6, ...), custom_call_target="tpu_custom_call" | custom-call | flops 12000000000 | bytes 40000000 | tf_op jit(solution)/shard_map/attend_forward/pallas_call | solution.py:294
  68.2 5.5 %attend_forward_two.1 = (bf16[6,256,256]{2,1,0:T(8,128)(2,1)S(1)}, bf16[256,384]{1,0:T(8,128)(2,1)S(1)}) custom-call(s32[16]{0:T(128)S(1)} %copy-done.6, bf16[256,768]{1,0:T(8,128)(2,1)S(1)} %get-tuple-element.92.q_ref, bf16[256,768]{1,0:T(8,128)(2,1)S(1)} %get-tuple-element.93.k_ref, bf16[256,768]{1,0:T(8,128)(2,1)S(1)} %get-tuple-element.94.v_ref, ...), custom_call_target="tpu_custom_call" | custom-call | flops 8000000000 | bytes 20000000 | tf_op jit(solution)/shard_map/attend_forward_two/pallas_call | solution.py:315
  76.1 22.1 %feed.1 = (bf16[256,768]{1,0:T(8,128)(2,1)S(1)}, bf16[256,768]{1,0:T(8,128)(2,1)S(1)}, f32[256,768]{1,0:T(8,128)S(1)}, bf16[4,4,128,768]{3,2,1,0:T(8,128)(2,1)},...) custom-call(s32[16]{0:T(128)S(1)} %copy-done.6, ...), custom_call_target="tpu_custom_call" | custom-call | flops 16000000000 | bytes 60000000 | tf_op jit(solution)/shard_map/feed/pallas_call | solution.py:589
  98.9 6.0 %attend_back_one.1 = (bf16[256,384]{1,0:T(8,128)(2,1)S(1)}, bf16[256,384]{1,0:T(8,128)(2,1)S(1)}, bf16[256,384]{1,0:T(8,128)(2,1)S(1)}, bf16[512,384]{1,0:T(8,128)(2,1)S(1)}, bf16[512,384]{1,0:T(8,128)(2,1)S(1)}) custom-call(bf16[256,768]{1,0:T(8,128)(2,1)S(1)} %get-tuple-element.92.q_ref, bf16[256,768]{1,0:T(8,128)(2,1)S(1)} %get-tuple-element.93.k_ref, ...), custom_call_target="tpu_custom_call" | custom-call | flops 8000000000 | bytes 20000000 | tf_op jit(solution)/shard_map/attend_back_one/pallas_call | solution.py:432
  110.5 14.4 %attend_back_two.1 = (bf16[4,2,64,768]{3,2,1,0:T(8,128)(2,1)}, bf16[4,352,768]{2,1,0:T(8,128)(2,1)S(1)}, bf16[4,352,768]{2,1,0:T(8,128)(2,1)S(1)}) custom-call(s32[16]{0:T(128)S(1)} %copy-done.6, bf16[256,768]{1,0:T(8,128)(2,1)S(1)} %get-tuple-element.92.q_ref, bf16[256,768]{1,0:T(8,128)(2,1)S(1)} %get-tuple-element.93.k_ref, ...), custom_call_target="tpu_custom_call" | custom-call | flops 14000000000 | bytes 40000000 | tf_op jit(solution)/shard_map/attend_back_two/pallas_call | solution.py:447
  126.0 3.9 %collective-permute-done.22 = bf16[4,352,768]{2,1,0:T(8,128)(2,1)S(1)} collective-permute-done((bf16[4,352,768]{2,1,0:T(8,128)(2,1)S(1)}, bf16[4,352,768]{2,1,0:T(8,128)(2,1)S(1)}, u32[]{:S(2)}, u32[]{:S(2)}) %collective-permute-start.22) | collective-permute-done | bytes 2162720 | tf_op jit(solution)/shard_map/ppermute | solution.py:681
  135.9 9.0 %collective-permute-done.25 = bf16[4,96,768]{2,1,0:T(8,128)(2,1)S(1)} collective-permute-done((bf16[4,96,768]{2,1,0:T(8,128)(2,1)S(1)}, bf16[4,96,768]{2,1,0:T(8,128)(2,1)S(1)}, u32[]{:S(2)}, u32[]{:S(2)}) %collective-permute-start.25) | collective-permute-done | bytes 589856 | tf_op jit(solution)/shard_map/ppermute | solution.py:677
  148.9 14.2 %collective-permute-done.26 = bf16[352,768]{1,0:T(8,128)(2,1)S(1)} collective-permute-done((bf16[352,768]{1,0:T(8,128)(2,1)S(1)}, bf16[352,768]{1,0:T(8,128)(2,1)S(1)}, u32[]{:S(2)}, u32[]{:S(2)}) %collective-permute-start.26) | collective-permute-done | bytes 540704 | tf_op jit(solution)/shard_map/ppermute | solution.py:666
  164.8 6.3 %collective-permute-done.29 = bf16[224,768]{1,0:T(8,128)(2,1)S(1)} collective-permute-done((bf16[224,768]{1,0:T(8,128)(2,1)S(1)}, bf16[224,768]{1,0:T(8,128)(2,1)S(1)}, u32[]{:S(2)}, u32[]{:S(2)}) %collective-permute-start.29) | collective-permute-done | bytes 344096 | tf_op jit(solution)/shard_map/ppermute | solution.py:666
  174.9 5.5 %collective-permute-done.31 = bf16[224,768]{1,0:T(8,128)(2,1)S(1)} collective-permute-done((bf16[224,768]{1,0:T(8,128)(2,1)S(1)}, bf16[224,768]{1,0:T(8,128)(2,1)S(1)}, u32[]{:S(2)}, u32[]{:S(2)}) %collective-permute-start.31) | collective-permute-done | bytes 344096 | tf_op jit(solution)/shard_map/ppermute | solution.py:677
  183.5 4.9 %collective-permute-done.33 = bf16[224,768]{1,0:T(8,128)(2,1)S(1)} collective-permute-done((bf16[224,768]{1,0:T(8,128)(2,1)S(1)}, bf16[224,768]{1,0:T(8,128)(2,1)S(1)}, u32[]{:S(2)}, u32[]{:S(2)}) %collective-permute-start.33) | collective-permute-done | bytes 344096 | tf_op jit(solution)/shard_map/ppermute | solution.py:677
  192.7 3.8 %all-to-all-start.1 = ((bf16[4,2,64,768]{3,2,1,0:T(8,128)(2,1)}), bf16[4,2,64,768]{3,2,1,0:T(8,128)(2,1)S(1)}, u32[]{:S(2)}, u32[]{:S(2)}) async-start(bf16[4,2,64,768]{3,2,1,0:T(8,128)(2,1)} %get-tuple-element.146), calls=%async_computation.1 | async-start | bytes 1572864 | tf_op jit(solution)/shard_map/all_to_all | solution.py:696
  201.6 6.9 %collective-permute-done.35 = bf16[224,768]{1,0:T(8,128)(2,1)S(1)} collective-permute-done((bf16[224,768]{1,0:T(8,128)(2,1)S(1)}, bf16[224,768]{1,0:T(8,128)(2,1)S(1)}, u32[]{:S(2)}, u32[]{:S(2)}) %collective-permute-start.35) | collective-permute-done | bytes 344096 | tf_op jit(solution)/shard_map/ppermute | solution.py:677
  208.6 4.7 %collective-permute-start.38 = (bf16[1248,768]{1,0:T(8,128)(2,1)S(1)}, bf16[1248,768]{1,0:T(8,128)(2,1)S(1)}, u32[]{:S(2)}, u32[]{:S(2)}) collective-permute-start(bf16[1248,768]{1,0:T(8,128)(2,1)S(1)} %constant_dynamic-update-slice_fusion.mine), channel_id=1, source_target_pairs={{0,4},{4,0},{1,5},{5,1},{2,6},{6,2},{3,7},{7,3},{8,12},{12,8},{9,1... | collective-permute-start | bytes 5750792 | tf_op jit(solution)/shard_map/ppermute | solution.py:681
  213.3 3.5 %collective-permute-done.38.other = bf16[1248,768]{1,0:T(8,128)(2,1)S(1)} collective-permute-done((bf16[1248,768]{1,0:T(8,128)(2,1)S(1)}, bf16[1248,768]{1,0:T(8,128)(2,1)S(1)}, u32[]{:S(2)}, u32[]{:S(2)}) %collective-permute-start.38) | collective-permute-done | bytes 1916960 | tf_op jit(solution)/shard_map/ppermute | solution.py:681
  216.9 4.5 %finish.1 = (f32[192,768]{1,0:T(8,128)}, f32[192,768]{1,0:T(8,128)}, f32[192,768]{1,0:T(8,128)}, f32[128,768]{1,0:T(8,128)}, f32[768,768]{1,0:T(8,128)}, /*index...) custom-call(s32[16]{0:T(128)S(1)} %copy-done.6, ...), custom_call_target="tpu_custom_call" | custom-call | tf_op jit(solution)/shard_map/finish/pallas_call | solution.py:647
  (126 shorter events, 54.7 us)
Async XLA Ops:
  8.7 17.4 %collective-permute-start.3 = (bf16[352,768]{1,0:T(8,128)(2,1)}, bf16[352,768]{1,0:T(8,128)(2,1)S(1)}, u32[]{:S(2)}, u32[]{:S(2)}) collective-permute-start(bf16[352,768]{1,0:T(8,128)(2,1)} %get-tuple-element.89), channel_id=1, source_target_pairs={{0,1},{1,0},{2,3},{3,2},{4,7},{5,6},{6,5},{7,4},{8,9},{9,8},{10,11... | collective-permute-start | bytes 1622024 | tf_op jit(solution)/shard_map/ppermute | solution.py:666
  8.9 25.1 %collective-permute-start.4 = (bf16[352,768]{1,0:T(8,128)(2,1)}, bf16[352,768]{1,0:T(8,128)(2,1)}, u32[]{:S(2)}, u32[]{:S(2)}) collective-permute-start(bf16[352,768]{1,0:T(8,128)(2,1)} %get-tuple-element.89), channel_id=1, source_target_pairs={{0,3},{1,2},{2,1},{3,0},{4,5},{5,4},{6,7},{7,6},{8,11},{9,10},{10,... | collective-permute-start | bytes 1622024 | tf_op jit(solution)/shard_map/ppermute | solution.py:666
  8.9 20.3 %collective-permute-start.1 = (bf16[224,768]{1,0:T(8,128)(2,1)}, bf16[224,768]{1,0:T(8,128)(2,1)S(1)}, u32[]{:S(2)}, u32[]{:S(2)}) collective-permute-start(bf16[224,768]{1,0:T(8,128)(2,1)} %get-tuple-element.88), channel_id=1, source_target_pairs={{0,3},{1,2},{2,1},{3,0},{4,5},{5,4},{6,7},{7,6},{8,11},{9,10},{10,... | collective-permute-start | bytes 1032200 | tf_op jit(solution)/shard_map/ppermute | solution.py:666
  14.6 18.3 %collective-permute-start.2 = (bf16[224,768]{1,0:T(8,128)(2,1)S(1)}, bf16[224,768]{1,0:T(8,128)(2,1)S(1)}, u32[]{:S(2)}, u32[]{:S(2)}) collective-permute-start(bf16[224,768]{1,0:T(8,128)(2,1)S(1)} %collective-permute-done), channel_id=1, source_target_pairs={{0,3},{1,2},{2,1},{3,0},{4,5},{5,4},{6,7},{7,6},{8,11},{9,10},{10,... | collective-permute-start | bytes 1032200 | tf_op jit(solution)/shard_map/ppermute | solution.py:666
  26.1 16.5 %collective-permute-start.7 = (bf16[352,768]{1,0:T(8,128)(2,1)S(1)}, bf16[352,768]{1,0:T(8,128)(2,1)}, u32[]{:S(2)}, u32[]{:S(2)}) collective-permute-start(bf16[352,768]{1,0:T(8,128)(2,1)S(1)} %collective-permute-done.3.p0), channel_id=1, source_target_pairs={{0,3},{1,2},{2,1},{3,0},{4,5},{5,4},{6,7},{7,6},{8,11},{9,10},{10,... | collective-permute-start | bytes 1622024 | tf_op jit(solution)/shard_map/ppermute | solution.py:666
  34.1 16.3 %collective-permute-start.6 = (bf16[3,224,768]{2,1,0:T(8,128)(2,1)}, bf16[3,224,768]{2,1,0:T(8,128)(2,1)}, u32[]{:S(2)}, u32[]{:S(2)}) collective-permute-start(bf16[3,224,768]{2,1,0:T(8,128)(2,1)} %pad_maximum_fusion.rest_0_), channel_id=1, source_target_pairs={{0,96},{4,28},{8,104},{12,20},{16,112},{20,12},{24,120},{28,4},{32... | collective-permute-start | bytes 3096584 | tf_op jit(solution)/shard_map/ppermute | solution.py:677
  37.8 14.3 %collective-permute-start.5 = (bf16[3,224,768]{2,1,0:T(8,128)(2,1)}, bf16[3,224,768]{2,1,0:T(8,128)(2,1)}, u32[]{:S(2)}, u32[]{:S(2)}) collective-permute-start(bf16[3,224,768]{2,1,0:T(8,128)(2,1)} %pad_maximum_fusion.rest_0_), channel_id=1, source_target_pairs={{0,32},{4,12},{8,40},{12,4},{16,48},{20,28},{24,56},{28,20},{32,0}... | collective-permute-start | bytes 3096584 | tf_op jit(solution)/shard_map/ppermute | solution.py:677
  37.8 18.9 %all-to-all-start = ((bf16[4,2,64,768]{3,2,1,0:T(8,128)(2,1)}), bf16[4,2,64,768]{3,2,1,0:T(8,128)(2,1)S(1)}, u32[]{:S(2)}, u32[]{:S(2)}) async-start(bf16[4,2,64,768]{3,2,1,0:T(8,128)(2,1)} %get-tuple-element.87), calls=%async_computation | async-start | bytes 1572864 | tf_op jit(solution)/shard_map/all_to_all | solution.py:696
  42.1 14.6 %collective-permute-start.9 = (bf16[352,768]{1,0:T(8,128)(2,1)}, bf16[352,768]{1,0:T(8,128)(2,1)}, u32[]{:S(2)}, u32[]{:S(2)}) collective-permute-start(bf16[352,768]{1,0:T(8,128)(2,1)} %collective-permute-done.4.p1), channel_id=1, source_target_pairs={{0,4},{4,0},{1,5},{5,1},{2,6},{6,2},{3,7},{7,3},{8,12},{12,8},{9,1... | collective-permute-start | bytes 1622024 | tf_op jit(solution)/shard_map/ppermute | solution.py:681
  42.1 14.6 %collective-permute-start.8 = (bf16[352,768]{1,0:T(8,128)(2,1)S(1)}, bf16[352,768]{1,0:T(8,128)(2,1)}, u32[]{:S(2)}, u32[]{:S(2)}) collective-permute-start(bf16[352,768]{1,0:T(8,128)(2,1)S(1)} %collective-permute-done.3.p0), channel_id=1, source_target_pairs={{0,4},{4,0},{1,5},{5,1},{2,6},{6,2},{3,7},{7,3},{8,12},{12,8},{9,1... | collective-permute-start | bytes 1622024 | tf_op jit(solution)/shard_map/ppermute | solution.py:681
  42.6 14.1 %collective-permute-start.10 = (bf16[352,768]{1,0:T(8,128)(2,1)}, bf16[352,768]{1,0:T(8,128)(2,1)}, u32[]{:S(2)}, u32[]{:S(2)}) collective-permute-start(bf16[352,768]{1,0:T(8,128)(2,1)} %collective-permute-done.7.p2), channel_id=1, source_target_pairs={{0,4},{4,0},{1,5},{5,1},{2,6},{6,2},{3,7},{7,3},{8,12},{12,8},{9,1... | collective-permute-start | bytes 1622024 | tf_op jit(solution)/shard_map/ppermute | solution.py:681
  52.1 14.9 %collective-permute-start.12 = (bf16[3,96,768]{2,1,0:T(8,128)(2,1)}, bf16[3,96,768]{2,1,0:T(8,128)(2,1)}, u32[]{:S(2)}, u32[]{:S(2)}) collective-permute-start(bf16[3,96,768]{2,1,0:T(8,128)(2,1)} %slice.158), channel_id=1, source_target_pairs={{0,32},{4,12},{8,40},{12,4},{16,48},{20,28},{24,56},{28,20},{32,0}... | collective-permute-start | bytes 1327112 | tf_op jit(solution)/shard_map/ppermute | solution.py:677
  54.1 13.0 %collective-permute-start.11 = (bf16[3,128,768]{2,1,0:T(8,128)(2,1)}, bf16[3,128,768]{2,1,0:T(8,128)(2,1)S(1)}, u32[]{:S(2)}, u32[]{:S(2)}) collective-permute-start(bf16[3,128,768]{2,1,0:T(8,128)(2,1)} %slice.157), channel_id=1, source_target_pairs={{0,96},{4,28},{8,104},{12,20},{16,112},{20,12},{24,120},{28,4},{32... | collective-permute-start | bytes 1769480 | tf_op jit(solution)/shard_map/ppermute | solution.py:677
  105.3 19.6 %collective-permute-start.20 = (bf16[2,4,128,768]{3,2,1,0:T(8,128)(2,1)S(1)}, bf16[2,4,128,768]{3,2,1,0:T(8,128)(2,1)S(1)}, u32[]{:S(2)}, u32[]{:S(2)}) collective-permute-start(bf16[2,4,128,768]{3,2,1,0:T(8,128)(2,1)S(1)} %add_convert_fusion), channel_id=1, source_target_pairs={{0,32},{4,12},{8,40},{12,4},{16,48},{20,28},{24,56},{28,20},{32,0}... | collective-permute-start | bytes 4718600 | tf_op jit(solution)/shard_map/ppermute | solution.py:677
  107.9 17.0 %collective-permute-start.21 = (bf16[2,4,96,768]{3,2,1,0:T(8,128)(2,1)S(1)}, bf16[2,4,96,768]{3,2,1,0:T(8,128)(2,1)S(1)}, u32[]{:S(2)}, u32[]{:S(2)}) collective-permute-start(bf16[2,4,96,768]{3,2,1,0:T(8,128)(2,1)S(1)} %add_convert_fusion.1), channel_id=1, source_target_pairs={{0,96},{4,28},{8,104},{12,20},{16,112},{20,12},{24,120},{28,4},{32... | collective-permute-start | bytes 3538952 | tf_op jit(solution)/shard_map/ppermute | solution.py:677
  130.1 15.3 %collective-permute-start.23 = (bf16[2,352,768]{2,1,0:T(8,128)(2,1)S(1)}, bf16[2,352,768]{2,1,0:T(8,128)(2,1)S(1)}, u32[]{:S(2)}, u32[]{:S(2)}) collective-permute-start(bf16[2,352,768]{2,1,0:T(8,128)(2,1)S(1)} %add_convert_fusion.2), channel_id=1, source_target_pairs={{0,1},{1,0},{2,3},{3,2},{4,7},{5,6},{6,5},{7,4},{8,9},{9,8},{10,11... | collective-permute-start | bytes 3244040 | tf_op jit(solution)/shard_map/ppermute | solution.py:666
  133.0 12.1 %collective-permute-start.24 = (bf16[4,128,768]{2,1,0:T(8,128)(2,1)S(1)}, bf16[4,128,768]{2,1,0:T(8,128)(2,1)S(1)}, u32[]{:S(2)}, u32[]{:S(2)}) collective-permute-start(bf16[4,128,768]{2,1,0:T(8,128)(2,1)S(1)} %fusion.3), channel_id=1, source_target_pairs={{0,96},{4,28},{8,104},{12,20},{16,112},{20,12},{24,120},{28,4},{32... | collective-permute-start | bytes 2359304 | tf_op jit(solution)/shard_map/ppermute | solution.py:677
  146.4 16.7 %collective-permute-start.27 = (bf16[2,224,768]{2,1,0:T(8,128)(2,1)S(1)}, bf16[2,224,768]{2,1,0:T(8,128)(2,1)S(1)}, u32[]{:S(2)}, u32[]{:S(2)}) collective-permute-start(bf16[2,224,768]{2,1,0:T(8,128)(2,1)S(1)} %fusion.4), channel_id=1, source_target_pairs={{0,1},{1,0},{2,3},{3,2},{4,7},{5,6},{6,5},{7,4},{8,9},{9,8},{10,11... | collective-permute-start | bytes 2064392 | tf_op jit(solution)/shard_map/ppermute | solution.py:666
  148.9 14.2 %collective-permute-start.26 = (bf16[352,768]{1,0:T(8,128)(2,1)S(1)}, bf16[352,768]{1,0:T(8,128)(2,1)S(1)}, u32[]{:S(2)}, u32[]{:S(2)}) collective-permute-start(bf16[352,768]{1,0:T(8,128)(2,1)S(1)} %fusion.7), channel_id=1, source_target_pairs={{0,3},{1,2},{2,1},{3,0},{4,5},{5,4},{6,7},{7,6},{8,11},{9,10},{10,... | collective-permute-start | bytes 1622024 | tf_op jit(solution)/shard_map/ppermute | solution.py:666
  189.6 10.7 %collective-permute-start.34 = (bf16[352,768]{1,0:T(8,128)(2,1)S(1)}, bf16[352,768]{1,0:T(8,128)(2,1)}, u32[]{:S(2)}, u32[]{:S(2)}) collective-permute-start(bf16[352,768]{1,0:T(8,128)(2,1)S(1)} %add_convert_fusion.6), channel_id=1, source_target_pairs={{0,96},{4,28},{8,104},{12,20},{16,112},{20,12},{24,120},{28,4},{32... | collective-permute-start | bytes 1622024 | tf_op jit(solution)/shard_map/ppermute | solution.py:677
  192.7 16.0 %all-to-all-start.1 = ((bf16[4,2,64,768]{3,2,1,0:T(8,128)(2,1)}), bf16[4,2,64,768]{3,2,1,0:T(8,128)(2,1)S(1)}, u32[]{:S(2)}, u32[]{:S(2)}) async-start(bf16[4,2,64,768]{3,2,1,0:T(8,128)(2,1)} %get-tuple-element.146), calls=%async_computation.1 | async-start | bytes 1572864 | tf_op jit(solution)/shard_map/all_to_all | solution.py:696
  196.5 12.1 %collective-permute-start.37 = (bf16[224,768]{1,0:T(8,128)(2,1)S(1)}, bf16[224,768]{1,0:T(8,128)(2,1)S(1)}, u32[]{:S(2)}, u32[]{:S(2)}) collective-permute-start(bf16[224,768]{1,0:T(8,128)(2,1)S(1)} %add_convert_fusion.10), channel_id=1, source_target_pairs={{0,96},{4,28},{8,104},{12,20},{16,112},{20,12},{24,120},{28,4},{32... | collective-permute-start | bytes 1032200 | tf_op jit(solution)/shard_map/ppermute | solution.py:677
  196.7 11.8 %collective-permute-start.36 = (bf16[224,768]{1,0:T(8,128)(2,1)S(1)}, bf16[224,768]{1,0:T(8,128)(2,1)S(1)}, u32[]{:S(2)}, u32[]{:S(2)}) collective-permute-start(bf16[224,768]{1,0:T(8,128)(2,1)S(1)} %add_convert_fusion.10), channel_id=1, source_target_pairs={{0,64},{4,20},{8,72},{12,28},{16,80},{20,4},{24,88},{28,12},{32,96... | collective-permute-start | bytes 1032200 | tf_op jit(solution)/shard_map/ppermute | solution.py:677
  197.9 10.6 %collective-permute-start.35 = (bf16[224,768]{1,0:T(8,128)(2,1)S(1)}, bf16[224,768]{1,0:T(8,128)(2,1)S(1)}, u32[]{:S(2)}, u32[]{:S(2)}) collective-permute-start(bf16[224,768]{1,0:T(8,128)(2,1)S(1)} %add_convert_fusion.10), channel_id=1, source_target_pairs={{0,32},{4,12},{8,40},{12,4},{16,48},{20,28},{24,56},{28,20},{32,0}... | collective-permute-start | bytes 1032200 | tf_op jit(solution)/shard_map/ppermute | solution.py:677
  (30 other events, 258.8 us)
where the time goes:
time: 226 us; the launch traced here: 223 us
  waiting for transfers between devices  89.4 us (40%)
  Pallas kernels  66.2 us (29%)
  starting transfers between devices  50.8 us (22%)
  other arithmetic  7.84 us (3%)
  local copies, waits for them, and re-layouts  7.15 us (3%)
    ppermute x10, waiting for transfers between devices, hop_x(): return lax.ppermute(value, ('core', 'shard'), pairs)  43.3 us
    ppermute x17, waiting for transfers between devices, hop_yz(): return lax.ppermute(value, ('y', 'z', 'core'), pairs)  36.7 us
    ppermute x17, starting transfers between devices, hop_yz(): return lax.ppermute(value, ('y', 'z', 'core'), pairs)  25.3 us
    pallas_call x1, Pallas kernels, feed(): pl.pallas_call(feed_body, out_shape=(shape((ROWS, D), LOW), shape((ROWS,...  22.1 us
    pallas_call x1, Pallas kernels, attend_back_two(): pl.pallas_call(attend_back_two_body, out_shape=(shape((GROUP, 2, PART, D)...  14.4 us
    pallas_call x1, Pallas kernels, attend_forward(): pl.pallas_call(attend_forward_body, out_shape=(*(shape((ROWS, D), LOW),)...  10.2 us
    ppermute x10, starting transfers between devices, hop_x(): return lax.ppermute(value, ('core', 'shard'), pairs)  9.5 us
    ppermute x12, waiting for transfers between devices, swap(): return lax.ppermute(value, 'core', [(0, 1), (1, 0)])  9.44 us
  transfers between devices with their start and end apart: 41, of which 21 were waited for; matrix products, arithmetic and copies ran while one was open for 4% of the time, Pallas kernels for 16%

commit v1 on v0

--- a/solution.py
+++ b/solution.py
@@ -598,7 +598,7 @@
             pltpu.VMEM((GROUP, ROWS, D), F32), pltpu.VMEM((2, GROUP, SECOND, D), LOW),
             pltpu.VMEM((2, GROUP, HALF, WIDE), LOW), pltpu.SemaphoreType.DMA((24,)),
         ],
-        compiler_params=pltpu.CompilerParams(vmem_limit_bytes=48 * MIB),
+        compiler_params=pltpu.CompilerParams(vmem_limit_bytes=28 * MIB),
         cost_estimate=pl.CostEstimate(flops=16_000_000_000, bytes_accessed=60_000_000, transcendentals=1_600_000),
         name="feed",
     )(meta, tok, ctx_one, ctx_two, rows, *own, *pieces)

time: 226 us -> 219 us (0.969)
  Pallas kernels: 66.2 us -> 60.8 us
    pallas_call x1, Pallas kernels: 22.1 us -> 16.6 us  [feed(): pl.pallas_call(feed_body, out_shape=(shape((ROWS, D), LOW), shape((ROWS,...]
  transfers between devices with their start and end apart: 41 -> 41, of which waited for: 21 -> 21; matrix products, arithmetic and copies ran while one was open for 4% -> 3% of each run, Pallas kernels for 16% -> 17%
where the time goes in v1:
time: 219 us; the launch traced here: 216 us
  waiting for transfers between devices  87.6 us (40%)
  Pallas kernels  60.8 us (28%)
  starting transfers between devices  52 us (24%)
  local copies, waits for them, and re-layouts  7.94 us (4%)
  other arithmetic  6.86 us (3%)
    ppermute x10, waiting for transfers between devices, hop_x(): return lax.ppermute(value, ('core', 'shard'), pairs)  42.9 us
    ppermute x17, waiting for transfers between devices, hop_yz(): return lax.ppermute(value, ('y', 'z', 'core'), pairs)  35.5 us
    ppermute x17, starting transfers between devices, hop_yz(): return lax.ppermute(value, ('y', 'z', 'core'), pairs)  25.8 us
    pallas_call x1, Pallas kernels, feed(): pl.pallas_call(feed_body, out_shape=(shape((ROWS, D), LOW), shape((ROWS,...  16.6 us
    pallas_call x1, Pallas kernels, attend_back_two(): pl.pallas_call(attend_back_two_body, out_shape=(shape((GROUP, 2, PART, D)...  14.4 us
    pallas_call x1, Pallas kernels, attend_forward(): pl.pallas_call(attend_forward_body, out_shape=(*(shape((ROWS, D), LOW),)...  10.3 us
    ppermute x10, starting transfers between devices, hop_x(): return lax.ppermute(value, ('core', 'shard'), pairs)  9.98 us
    ppermute x12, waiting for transfers between devices, swap(): return lax.ppermute(value, 'core', [(0, 1), (1, 0)])  9.23 us
  transfers between devices with their start and end apart: 41, of which 21 were waited for; matrix products, arithmetic and copies ran while one was open for 3% of the time, Pallas kernels for 17%

profile of v1, /device:TPU:17, one launch (start us, length us, event | category | flops | bytes accessed | tf_op | source)
XLA Modules:
  0.0 216.2 jit_solution(10892857032847769640)
XLA Ops:
  2.7 3.5 %pack.1 = (s32[16]{0:T(128)}, bf16[352,768]{1,0:T(8,128)(2,1)}, bf16[224,768]{1,0:T(8,128)(2,1)}, bf16[4,2,64,768]{3,2,1,0:T(8,128)(2,1)}) custom-call(s32[4]{0:T(128)} %pad_add_fusion.1.coord_ref, s32[4]{0:T(128)} %length_ref.1, bf16[4,64,768]{2,1,0:T(8,128)(2,1)} %hidden_ref.1, bf16[4,64,768]{2,1,0:T(8,128)(2,1)} %grad_ref.1, bf16[192,768]{1,0:T(8,128)(2,1)} %own_q.1, ...), custom_call_target="tpu_custom_call" | custom-call | tf_op jit(solution)/shard_map/pack/pallas_call | solution.py:166
  10.4 4.2 %collective-permute-done = bf16[224,768]{1,0:T(8,128)(2,1)S(1)} collective-permute-done((bf16[224,768]{1,0:T(8,128)(2,1)}, bf16[224,768]{1,0:T(8,128)(2,1)S(1)}, u32[]{:S(2)}, u32[]{:S(2)}) %collective-permute-start) | collective-permute-done | bytes 344096 | tf_op jit(solution)/shard_map/ppermute | solution.py:666
  14.6 11.5 %collective-permute-done.3.p0 = bf16[352,768]{1,0:T(8,128)(2,1)} collective-permute-done((bf16[352,768]{1,0:T(8,128)(2,1)}, bf16[352,768]{1,0:T(8,128)(2,1)}, u32[]{:S(2)}, u32[]{:S(2)}) %collective-permute-start.3) | collective-permute-done | bytes 540704 | tf_op jit(solution)/shard_map/ppermute | solution.py:666
  26.2 3.0 %collective-permute-done.1 = bf16[224,768]{1,0:T(8,128)(2,1)S(1)} collective-permute-done((bf16[224,768]{1,0:T(8,128)(2,1)}, bf16[224,768]{1,0:T(8,128)(2,1)S(1)}, u32[]{:S(2)}, u32[]{:S(2)}) %collective-permute-start.1) | collective-permute-done | bytes 344096 | tf_op jit(solution)/shard_map/ppermute | solution.py:666
  29.3 3.7 %collective-permute-done.2 = bf16[224,768]{1,0:T(8,128)(2,1)S(1)} collective-permute-done((bf16[224,768]{1,0:T(8,128)(2,1)S(1)}, bf16[224,768]{1,0:T(8,128)(2,1)S(1)}, u32[]{:S(2)}, u32[]{:S(2)}) %collective-permute-start.2) | collective-permute-done | bytes 344096 | tf_op jit(solution)/shard_map/ppermute | solution.py:666
  33.1 3.8 %collective-permute-start.6 = (bf16[3,224,768]{2,1,0:T(8,128)(2,1)S(1)}, bf16[3,224,768]{2,1,0:T(8,128)(2,1)}, u32[]{:S(2)}, u32[]{:S(2)}) collective-permute-start(bf16[3,224,768]{2,1,0:T(8,128)(2,1)S(1)} %pad_maximum_fusion.rest_0_), channel_id=1, source_target_pairs={{0,96},{4,28},{8,104},{12,20},{16,112},{20,12},{24,120},{28,4},{32... | collective-permute-start | bytes 3096584 | tf_op jit(solution)/shard_map/ppermute | solution.py:677
  36.9 4.3 %all-to-all-start = ((bf16[4,2,64,768]{3,2,1,0:T(8,128)(2,1)}), bf16[4,2,64,768]{3,2,1,0:T(8,128)(2,1)S(1)}, u32[]{:S(2)}, u32[]{:S(2)}) async-start(bf16[4,2,64,768]{3,2,1,0:T(8,128)(2,1)} %get-tuple-element.87), calls=%async_computation | async-start | bytes 1572864 | tf_op jit(solution)/shard_map/all_to_all | solution.py:696
  42.8 6.4 %collective-permute-done.6.rest_2_ = bf16[3,224,768]{2,1,0:T(8,128)(2,1)} collective-permute-done((bf16[3,224,768]{2,1,0:T(8,128)(2,1)S(1)}, bf16[3,224,768]{2,1,0:T(8,128)(2,1)}, u32[]{:S(2)}, u32[]{:S(2)}) %collective-permute-start.6) | collective-permute-done | bytes 1032224 | tf_op jit(solution)/shard_map/ppermute | solution.py:677
  57.3 10.3 %attend_forward.1 = (bf16[256,768]{1,0:T(8,128)(2,1)S(1)}, bf16[256,768]{1,0:T(8,128)(2,1)S(1)}, bf16[256,768]{1,0:T(8,128)(2,1)S(1)}, bf16[256,768]{1,0:T(8,128...) custom-call(s32[16]{0:T(128)S(1)} %copy-done.12, ...), custom_call_target="tpu_custom_call" | custom-call | flops 12000000000 | bytes 40000000 | tf_op jit(solution)/shard_map/attend_forward/pallas_call | solution.py:294
  68.8 5.5 %attend_forward_two.1 = (bf16[6,256,256]{2,1,0:T(8,128)(2,1)S(1)}, bf16[256,384]{1,0:T(8,128)(2,1)S(1)}) custom-call(s32[16]{0:T(128)S(1)} %copy-done.12, bf16[256,768]{1,0:T(8,128)(2,1)S(1)} %get-tuple-element.92.q_ref, bf16[256,768]{1,0:T(8,128)(2,1)S(1)} %get-tuple-element.93.k_ref, bf16[256,768]{1,0:T(8,128)(2,1)S(1)} %get-tuple-element.94.v_ref, ...), custom_call_target="tpu_custom_call" | custom-call | flops 8000000000 | bytes 20000000 | tf_op jit(solution)/shard_map/attend_forward_two/pallas_call | solution.py:315
  75.0 16.6 %feed.1 = (bf16[256,768]{1,0:T(8,128)(2,1)S(1)}, bf16[256,768]{1,0:T(8,128)(2,1)S(1)}, f32[256,768]{1,0:T(8,128)S(1)}, bf16[4,4,128,768]{3,2,1,0:T(8,128)(2,1)S(...) custom-call(s32[16]{0:T(128)S(1)} %copy-done.12, ...), custom_call_target="tpu_custom_call" | custom-call | flops 16000000000 | bytes 60000000 | tf_op jit(solution)/shard_map/feed/pallas_call | solution.py:589
  92.2 6.0 %attend_back_one.1 = (bf16[256,384]{1,0:T(8,128)(2,1)S(1)}, bf16[256,384]{1,0:T(8,128)(2,1)S(1)}, bf16[256,384]{1,0:T(8,128)(2,1)S(1)}, bf16[512,384]{1,0:T(8,128)(2,1)S(1)}, bf16[512,384]{1,0:T(8,128)(2,1)S(1)}) custom-call(bf16[256,768]{1,0:T(8,128)(2,1)S(1)} %get-tuple-element.92.q_ref, bf16[256,768]{1,0:T(8,128)(2,1)S(1)} %get-tuple-element.93.k_ref, ...), custom_call_target="tpu_custom_call" | custom-call | flops 8000000000 | bytes 20000000 | tf_op jit(solution)/shard_map/attend_back_one/pallas_call | solution.py:432
  103.9 14.4 %attend_back_two.1 = (bf16[4,2,64,768]{3,2,1,0:T(8,128)(2,1)}, bf16[4,352,768]{2,1,0:T(8,128)(2,1)S(1)}, bf16[4,352,768]{2,1,0:T(8,128)(2,1)S(1)}) custom-call(s32[16]{0:T(128)S(1)} %copy-done.12, bf16[256,768]{1,0:T(8,128)(2,1)S(1)} %get-tuple-element.92.q_ref, bf16[256,768]{1,0:T(8,128)(2,1)S(1)} %get-tuple-element.93.k_ref, ...), custom_call_target="tpu_custom_call" | custom-call | flops 14000000000 | bytes 40000000 | tf_op jit(solution)/shard_map/attend_back_two/pallas_call | solution.py:447
  119.3 3.9 %collective-permute-done.22 = bf16[4,352,768]{2,1,0:T(8,128)(2,1)S(1)} collective-permute-done((bf16[4,352,768]{2,1,0:T(8,128)(2,1)S(1)}, bf16[4,352,768]{2,1,0:T(8,128)(2,1)S(1)}, u32[]{:S(2)}, u32[]{:S(2)}) %collective-permute-start.22) | collective-permute-done | bytes 2162720 | tf_op jit(solution)/shard_map/ppermute | solution.py:681
  129.5 9.0 %collective-permute-done.25 = bf16[4,96,768]{2,1,0:T(8,128)(2,1)S(1)} collective-permute-done((bf16[4,96,768]{2,1,0:T(8,128)(2,1)S(1)}, bf16[4,96,768]{2,1,0:T(8,128)(2,1)S(1)}, u32[]{:S(2)}, u32[]{:S(2)}) %collective-permute-start.25) | collective-permute-done | bytes 589856 | tf_op jit(solution)/shard_map/ppermute | solution.py:677
  142.5 14.0 %collective-permute-done.26 = bf16[352,768]{1,0:T(8,128)(2,1)S(1)} collective-permute-done((bf16[352,768]{1,0:T(8,128)(2,1)S(1)}, bf16[352,768]{1,0:T(8,128)(2,1)S(1)}, u32[]{:S(2)}, u32[]{:S(2)}) %collective-permute-start.26) | collective-permute-done | bytes 540704 | tf_op jit(solution)/shard_map/ppermute | solution.py:666
  158.4 6.3 %collective-permute-done.29 = bf16[224,768]{1,0:T(8,128)(2,1)S(1)} collective-permute-done((bf16[224,768]{1,0:T(8,128)(2,1)S(1)}, bf16[224,768]{1,0:T(8,128)(2,1)S(1)}, u32[]{:S(2)}, u32[]{:S(2)}) %collective-permute-start.29) | collective-permute-done | bytes 344096 | tf_op jit(solution)/shard_map/ppermute | solution.py:666
  168.4 5.5 %collective-permute-done.31 = bf16[224,768]{1,0:T(8,128)(2,1)S(1)} collective-permute-done((bf16[224,768]{1,0:T(8,128)(2,1)S(1)}, bf16[224,768]{1,0:T(8,128)(2,1)S(1)}, u32[]{:S(2)}, u32[]{:S(2)}) %collective-permute-start.31) | collective-permute-done | bytes 344096 | tf_op jit(solution)/shard_map/ppermute | solution.py:677
  177.0 4.9 %collective-permute-done.33 = bf16[224,768]{1,0:T(8,128)(2,1)S(1)} collective-permute-done((bf16[224,768]{1,0:T(8,128)(2,1)S(1)}, bf16[224,768]{1,0:T(8,128)(2,1)S(1)}, u32[]{:S(2)}, u32[]{:S(2)}) %collective-permute-start.33) | collective-permute-done | bytes 344096 | tf_op jit(solution)/shard_map/ppermute | solution.py:677
  186.2 3.7 %all-to-all-start.1 = ((bf16[4,2,64,768]{3,2,1,0:T(8,128)(2,1)}), bf16[4,2,64,768]{3,2,1,0:T(8,128)(2,1)S(1)}, u32[]{:S(2)}, u32[]{:S(2)}) async-start(bf16[4,2,64,768]{3,2,1,0:T(8,128)(2,1)} %get-tuple-element.146), calls=%async_computation.1 | async-start | bytes 1572864 | tf_op jit(solution)/shard_map/all_to_all | solution.py:696
  195.1 6.9 %collective-permute-done.35 = bf16[224,768]{1,0:T(8,128)(2,1)S(1)} collective-permute-done((bf16[224,768]{1,0:T(8,128)(2,1)S(1)}, bf16[224,768]{1,0:T(8,128)(2,1)S(1)}, u32[]{:S(2)}, u32[]{:S(2)}) %collective-permute-start.35) | collective-permute-done | bytes 344096 | tf_op jit(solution)/shard_map/ppermute | solution.py:677
  202.1 4.9 %collective-permute-start.38 = (bf16[1248,768]{1,0:T(8,128)(2,1)S(1)}, bf16[1248,768]{1,0:T(8,128)(2,1)S(1)}, u32[]{:S(2)}, u32[]{:S(2)}) collective-permute-start(bf16[1248,768]{1,0:T(8,128)(2,1)S(1)} %constant_dynamic-update-slice_fusion.mine), channel_id=1, source_target_pairs={{0,4},{4,0},{1,5},{5,1},{2,6},{6,2},{3,7},{7,3},{8,12},{12,8},{9,1... | collective-permute-start | bytes 5750792 | tf_op jit(solution)/shard_map/ppermute | solution.py:681
  207.0 3.5 %collective-permute-done.38.other = bf16[1248,768]{1,0:T(8,128)(2,1)S(1)} collective-permute-done((bf16[1248,768]{1,0:T(8,128)(2,1)S(1)}, bf16[1248,768]{1,0:T(8,128)(2,1)S(1)}, u32[]{:S(2)}, u32[]{:S(2)}) %collective-permute-start.38) | collective-permute-done | bytes 1916960 | tf_op jit(solution)/shard_map/ppermute | solution.py:681
  210.5 4.5 %finish.1 = (f32[192,768]{1,0:T(8,128)}, f32[192,768]{1,0:T(8,128)}, f32[192,768]{1,0:T(8,128)}, f32[128,768]{1,0:T(8,128)}, f32[768,768]{1,0:T(8,128)}, /*index...) custom-call(s32[16]{0:T(128)S(1)} %copy-done.12, ...), custom_call_target="tpu_custom_call" | custom-call | tf_op jit(solution)/shard_map/finish/pallas_call | solution.py:647
  (128 shorter events, 54.8 us)
Async XLA Ops:
  8.7 17.4 %collective-permute-start.3 = (bf16[352,768]{1,0:T(8,128)(2,1)}, bf16[352,768]{1,0:T(8,128)(2,1)}, u32[]{:S(2)}, u32[]{:S(2)}) collective-permute-start(bf16[352,768]{1,0:T(8,128)(2,1)} %get-tuple-element.89), channel_id=1, source_target_pairs={{0,1},{1,0},{2,3},{3,2},{4,7},{5,6},{6,5},{7,4},{8,9},{9,8},{10,11... | collective-permute-start | bytes 1622024 | tf_op jit(solution)/shard_map/ppermute | solution.py:666
  8.9 24.1 %collective-permute-start.4 = (bf16[352,768]{1,0:T(8,128)(2,1)}, bf16[352,768]{1,0:T(8,128)(2,1)}, u32[]{:S(2)}, u32[]{:S(2)}) collective-permute-start(bf16[352,768]{1,0:T(8,128)(2,1)} %get-tuple-element.89), channel_id=1, source_target_pairs={{0,3},{1,2},{2,1},{3,0},{4,5},{5,4},{6,7},{7,6},{8,11},{9,10},{10,... | collective-permute-start | bytes 1622024 | tf_op jit(solution)/shard_map/ppermute | solution.py:666
  8.9 20.3 %collective-permute-start.1 = (bf16[224,768]{1,0:T(8,128)(2,1)}, bf16[224,768]{1,0:T(8,128)(2,1)S(1)}, u32[]{:S(2)}, u32[]{:S(2)}) collective-permute-start(bf16[224,768]{1,0:T(8,128)(2,1)} %get-tuple-element.88), channel_id=1, source_target_pairs={{0,3},{1,2},{2,1},{3,0},{4,5},{5,4},{6,7},{7,6},{8,11},{9,10},{10,... | collective-permute-start | bytes 1032200 | tf_op jit(solution)/shard_map/ppermute | solution.py:666
  14.6 18.3 %collective-permute-start.2 = (bf16[224,768]{1,0:T(8,128)(2,1)S(1)}, bf16[224,768]{1,0:T(8,128)(2,1)S(1)}, u32[]{:S(2)}, u32[]{:S(2)}) collective-permute-start(bf16[224,768]{1,0:T(8,128)(2,1)S(1)} %collective-permute-done), channel_id=1, source_target_pairs={{0,3},{1,2},{2,1},{3,0},{4,5},{5,4},{6,7},{7,6},{8,11},{9,10},{10,... | collective-permute-start | bytes 1032200 | tf_op jit(solution)/shard_map/ppermute | solution.py:666
  26.1 15.6 %collective-permute-start.7 = (bf16[352,768]{1,0:T(8,128)(2,1)}, bf16[352,768]{1,0:T(8,128)(2,1)}, u32[]{:S(2)}, u32[]{:S(2)}) collective-permute-start(bf16[352,768]{1,0:T(8,128)(2,1)} %collective-permute-done.3.p0), channel_id=1, source_target_pairs={{0,3},{1,2},{2,1},{3,0},{4,5},{5,4},{6,7},{7,6},{8,11},{9,10},{10,... | collective-permute-start | bytes 1622024 | tf_op jit(solution)/shard_map/ppermute | solution.py:666
  33.1 16.1 %collective-permute-start.6 = (bf16[3,224,768]{2,1,0:T(8,128)(2,1)S(1)}, bf16[3,224,768]{2,1,0:T(8,128)(2,1)}, u32[]{:S(2)}, u32[]{:S(2)}) collective-permute-start(bf16[3,224,768]{2,1,0:T(8,128)(2,1)S(1)} %pad_maximum_fusion.rest_0_), channel_id=1, source_target_pairs={{0,96},{4,28},{8,104},{12,20},{16,112},{20,12},{24,120},{28,4},{32... | collective-permute-start | bytes 3096584 | tf_op jit(solution)/shard_map/ppermute | solution.py:677
  36.9 14.1 %collective-permute-start.5 = (bf16[3,224,768]{2,1,0:T(8,128)(2,1)S(1)}, bf16[3,224,768]{2,1,0:T(8,128)(2,1)S(1)}, u32[]{:S(2)}, u32[]{:S(2)}) collective-permute-start(bf16[3,224,768]{2,1,0:T(8,128)(2,1)S(1)} %pad_maximum_fusion.rest_0_), channel_id=1, source_target_pairs={{0,32},{4,12},{8,40},{12,4},{16,48},{20,28},{24,56},{28,20},{32,0}... | collective-permute-start | bytes 3096584 | tf_op jit(solution)/shard_map/ppermute | solution.py:677
  36.9 17.4 %all-to-all-start = ((bf16[4,2,64,768]{3,2,1,0:T(8,128)(2,1)}), bf16[4,2,64,768]{3,2,1,0:T(8,128)(2,1)S(1)}, u32[]{:S(2)}, u32[]{:S(2)}) async-start(bf16[4,2,64,768]{3,2,1,0:T(8,128)(2,1)} %get-tuple-element.87), calls=%async_computation | async-start | bytes 1572864 | tf_op jit(solution)/shard_map/all_to_all | solution.py:696
  41.2 13.2 %collective-permute-start.9 = (bf16[352,768]{1,0:T(8,128)(2,1)}, bf16[352,768]{1,0:T(8,128)(2,1)}, u32[]{:S(2)}, u32[]{:S(2)}) collective-permute-start(bf16[352,768]{1,0:T(8,128)(2,1)} %collective-permute-done.4.p1), channel_id=1, source_target_pairs={{0,4},{4,0},{1,5},{5,1},{2,6},{6,2},{3,7},{7,3},{8,12},{12,8},{9,1... | collective-permute-start | bytes 1622024 | tf_op jit(solution)/shard_map/ppermute | solution.py:681
  41.2 13.2 %collective-permute-start.8 = (bf16[352,768]{1,0:T(8,128)(2,1)}, bf16[352,768]{1,0:T(8,128)(2,1)}, u32[]{:S(2)}, u32[]{:S(2)}) collective-permute-start(bf16[352,768]{1,0:T(8,128)(2,1)} %collective-permute-done.3.p0), channel_id=1, source_target_pairs={{0,4},{4,0},{1,5},{5,1},{2,6},{6,2},{3,7},{7,3},{8,12},{12,8},{9,1... | collective-permute-start | bytes 1622024 | tf_op jit(solution)/shard_map/ppermute | solution.py:681
  41.7 12.7 %collective-permute-start.10 = (bf16[352,768]{1,0:T(8,128)(2,1)}, bf16[352,768]{1,0:T(8,128)(2,1)}, u32[]{:S(2)}, u32[]{:S(2)}) collective-permute-start(bf16[352,768]{1,0:T(8,128)(2,1)} %collective-permute-done.7.p2), channel_id=1, source_target_pairs={{0,4},{4,0},{1,5},{5,1},{2,6},{6,2},{3,7},{7,3},{8,12},{12,8},{9,1... | collective-permute-start | bytes 1622024 | tf_op jit(solution)/shard_map/ppermute | solution.py:681
  51.0 16.6 %collective-permute-start.12 = (bf16[3,96,768]{2,1,0:T(8,128)(2,1)}, bf16[3,96,768]{2,1,0:T(8,128)(2,1)}, u32[]{:S(2)}, u32[]{:S(2)}) collective-permute-start(bf16[3,96,768]{2,1,0:T(8,128)(2,1)} %slice.158), channel_id=1, source_target_pairs={{0,32},{4,12},{8,40},{12,4},{16,48},{20,28},{24,56},{28,20},{32,0}... | collective-permute-start | bytes 1327112 | tf_op jit(solution)/shard_map/ppermute | solution.py:677
  51.9 15.7 %collective-permute-start.11 = (bf16[3,128,768]{2,1,0:T(8,128)(2,1)}, bf16[3,128,768]{2,1,0:T(8,128)(2,1)}, u32[]{:S(2)}, u32[]{:S(2)}) collective-permute-start(bf16[3,128,768]{2,1,0:T(8,128)(2,1)} %slice.157), channel_id=1, source_target_pairs={{0,96},{4,28},{8,104},{12,20},{16,112},{20,12},{24,120},{28,4},{32... | collective-permute-start | bytes 1769480 | tf_op jit(solution)/shard_map/ppermute | solution.py:677
  98.7 19.6 %collective-permute-start.20 = (bf16[2,4,128,768]{3,2,1,0:T(8,128)(2,1)S(1)}, bf16[2,4,128,768]{3,2,1,0:T(8,128)(2,1)S(1)}, u32[]{:S(2)}, u32[]{:S(2)}) collective-permute-start(bf16[2,4,128,768]{3,2,1,0:T(8,128)(2,1)S(1)} %add_convert_fusion), channel_id=1, source_target_pairs={{0,32},{4,12},{8,40},{12,4},{16,48},{20,28},{24,56},{28,20},{32,0}... | collective-permute-start | bytes 4718600 | tf_op jit(solution)/shard_map/ppermute | solution.py:677
  101.1 17.2 %collective-permute-start.21 = (bf16[2,4,96,768]{3,2,1,0:T(8,128)(2,1)S(1)}, bf16[2,4,96,768]{3,2,1,0:T(8,128)(2,1)S(1)}, u32[]{:S(2)}, u32[]{:S(2)}) collective-permute-start(bf16[2,4,96,768]{3,2,1,0:T(8,128)(2,1)S(1)} %add_convert_fusion.1), channel_id=1, source_target_pairs={{0,96},{4,28},{8,104},{12,20},{16,112},{20,12},{24,120},{28,4},{32... | collective-permute-start | bytes 3538952 | tf_op jit(solution)/shard_map/ppermute | solution.py:677
  123.5 15.3 %collective-permute-start.23 = (bf16[2,352,768]{2,1,0:T(8,128)(2,1)S(1)}, bf16[2,352,768]{2,1,0:T(8,128)(2,1)S(1)}, u32[]{:S(2)}, u32[]{:S(2)}) collective-permute-start(bf16[2,352,768]{2,1,0:T(8,128)(2,1)S(1)} %add_convert_fusion.2), channel_id=1, source_target_pairs={{0,1},{1,0},{2,3},{3,2},{4,7},{5,6},{6,5},{7,4},{8,9},{9,8},{10,11... | collective-permute-start | bytes 3244040 | tf_op jit(solution)/shard_map/ppermute | solution.py:666
  126.5 12.1 %collective-permute-start.24 = (bf16[4,128,768]{2,1,0:T(8,128)(2,1)S(1)}, bf16[4,128,768]{2,1,0:T(8,128)(2,1)S(1)}, u32[]{:S(2)}, u32[]{:S(2)}) collective-permute-start(bf16[4,128,768]{2,1,0:T(8,128)(2,1)S(1)} %fusion.3), channel_id=1, source_target_pairs={{0,96},{4,28},{8,104},{12,20},{16,112},{20,12},{24,120},{28,4},{32... | collective-permute-start | bytes 2359304 | tf_op jit(solution)/shard_map/ppermute | solution.py:677
  139.7 16.7 %collective-permute-start.27 = (bf16[2,224,768]{2,1,0:T(8,128)(2,1)S(1)}, bf16[2,224,768]{2,1,0:T(8,128)(2,1)S(1)}, u32[]{:S(2)}, u32[]{:S(2)}) collective-permute-start(bf16[2,224,768]{2,1,0:T(8,128)(2,1)S(1)} %fusion.4), channel_id=1, source_target_pairs={{0,1},{1,0},{2,3},{3,2},{4,7},{5,6},{6,5},{7,4},{8,9},{9,8},{10,11... | collective-permute-start | bytes 2064392 | tf_op jit(solution)/shard_map/ppermute | solution.py:666
  142.5 14.0 %collective-permute-start.26 = (bf16[352,768]{1,0:T(8,128)(2,1)S(1)}, bf16[352,768]{1,0:T(8,128)(2,1)S(1)}, u32[]{:S(2)}, u32[]{:S(2)}) collective-permute-start(bf16[352,768]{1,0:T(8,128)(2,1)S(1)} %fusion.7), channel_id=1, source_target_pairs={{0,3},{1,2},{2,1},{3,0},{4,5},{5,4},{6,7},{7,6},{8,11},{9,10},{10,... | collective-permute-start | bytes 1622024 | tf_op jit(solution)/shard_map/ppermute | solution.py:666
  183.1 10.7 %collective-permute-start.34 = (bf16[352,768]{1,0:T(8,128)(2,1)S(1)}, bf16[352,768]{1,0:T(8,128)(2,1)}, u32[]{:S(2)}, u32[]{:S(2)}) collective-permute-start(bf16[352,768]{1,0:T(8,128)(2,1)S(1)} %add_convert_fusion.6), channel_id=1, source_target_pairs={{0,96},{4,28},{8,104},{12,20},{16,112},{20,12},{24,120},{28,4},{32... | collective-permute-start | bytes 1622024 | tf_op jit(solution)/shard_map/ppermute | solution.py:677
  186.2 15.9 %all-to-all-start.1 = ((bf16[4,2,64,768]{3,2,1,0:T(8,128)(2,1)}), bf16[4,2,64,768]{3,2,1,0:T(8,128)(2,1)S(1)}, u32[]{:S(2)}, u32[]{:S(2)}) async-start(bf16[4,2,64,768]{3,2,1,0:T(8,128)(2,1)} %get-tuple-element.146), calls=%async_computation.1 | async-start | bytes 1572864 | tf_op jit(solution)/shard_map/all_to_all | solution.py:696
  190.0 12.1 %collective-permute-start.37 = (bf16[224,768]{1,0:T(8,128)(2,1)S(1)}, bf16[224,768]{1,0:T(8,128)(2,1)S(1)}, u32[]{:S(2)}, u32[]{:S(2)}) collective-permute-start(bf16[224,768]{1,0:T(8,128)(2,1)S(1)} %add_convert_fusion.10), channel_id=1, source_target_pairs={{0,96},{4,28},{8,104},{12,20},{16,112},{20,12},{24,120},{28,4},{32... | collective-permute-start | bytes 1032200 | tf_op jit(solution)/shard_map/ppermute | solution.py:677
  190.2 11.8 %collective-permute-start.36 = (bf16[224,768]{1,0:T(8,128)(2,1)S(1)}, bf16[224,768]{1,0:T(8,128)(2,1)S(1)}, u32[]{:S(2)}, u32[]{:S(2)}) collective-permute-start(bf16[224,768]{1,0:T(8,128)(2,1)S(1)} %add_convert_fusion.10), channel_id=1, source_target_pairs={{0,64},{4,20},{8,72},{12,28},{16,80},{20,4},{24,88},{28,12},{32,96... | collective-permute-start | bytes 1032200 | tf_op jit(solution)/shard_map/ppermute | solution.py:677
  191.4 10.6 %collective-permute-start.35 = (bf16[224,768]{1,0:T(8,128)(2,1)S(1)}, bf16[224,768]{1,0:T(8,128)(2,1)S(1)}, u32[]{:S(2)}, u32[]{:S(2)}) collective-permute-start(bf16[224,768]{1,0:T(8,128)(2,1)S(1)} %add_convert_fusion.10), channel_id=1, source_target_pairs={{0,32},{4,12},{8,40},{12,4},{16,48},{20,28},{24,56},{28,20},{32,0}... | collective-permute-start | bytes 1032200 | tf_op jit(solution)/shard_map/ppermute | solution.py:677
  (31 other events, 223.6 us)

commit v2 on v1

--- a/solution.py
+++ b/solution.py
@@ -323,6 +323,11 @@
     )(meta, *saved)
 
 
+def both_heads(pair, side):
+    zero = jnp.zeros_like(pair)
+    return jnp.concatenate([jnp.where(side == h, pair, zero) for h in range(2)], axis=0)
+
+
 def heads_back(first_pair, count, refs, outs):
     q_ref, k_ref, v_ref, pk_ref, pq_ref, probs_ref, gctx_ref = refs
     gq_ref, gk_ref, gv_ref, gpk_ref, gpq_ref, qr_ref, kr_ref = outs
@@ -338,26 +343,37 @@
         q_pair, k_pair, v_pair = q_ref[:, cols], k_ref[:, cols], v_ref[:, cols]
         pk_pair, pq_pair, gctx_pair = pk_ref[:, cols], pq_ref[:, cols], gctx_ref[:, cols]
         qr_pair, kr_pair = qr_ref[:, cols], kr_ref[:, cols]
-        zero = jnp.zeros_like(q_pair)
-        parts = []
+        grad_probs_both = mm_nt(both_heads(gctx_pair, side), v_pair)
+        scores_both, probs_both = [], []
         for h in range(2):
-            gctx_head = jnp.where(side == h, gctx_pair, zero)
-            grad_probs = mm_nt(gctx_head, v_pair)
+            grad_probs = grad_probs_both[h * ROWS : (h + 1) * ROWS]
             probs_low = probs_ref[2 * (pair - first_pair) + h]
             probs = probs_low.astype(F32)
             inner = jnp.sum(probs * grad_probs, axis=1, keepdims=True)
-            grad_scores = (probs * (grad_probs - inner)).astype(LOW)
-            g_value = mm_tn(probs_low, gctx_pair)
-            rows_back = mm(flip, grad_scores)
-            cols_back = mm_nt(flip, grad_scores)
-            to_off = pltpu.roll(jnp.concatenate([rows_back, blank], axis=1), 0, 1, stride=1, stride_axis=0).astype(LOW)
-            from_off = pltpu.roll(jnp.concatenate([cols_back, blank], axis=1), 0, 1, stride=1, stride_axis=0).astype(LOW)
-            g_query = mm(rows_back.astype(LOW), k_pair) + mm(to_off, pk_pair)
-            g_key = mm(cols_back.astype(LOW), q_pair) + mm(from_off, pq_pair)
-            g_pk = mm_tn(to_off, qr_pair)
-            g_pq = mm_tn(from_off, kr_pair)
-            parts.append((g_value, g_query, g_key, g_pk, g_pq))
-        first, second = parts
+            scores_both.append((probs * (grad_probs - inner)).astype(LOW))
+            probs_both.append(probs_low)
+        g_value = mm_tn(jnp.concatenate(probs_both, axis=1), gctx_pair)
+        rows_both = mm(flip, jnp.concatenate(scores_both, axis=1))
+        cols_both = mm_nt(flip, jnp.concatenate(scores_both, axis=0))
+
+        def spread_out(both):
+            return [
+                pltpu.roll(
+                    jnp.concatenate([both[:, h * ROWS : (h + 1) * ROWS], blank], axis=1), 0, 1, stride=1, stride_axis=0
+                ).astype(LOW)
+                for h in range(2)
+            ]
+
+        def stacked(both):
+            return jnp.concatenate([both[:, :ROWS], both[:, ROWS:]], axis=0).astype(LOW)
+
+        to_off, from_off = spread_out(rows_both), spread_out(cols_both)
+        g_query = mm(stacked(rows_both), k_pair) + mm(jnp.concatenate(to_off, axis=0), pk_pair)
+        g_key = mm(stacked(cols_both), q_pair) + mm(jnp.concatenate(from_off, axis=0), pq_pair)
+        g_pk = mm_tn(jnp.concatenate(to_off, axis=1), qr_pair)
+        g_pq = mm_tn(jnp.concatenate(from_off, axis=1), kr_pair)
+        first = [grad[: grad.shape[0] // 2] for grad in (g_value, g_query, g_key, g_pk, g_pq)]
+        second = [grad[grad.shape[0] // 2 :] for grad in (g_value, g_query, g_key, g_pk, g_pq)]
         gv_ref[:, cols] = jnp.where(side == 0, first[0], second[0]).astype(LOW)
         gq_ref[:, cols] = (jnp.where(side == 0, first[1], second[1]) * SCALING).astype(LOW)
         gk_ref[:, cols] = (jnp.where(side == 0, first[2], second[2]) * SCALING).astype(LOW)
@@ -706,7 +722,9 @@
     )
     bucket_column = jnp.concatenate([bucket[::-1], jnp.full((1,), -1, jnp.int32)])[:, None]
     own_first = (w_query, w_key, w_value, rel_table)
-    own_halves = tuple(ref.reshape(2, ref.shape[0] // 2, D) for ref in own_first)
+    own_halves = tuple(
+        pltpu.with_memory_space_constraint(ref.reshape(2, ref.shape[0] // 2, D), pltpu.HBM) for ref in own_first
+    )
     meta, first, second, rows = pack(
         coords, lengths, hidden, grad_out, own_first, (w_outer, w_out, w_inner), norm_block
     )

time: 219 us -> 216 us (0.986)
  local copies, waits for them, and re-layouts: 7.94 us -> 4.38 us
  Pallas kernels: 60.8 us -> 58.2 us
  waiting for transfers between devices: 87.6 us -> 90 us
    unnamed x33 -> x19, local copies, waits for them, and re-layouts: 3.12 us -> 0.27 us
  transfers between devices with their start and end apart: 41 -> 41, of which waited for: 21 -> 23; matrix products, arithmetic and copies ran while one was open for 3% -> 3% of each run, Pallas kernels for 17% -> 16%
where the time goes in v2:
time: 216 us; the launch traced here: 213 us
  waiting for transfers between devices  90 us (42%)
  Pallas kernels  58.2 us (27%)
  starting transfers between devices  53 us (25%)
  other arithmetic  6.91 us (3%)
  local copies, waits for them, and re-layouts  4.38 us (2%)
    ppermute x10, waiting for transfers between devices, hop_x(): return lax.ppermute(value, ('core', 'shard'), pairs)  42.9 us
    ppermute x17, waiting for transfers between devices, hop_yz(): return lax.ppermute(value, ('y', 'z', 'core'), pairs)  36.7 us
    ppermute x17, starting transfers between devices, hop_yz(): return lax.ppermute(value, ('y', 'z', 'core'), pairs)  26.3 us
    pallas_call x1, Pallas kernels, feed(): pl.pallas_call(feed_body, out_shape=(shape((ROWS, D), LOW), shape((ROWS,...  16.6 us
    pallas_call x1, Pallas kernels, attend_back_two(): pl.pallas_call(attend_back_two_body, out_shape=(shape((GROUP, 2, PART, D)...  12.8 us
    pallas_call x1, Pallas kernels, attend_forward(): pl.pallas_call(attend_forward_body, out_shape=(*(shape((ROWS, D), LOW),)...  10.6 us
    ppermute x12, waiting for transfers between devices, swap(): return lax.ppermute(value, 'core', [(0, 1), (1, 0)])  10.5 us
    ppermute x10, starting transfers between devices, hop_x(): return lax.ppermute(value, ('core', 'shard'), pairs)  9.99 us
  transfers between devices with their start and end apart: 41, of which 23 were waited for; matrix products, arithmetic and copies ran while one was open for 3% of the time, Pallas kernels for 16%

profile of v2, /device:TPU:17, one launch (start us, length us, event | category | flops | bytes accessed | tf_op | source)
XLA Modules:
  0.0 213.5 jit_solution(4881624518332370304)
XLA Ops:
  2.7 3.5 %pack.1 = (s32[16]{0:T(128)}, bf16[352,768]{1,0:T(8,128)(2,1)}, bf16[224,768]{1,0:T(8,128)(2,1)}, bf16[4,2,64,768]{3,2,1,0:T(8,128)(2,1)}) custom-call(s32[4]{0:T(128)} %pad_add_fusion.1.coord_ref, s32[4]{0:T(128)} %length_ref.1, bf16[4,64,768]{2,1,0:T(8,128)(2,1)} %hidden_ref.1, bf16[4,64,768]{2,1,0:T(8,128)(2,1)} %grad_ref.1, bf16[192,768]{1,0:T(8,128)(2,1)} %own_q.1, ...), custom_call_target="tpu_custom_call" | custom-call | tf_op jit(solution)/shard_map/pack/pallas_call | solution.py:166
  10.4 4.2 %collective-permute-done = bf16[224,768]{1,0:T(8,128)(2,1)S(1)} collective-permute-done((bf16[224,768]{1,0:T(8,128)(2,1)}, bf16[224,768]{1,0:T(8,128)(2,1)S(1)}, u32[]{:S(2)}, u32[]{:S(2)}) %collective-permute-start) | collective-permute-done | bytes 344096 | tf_op jit(solution)/shard_map/ppermute | solution.py:682
  14.6 11.5 %collective-permute-done.3.p0 = bf16[352,768]{1,0:T(8,128)(2,1)} collective-permute-done((bf16[352,768]{1,0:T(8,128)(2,1)}, bf16[352,768]{1,0:T(8,128)(2,1)}, u32[]{:S(2)}, u32[]{:S(2)}) %collective-permute-start.3) | collective-permute-done | bytes 540704 | tf_op jit(solution)/shard_map/ppermute | solution.py:682
  26.2 3.0 %collective-permute-done.1 = bf16[224,768]{1,0:T(8,128)(2,1)S(1)} collective-permute-done((bf16[224,768]{1,0:T(8,128)(2,1)}, bf16[224,768]{1,0:T(8,128)(2,1)S(1)}, u32[]{:S(2)}, u32[]{:S(2)}) %collective-permute-start.1) | collective-permute-done | bytes 344096 | tf_op jit(solution)/shard_map/ppermute | solution.py:682
  29.3 3.7 %collective-permute-done.2 = bf16[224,768]{1,0:T(8,128)(2,1)S(1)} collective-permute-done((bf16[224,768]{1,0:T(8,128)(2,1)S(1)}, bf16[224,768]{1,0:T(8,128)(2,1)S(1)}, u32[]{:S(2)}, u32[]{:S(2)}) %collective-permute-start.2) | collective-permute-done | bytes 344096 | tf_op jit(solution)/shard_map/ppermute | solution.py:682
  33.1 3.8 %collective-permute-start.6 = (bf16[3,224,768]{2,1,0:T(8,128)(2,1)S(1)}, bf16[3,224,768]{2,1,0:T(8,128)(2,1)}, u32[]{:S(2)}, u32[]{:S(2)}) collective-permute-start(bf16[3,224,768]{2,1,0:T(8,128)(2,1)S(1)} %pad_maximum_fusion.rest_0_), channel_id=1, source_target_pairs={{0,96},{4,28},{8,104},{12,20},{16,112},{20,12},{24,120},{28,4},{32... | collective-permute-start | bytes 3096584 | tf_op jit(solution)/shard_map/ppermute | solution.py:693
  36.9 4.2 %all-to-all-start = ((bf16[4,2,64,768]{3,2,1,0:T(8,128)(2,1)}), bf16[4,2,64,768]{3,2,1,0:T(8,128)(2,1)S(1)}, u32[]{:S(2)}, u32[]{:S(2)}) async-start(bf16[4,2,64,768]{3,2,1,0:T(8,128)(2,1)} %get-tuple-element.87), calls=%async_computation | async-start | bytes 1572864 | tf_op jit(solution)/shard_map/all_to_all | solution.py:712
  42.1 7.1 %collective-permute-done.6.rest_2_ = bf16[3,224,768]{2,1,0:T(8,128)(2,1)} collective-permute-done((bf16[3,224,768]{2,1,0:T(8,128)(2,1)S(1)}, bf16[3,224,768]{2,1,0:T(8,128)(2,1)}, u32[]{:S(2)}, u32[]{:S(2)}) %collective-permute-start.6) | collective-permute-done | bytes 1032224 | tf_op jit(solution)/shard_map/ppermute | solution.py:693
  54.4 10.6 %attend_forward.1 = (bf16[256,768]{1,0:T(8,128)(2,1)S(1)}, bf16[256,768]{1,0:T(8,128)(2,1)S(1)}, bf16[256,768]{1,0:T(8,128)(2,1)S(1)}, bf16[256,768]{1,0:T(8,128...) custom-call(s32[16]{0:T(128)S(1)} %copy-done.4, ...), custom_call_target="tpu_custom_call" | custom-call | flops 12000000000 | bytes 40000000 | tf_op jit(solution)/shard_map/attend_forward/pallas_call | solution.py:294
  66.3 5.5 %attend_forward_two.1 = (bf16[6,256,256]{2,1,0:T(8,128)(2,1)S(1)}, bf16[256,384]{1,0:T(8,128)(2,1)S(1)}) custom-call(s32[16]{0:T(128)S(1)} %copy-done.4, bf16[256,768]{1,0:T(8,128)(2,1)S(1)} %get-tuple-element.92.q_ref, bf16[256,768]{1,0:T(8,128)(2,1)S(1)} %get-tuple-element.93.k_ref, bf16[256,768]{1,0:T(8,128)(2,1)S(1)} %get-tuple-element.94.v_ref, ...), custom_call_target="tpu_custom_call" | custom-call | flops 8000000000 | bytes 20000000 | tf_op jit(solution)/shard_map/attend_forward_two/pallas_call | solution.py:315
  72.5 16.6 %feed.1 = (bf16[256,768]{1,0:T(8,128)(2,1)S(1)}, bf16[256,768]{1,0:T(8,128)(2,1)S(1)}, f32[256,768]{1,0:T(8,128)S(1)}, bf16[4,4,128,768]{3,2,1,0:T(8,128)(2,1)S(...) custom-call(s32[16]{0:T(128)S(1)} %copy-done.4, ...), custom_call_target="tpu_custom_call" | custom-call | flops 16000000000 | bytes 60000000 | tf_op jit(solution)/shard_map/feed/pallas_call | solution.py:605
  89.7 4.7 %attend_back_one.1 = (bf16[256,384]{1,0:T(8,128)(2,1)S(1)}, bf16[256,384]{1,0:T(8,128)(2,1)S(1)}, bf16[256,384]{1,0:T(8,128)(2,1)S(1)}, bf16[512,384]{1,0:T(8,128)(2,1)S(1)}, bf16[512,384]{1,0:T(8,128)(2,1)S(1)}) custom-call(bf16[256,768]{1,0:T(8,128)(2,1)S(1)} %get-tuple-element.92.q_ref, bf16[256,768]{1,0:T(8,128)(2,1)S(1)} %get-tuple-element.93.k_ref, ...), custom_call_target="tpu_custom_call" | custom-call | flops 8000000000 | bytes 20000000 | tf_op jit(solution)/shard_map/attend_back_one/pallas_call | solution.py:448
  101.3 12.8 %attend_back_two.1 = (bf16[4,2,64,768]{3,2,1,0:T(8,128)(2,1)}, bf16[4,352,768]{2,1,0:T(8,128)(2,1)S(1)}, bf16[4,352,768]{2,1,0:T(8,128)(2,1)S(1)}) custom-call(s32[16]{0:T(128)S(1)} %copy-done.4, bf16[256,768]{1,0:T(8,128)(2,1)S(1)} %get-tuple-element.92.q_ref, bf16[256,768]{1,0:T(8,128)(2,1)S(1)} %get-tuple-element.93.k_ref, ...), custom_call_target="tpu_custom_call" | custom-call | flops 14000000000 | bytes 40000000 | tf_op jit(solution)/shard_map/attend_back_two/pallas_call | solution.py:463
  115.9 3.9 %collective-permute-done.22 = bf16[4,352,768]{2,1,0:T(8,128)(2,1)S(1)} collective-permute-done((bf16[4,352,768]{2,1,0:T(8,128)(2,1)S(1)}, bf16[4,352,768]{2,1,0:T(8,128)(2,1)S(1)}, u32[]{:S(2)}, u32[]{:S(2)}) %collective-permute-start.22) | collective-permute-done | bytes 2162720 | tf_op jit(solution)/shard_map/ppermute | solution.py:697
  126.0 9.0 %collective-permute-done.25 = bf16[4,96,768]{2,1,0:T(8,128)(2,1)S(1)} collective-permute-done((bf16[4,96,768]{2,1,0:T(8,128)(2,1)S(1)}, bf16[4,96,768]{2,1,0:T(8,128)(2,1)S(1)}, u32[]{:S(2)}, u32[]{:S(2)}) %collective-permute-start.25) | collective-permute-done | bytes 589856 | tf_op jit(solution)/shard_map/ppermute | solution.py:693
  139.0 14.0 %collective-permute-done.26 = bf16[352,768]{1,0:T(8,128)(2,1)S(1)} collective-permute-done((bf16[352,768]{1,0:T(8,128)(2,1)S(1)}, bf16[352,768]{1,0:T(8,128)(2,1)S(1)}, u32[]{:S(2)}, u32[]{:S(2)}) %collective-permute-start.26) | collective-permute-done | bytes 540704 | tf_op jit(solution)/shard_map/ppermute | solution.py:682
  155.4 6.3 %collective-permute-done.29 = bf16[224,768]{1,0:T(8,128)(2,1)S(1)} collective-permute-done((bf16[224,768]{1,0:T(8,128)(2,1)S(1)}, bf16[224,768]{1,0:T(8,128)(2,1)S(1)}, u32[]{:S(2)}, u32[]{:S(2)}) %collective-permute-start.29) | collective-permute-done | bytes 344096 | tf_op jit(solution)/shard_map/ppermute | solution.py:682
  165.4 5.0 %collective-permute-done.31 = bf16[224,768]{1,0:T(8,128)(2,1)S(1)} collective-permute-done((bf16[224,768]{1,0:T(8,128)(2,1)S(1)}, bf16[224,768]{1,0:T(8,128)(2,1)S(1)}, u32[]{:S(2)}, u32[]{:S(2)}) %collective-permute-start.31) | collective-permute-done | bytes 344096 | tf_op jit(solution)/shard_map/ppermute | solution.py:693
  173.5 5.0 %collective-permute-done.33 = bf16[224,768]{1,0:T(8,128)(2,1)S(1)} collective-permute-done((bf16[224,768]{1,0:T(8,128)(2,1)S(1)}, bf16[224,768]{1,0:T(8,128)(2,1)S(1)}, u32[]{:S(2)}, u32[]{:S(2)}) %collective-permute-start.33) | collective-permute-done | bytes 344096 | tf_op jit(solution)/shard_map/ppermute | solution.py:693
  182.7 3.8 %all-to-all-start.1 = ((bf16[4,2,64,768]{3,2,1,0:T(8,128)(2,1)}), bf16[4,2,64,768]{3,2,1,0:T(8,128)(2,1)S(1)}, u32[]{:S(2)}, u32[]{:S(2)}) async-start(bf16[4,2,64,768]{3,2,1,0:T(8,128)(2,1)} %get-tuple-element.146), calls=%async_computation.1 | async-start | bytes 1572864 | tf_op jit(solution)/shard_map/all_to_all | solution.py:712
  192.2 6.3 %collective-permute-done.35 = bf16[224,768]{1,0:T(8,128)(2,1)S(1)} collective-permute-done((bf16[224,768]{1,0:T(8,128)(2,1)S(1)}, bf16[224,768]{1,0:T(8,128)(2,1)S(1)}, u32[]{:S(2)}, u32[]{:S(2)}) %collective-permute-start.35) | collective-permute-done | bytes 344096 | tf_op jit(solution)/shard_map/ppermute | solution.py:693
  198.7 5.6 %collective-permute-start.38 = (bf16[1248,768]{1,0:T(8,128)(2,1)S(1)}, bf16[1248,768]{1,0:T(8,128)(2,1)S(1)}, u32[]{:S(2)}, u32[]{:S(2)}) collective-permute-start(bf16[1248,768]{1,0:T(8,128)(2,1)S(1)} %constant_dynamic-update-slice_fusion.mine), channel_id=1, source_target_pairs={{0,4},{4,0},{1,5},{5,1},{2,6},{6,2},{3,7},{7,3},{8,12},{12,8},{9,1... | collective-permute-start | bytes 5750792 | tf_op jit(solution)/shard_map/ppermute | solution.py:697
  204.3 3.5 %collective-permute-done.38.other = bf16[1248,768]{1,0:T(8,128)(2,1)S(1)} collective-permute-done((bf16[1248,768]{1,0:T(8,128)(2,1)S(1)}, bf16[1248,768]{1,0:T(8,128)(2,1)S(1)}, u32[]{:S(2)}, u32[]{:S(2)}) %collective-permute-start.38) | collective-permute-done | bytes 1916960 | tf_op jit(solution)/shard_map/ppermute | solution.py:697
  207.8 4.5 %finish.1 = (f32[192,768]{1,0:T(8,128)}, f32[192,768]{1,0:T(8,128)}, f32[192,768]{1,0:T(8,128)}, f32[128,768]{1,0:T(8,128)}, f32[768,768]{1,0:T(8,128)}, /*index...) custom-call(s32[16]{0:T(128)S(1)} %copy-done.4, ...), custom_call_target="tpu_custom_call" | custom-call | tf_op jit(solution)/shard_map/finish/pallas_call | solution.py:663
  (114 shorter events, 54.2 us)
Async XLA Ops:
  8.7 17.4 %collective-permute-start.3 = (bf16[352,768]{1,0:T(8,128)(2,1)}, bf16[352,768]{1,0:T(8,128)(2,1)}, u32[]{:S(2)}, u32[]{:S(2)}) collective-permute-start(bf16[352,768]{1,0:T(8,128)(2,1)} %get-tuple-element.89), channel_id=1, source_target_pairs={{0,1},{1,0},{2,3},{3,2},{4,7},{5,6},{6,5},{7,4},{8,9},{9,8},{10,11... | collective-permute-start | bytes 1622024 | tf_op jit(solution)/shard_map/ppermute | solution.py:682
  8.9 24.1 %collective-permute-start.4 = (bf16[352,768]{1,0:T(8,128)(2,1)}, bf16[352,768]{1,0:T(8,128)(2,1)}, u32[]{:S(2)}, u32[]{:S(2)}) collective-permute-start(bf16[352,768]{1,0:T(8,128)(2,1)} %get-tuple-element.89), channel_id=1, source_target_pairs={{0,3},{1,2},{2,1},{3,0},{4,5},{5,4},{6,7},{7,6},{8,11},{9,10},{10,... | collective-permute-start | bytes 1622024 | tf_op jit(solution)/shard_map/ppermute | solution.py:682
  8.9 20.3 %collective-permute-start.1 = (bf16[224,768]{1,0:T(8,128)(2,1)}, bf16[224,768]{1,0:T(8,128)(2,1)S(1)}, u32[]{:S(2)}, u32[]{:S(2)}) collective-permute-start(bf16[224,768]{1,0:T(8,128)(2,1)} %get-tuple-element.88), channel_id=1, source_target_pairs={{0,3},{1,2},{2,1},{3,0},{4,5},{5,4},{6,7},{7,6},{8,11},{9,10},{10,... | collective-permute-start | bytes 1032200 | tf_op jit(solution)/shard_map/ppermute | solution.py:682
  14.6 18.3 %collective-permute-start.2 = (bf16[224,768]{1,0:T(8,128)(2,1)S(1)}, bf16[224,768]{1,0:T(8,128)(2,1)S(1)}, u32[]{:S(2)}, u32[]{:S(2)}) collective-permute-start(bf16[224,768]{1,0:T(8,128)(2,1)S(1)} %collective-permute-done), channel_id=1, source_target_pairs={{0,3},{1,2},{2,1},{3,0},{4,5},{5,4},{6,7},{7,6},{8,11},{9,10},{10,... | collective-permute-start | bytes 1032200 | tf_op jit(solution)/shard_map/ppermute | solution.py:682
  26.1 15.6 %collective-permute-start.7 = (bf16[352,768]{1,0:T(8,128)(2,1)}, bf16[352,768]{1,0:T(8,128)(2,1)}, u32[]{:S(2)}, u32[]{:S(2)}) collective-permute-start(bf16[352,768]{1,0:T(8,128)(2,1)} %collective-permute-done.3.p0), channel_id=1, source_target_pairs={{0,3},{1,2},{2,1},{3,0},{4,5},{5,4},{6,7},{7,6},{8,11},{9,10},{10,... | collective-permute-start | bytes 1622024 | tf_op jit(solution)/shard_map/ppermute | solution.py:682
  33.1 16.1 %collective-permute-start.6 = (bf16[3,224,768]{2,1,0:T(8,128)(2,1)S(1)}, bf16[3,224,768]{2,1,0:T(8,128)(2,1)}, u32[]{:S(2)}, u32[]{:S(2)}) collective-permute-start(bf16[3,224,768]{2,1,0:T(8,128)(2,1)S(1)} %pad_maximum_fusion.rest_0_), channel_id=1, source_target_pairs={{0,96},{4,28},{8,104},{12,20},{16,112},{20,12},{24,120},{28,4},{32... | collective-permute-start | bytes 3096584 | tf_op jit(solution)/shard_map/ppermute | solution.py:693
  36.9 14.1 %collective-permute-start.5 = (bf16[3,224,768]{2,1,0:T(8,128)(2,1)S(1)}, bf16[3,224,768]{2,1,0:T(8,128)(2,1)S(1)}, u32[]{:S(2)}, u32[]{:S(2)}) collective-permute-start(bf16[3,224,768]{2,1,0:T(8,128)(2,1)S(1)} %pad_maximum_fusion.rest_0_), channel_id=1, source_target_pairs={{0,32},{4,12},{8,40},{12,4},{16,48},{20,28},{24,56},{28,20},{32,0}... | collective-permute-start | bytes 3096584 | tf_op jit(solution)/shard_map/ppermute | solution.py:693
  36.9 17.5 %all-to-all-start = ((bf16[4,2,64,768]{3,2,1,0:T(8,128)(2,1)}), bf16[4,2,64,768]{3,2,1,0:T(8,128)(2,1)S(1)}, u32[]{:S(2)}, u32[]{:S(2)}) async-start(bf16[4,2,64,768]{3,2,1,0:T(8,128)(2,1)} %get-tuple-element.87), calls=%async_computation | async-start | bytes 1572864 | tf_op jit(solution)/shard_map/all_to_all | solution.py:712
  41.2 13.2 %collective-permute-start.9 = (bf16[352,768]{1,0:T(8,128)(2,1)}, bf16[352,768]{1,0:T(8,128)(2,1)}, u32[]{:S(2)}, u32[]{:S(2)}) collective-permute-start(bf16[352,768]{1,0:T(8,128)(2,1)} %collective-permute-done.4.p1), channel_id=1, source_target_pairs={{0,4},{4,0},{1,5},{5,1},{2,6},{6,2},{3,7},{7,3},{8,12},{12,8},{9,1... | collective-permute-start | bytes 1622024 | tf_op jit(solution)/shard_map/ppermute | solution.py:697
  41.2 13.2 %collective-permute-start.8 = (bf16[352,768]{1,0:T(8,128)(2,1)}, bf16[352,768]{1,0:T(8,128)(2,1)}, u32[]{:S(2)}, u32[]{:S(2)}) collective-permute-start(bf16[352,768]{1,0:T(8,128)(2,1)} %collective-permute-done.3.p0), channel_id=1, source_target_pairs={{0,4},{4,0},{1,5},{5,1},{2,6},{6,2},{3,7},{7,3},{8,12},{12,8},{9,1... | collective-permute-start | bytes 1622024 | tf_op jit(solution)/shard_map/ppermute | solution.py:697
  41.7 12.7 %collective-permute-start.10 = (bf16[352,768]{1,0:T(8,128)(2,1)}, bf16[352,768]{1,0:T(8,128)(2,1)}, u32[]{:S(2)}, u32[]{:S(2)}) collective-permute-start(bf16[352,768]{1,0:T(8,128)(2,1)} %collective-permute-done.7.p2), channel_id=1, source_target_pairs={{0,4},{4,0},{1,5},{5,1},{2,6},{6,2},{3,7},{7,3},{8,12},{12,8},{9,1... | collective-permute-start | bytes 1622024 | tf_op jit(solution)/shard_map/ppermute | solution.py:697
  51.0 14.0 %collective-permute-start.12 = (bf16[3,96,768]{2,1,0:T(8,128)(2,1)}, bf16[3,96,768]{2,1,0:T(8,128)(2,1)}, u32[]{:S(2)}, u32[]{:S(2)}) collective-permute-start(bf16[3,96,768]{2,1,0:T(8,128)(2,1)} %slice.158), channel_id=1, source_target_pairs={{0,32},{4,12},{8,40},{12,4},{16,48},{20,28},{24,56},{28,20},{32,0}... | collective-permute-start | bytes 1327112 | tf_op jit(solution)/shard_map/ppermute | solution.py:693
  51.9 13.2 %collective-permute-start.11 = (bf16[3,128,768]{2,1,0:T(8,128)(2,1)}, bf16[3,128,768]{2,1,0:T(8,128)(2,1)}, u32[]{:S(2)}, u32[]{:S(2)}) collective-permute-start(bf16[3,128,768]{2,1,0:T(8,128)(2,1)} %slice.157), channel_id=1, source_target_pairs={{0,96},{4,28},{8,104},{12,20},{16,112},{20,12},{24,120},{28,4},{32... | collective-permute-start | bytes 1769480 | tf_op jit(solution)/shard_map/ppermute | solution.py:693
  95.2 19.8 %collective-permute-start.20 = (bf16[2,4,128,768]{3,2,1,0:T(8,128)(2,1)S(1)}, bf16[2,4,128,768]{3,2,1,0:T(8,128)(2,1)S(1)}, u32[]{:S(2)}, u32[]{:S(2)}) collective-permute-start(bf16[2,4,128,768]{3,2,1,0:T(8,128)(2,1)S(1)} %add_convert_fusion), channel_id=1, source_target_pairs={{0,32},{4,12},{8,40},{12,4},{16,48},{20,28},{24,56},{28,20},{32,0}... | collective-permute-start | bytes 4718600 | tf_op jit(solution)/shard_map/ppermute | solution.py:693
  98.5 16.6 %collective-permute-start.21 = (bf16[2,4,96,768]{3,2,1,0:T(8,128)(2,1)S(1)}, bf16[2,4,96,768]{3,2,1,0:T(8,128)(2,1)S(1)}, u32[]{:S(2)}, u32[]{:S(2)}) collective-permute-start(bf16[2,4,96,768]{3,2,1,0:T(8,128)(2,1)S(1)} %add_convert_fusion.1), channel_id=1, source_target_pairs={{0,96},{4,28},{8,104},{12,20},{16,112},{20,12},{24,120},{28,4},{32... | collective-permute-start | bytes 3538952 | tf_op jit(solution)/shard_map/ppermute | solution.py:693
  120.0 15.3 %collective-permute-start.23 = (bf16[2,352,768]{2,1,0:T(8,128)(2,1)S(1)}, bf16[2,352,768]{2,1,0:T(8,128)(2,1)S(1)}, u32[]{:S(2)}, u32[]{:S(2)}) collective-permute-start(bf16[2,352,768]{2,1,0:T(8,128)(2,1)S(1)} %add_convert_fusion.2), channel_id=1, source_target_pairs={{0,1},{1,0},{2,3},{3,2},{4,7},{5,6},{6,5},{7,4},{8,9},{9,8},{10,11... | collective-permute-start | bytes 3244040 | tf_op jit(solution)/shard_map/ppermute | solution.py:682
  123.1 12.1 %collective-permute-start.24 = (bf16[4,128,768]{2,1,0:T(8,128)(2,1)S(1)}, bf16[4,128,768]{2,1,0:T(8,128)(2,1)S(1)}, u32[]{:S(2)}, u32[]{:S(2)}) collective-permute-start(bf16[4,128,768]{2,1,0:T(8,128)(2,1)S(1)} %fusion.3), channel_id=1, source_target_pairs={{0,96},{4,28},{8,104},{12,20},{16,112},{20,12},{24,120},{28,4},{32... | collective-permute-start | bytes 2359304 | tf_op jit(solution)/shard_map/ppermute | solution.py:693
  136.3 16.7 %collective-permute-start.27 = (bf16[2,224,768]{2,1,0:T(8,128)(2,1)S(1)}, bf16[2,224,768]{2,1,0:T(8,128)(2,1)S(1)}, u32[]{:S(2)}, u32[]{:S(2)}) collective-permute-start(bf16[2,224,768]{2,1,0:T(8,128)(2,1)S(1)} %fusion.4), channel_id=1, source_target_pairs={{0,1},{1,0},{2,3},{3,2},{4,7},{5,6},{6,5},{7,4},{8,9},{9,8},{10,11... | collective-permute-start | bytes 2064392 | tf_op jit(solution)/shard_map/ppermute | solution.py:682
  139.0 14.0 %collective-permute-start.26 = (bf16[352,768]{1,0:T(8,128)(2,1)S(1)}, bf16[352,768]{1,0:T(8,128)(2,1)S(1)}, u32[]{:S(2)}, u32[]{:S(2)}) collective-permute-start(bf16[352,768]{1,0:T(8,128)(2,1)S(1)} %fusion.7), channel_id=1, source_target_pairs={{0,3},{1,2},{2,1},{3,0},{4,5},{5,4},{6,7},{7,6},{8,11},{9,10},{10,... | collective-permute-start | bytes 1622024 | tf_op jit(solution)/shard_map/ppermute | solution.py:682
  179.8 11.1 %collective-permute-start.34 = (bf16[352,768]{1,0:T(8,128)(2,1)S(1)}, bf16[352,768]{1,0:T(8,128)(2,1)}, u32[]{:S(2)}, u32[]{:S(2)}) collective-permute-start(bf16[352,768]{1,0:T(8,128)(2,1)S(1)} %add_convert_fusion.6), channel_id=1, source_target_pairs={{0,96},{4,28},{8,104},{12,20},{16,112},{20,12},{24,120},{28,4},{32... | collective-permute-start | bytes 1622024 | tf_op jit(solution)/shard_map/ppermute | solution.py:693
  182.7 16.0 %all-to-all-start.1 = ((bf16[4,2,64,768]{3,2,1,0:T(8,128)(2,1)}), bf16[4,2,64,768]{3,2,1,0:T(8,128)(2,1)S(1)}, u32[]{:S(2)}, u32[]{:S(2)}) async-start(bf16[4,2,64,768]{3,2,1,0:T(8,128)(2,1)} %get-tuple-element.146), calls=%async_computation.1 | async-start | bytes 1572864 | tf_op jit(solution)/shard_map/all_to_all | solution.py:712
  186.5 12.1 %collective-permute-start.37 = (bf16[224,768]{1,0:T(8,128)(2,1)S(1)}, bf16[224,768]{1,0:T(8,128)(2,1)S(1)}, u32[]{:S(2)}, u32[]{:S(2)}) collective-permute-start(bf16[224,768]{1,0:T(8,128)(2,1)S(1)} %add_convert_fusion.10), channel_id=1, source_target_pairs={{0,96},{4,28},{8,104},{12,20},{16,112},{20,12},{24,120},{28,4},{32... | collective-permute-start | bytes 1032200 | tf_op jit(solution)/shard_map/ppermute | solution.py:693
  186.7 11.8 %collective-permute-start.36 = (bf16[224,768]{1,0:T(8,128)(2,1)S(1)}, bf16[224,768]{1,0:T(8,128)(2,1)S(1)}, u32[]{:S(2)}, u32[]{:S(2)}) collective-permute-start(bf16[224,768]{1,0:T(8,128)(2,1)S(1)} %add_convert_fusion.10), channel_id=1, source_target_pairs={{0,64},{4,20},{8,72},{12,28},{16,80},{20,4},{24,88},{28,12},{32,96... | collective-permute-start | bytes 1032200 | tf_op jit(solution)/shard_map/ppermute | solution.py:693
  187.9 10.6 %collective-permute-start.35 = (bf16[224,768]{1,0:T(8,128)(2,1)S(1)}, bf16[224,768]{1,0:T(8,128)(2,1)S(1)}, u32[]{:S(2)}, u32[]{:S(2)}) collective-permute-start(bf16[224,768]{1,0:T(8,128)(2,1)S(1)} %add_convert_fusion.10), channel_id=1, source_target_pairs={{0,32},{4,12},{8,40},{12,4},{16,48},{20,28},{24,56},{28,20},{32,0}... | collective-permute-start | bytes 1032200 | tf_op jit(solution)/shard_map/ppermute | solution.py:693
  (24 other events, 186.3 us)

commit v3 on v2

--- a/solution.py
+++ b/solution.py
@@ -622,7 +622,8 @@
 
 def finish_body(
     meta_ref, mine, other, rows_ref,
-    q_ref, k_ref, v_ref, rel_ref, outer_ref, wout_ref, inner_ref, extra_ref, out_ref, gtok_ref,
+    q_ref, k_ref, v_ref, rel_ref, outer_ref, wout_ref, inner_ref, g1_ref, b1_ref, g2_ref, b2_ref, rms_ref,
+    out_ref, gtok_ref, extra_ref,
 ):
     for piece, side in ((mine, 0), (other, 1)):
         core = meta_ref[CORE] if side == 0 else 1 - meta_ref[CORE]
@@ -651,6 +652,11 @@
             return carry
 
         lax.fori_loop(0, GROUP, piece_step, 0)
+    norms = extra_ref[0, 0:1, :]
+    for i, ref in enumerate((g1_ref, b1_ref, g2_ref, b2_ref)):
+        ref[...] = norms[:, i * PIECE : (i + 1) * PIECE]
+    stats = extra_ref[1, 0:1, :] + extra_ref[1, 1:2, :]
+    rms_ref[...] = jnp.sqrt(stats[:, :GROUP] * (1.0 / (TOKENS * D)))
     for k in range(GROUP):
         member = meta_ref[X] ^ k
         out_ref[meta_ref[SEQ + k]] = rows_ref[member, 0]
@@ -664,11 +670,13 @@
         finish_body,
         out_shape=(
             *(shape((PIECE, D), F32),) * 3, shape((OFFS // GROUP, D), F32),
-            shape((D, D), F32), shape((PIECE, D), F32), shape((PIECE, WIDE), F32), shape((2, QUARTER - HALF, D), F32),
+            shape((D, D), F32), shape((PIECE, D), F32), shape((PIECE, WIDE), F32),
+            *(shape((1, PIECE), F32),) * 4, shape((1, GROUP), F32),
             *(shape((GROUP, PART, D), LOW),) * 2,
         ),
         in_specs=[pl.BlockSpec(memory_space=pltpu.SMEM)] + [full] * 3,
-        out_specs=(full,) * 10,
+        out_specs=(full,) * 14,
+        scratch_shapes=[pltpu.VMEM((2, QUARTER - HALF, D), F32)],
         compiler_params=pltpu.CompilerParams(vmem_limit_bytes=24 * MIB),
         name="finish",
     )(meta, mine, other, rows)
@@ -774,7 +782,6 @@
     both = jnp.concatenate([mine, mine_in], axis=1)
     came_x = hop_x(both[:2], NEAR)
     home = exchange_rows(leaving)
-    last_one = after(last_one, came_x)
     mine_one = add(keep_one[3], other_one[3], came_one[1], last_one)
     come_one = hop_yz(mine_one, 1, swapped=True)
     last_x = hop_x(after(add(both[2], came_x[0]), mine_one), FAR)
@@ -793,15 +800,12 @@
     both[1], both[2], both[3] = both[1], both[3], both[2]
     mine_one = add(mine_one, come_one)
     packed = after(jnp.concatenate([mine_one, *both], axis=0), home)
-    q_grad, k_grad, v_grad, rel_grad, outer_grad, out_grad, inner_grad, extra, layer_output, grad_hidden = finish(
+    q_grad, k_grad, v_grad, rel_grad, outer_grad, out_grad, inner_grad, *small, layer_output, grad_hidden = finish(
         meta, packed, swap(packed), home
     )
-    norm_sums = extra[0, 0].reshape(GROUP, PIECE)
-    stats = extra[1, 0, :GROUP] + extra[1, 1, :GROUP]
     return (
         layer_output, grad_hidden, q_grad, k_grad, v_grad, out_grad, inner_grad, outer_grad, rel_grad,
-        norm_sums[0], norm_sums[1], norm_sums[2], norm_sums[3],
-        jnp.sqrt(stats / (TOKENS * D)),
+        *(row[0] for row in small),
     )
 
 

time: 216 us -> 215 us (level)
    ppermute x10, waiting for transfers between devices: 42.9 us -> 40.5 us  [hop_x(): return lax.ppermute(value, ('core', 'shard'), pairs)]
  transfers between devices with their start and end apart: 41 -> 41, of which waited for: 23 -> 24; matrix products, arithmetic and copies ran while one was open for 3% -> 3% of each run, Pallas kernels for 16% -> 16%
where the time goes in v3:
time: 215 us; the launch traced here: 212 us
  waiting for transfers between devices  88.8 us (41%)
  Pallas kernels  58.2 us (27%)
  starting transfers between devices  53.7 us (25%)
  other arithmetic  6.41 us (3%)
  local copies, waits for them, and re-layouts  3.74 us (2%)
    ppermute x10, waiting for transfers between devices, hop_x(): return lax.ppermute(value, ('core', 'shard'), pairs)  40.5 us
    ppermute x17, waiting for transfers between devices, hop_yz(): return lax.ppermute(value, ('y', 'z', 'core'), pairs)  37.7 us
    ppermute x17, starting transfers between devices, hop_yz(): return lax.ppermute(value, ('y', 'z', 'core'), pairs)  25.4 us
    pallas_call x1, Pallas kernels, feed(): pl.pallas_call(feed_body, out_shape=(shape((ROWS, D), LOW), shape((ROWS,...  16.6 us
    pallas_call x1, Pallas kernels, attend_back_two(): pl.pallas_call(attend_back_two_body, out_shape=(shape((GROUP, 2, PART, D)...  12.8 us
    pallas_call x1, Pallas kernels, attend_forward(): pl.pallas_call(attend_forward_body, out_shape=(*(shape((ROWS, D), LOW),)...  10.6 us
    ppermute x12, waiting for transfers between devices, swap(): return lax.ppermute(value, 'core', [(0, 1), (1, 0)])  10.5 us
    ppermute x12, starting transfers between devices, swap(): return lax.ppermute(value, 'core', [(0, 1), (1, 0)])  10.2 us
  transfers between devices with their start and end apart: 41, of which 24 were waited for; matrix products, arithmetic and copies ran while one was open for 3% of the time, Pallas kernels for 16%

profile of v3, /device:TPU:17, one launch (start us, length us, event | category | flops | bytes accessed | tf_op | source)
XLA Modules:
  0.0 211.9 jit_solution(13116881381631136093)
XLA Ops:
  2.7 3.5 %pack.1 = (s32[16]{0:T(128)}, bf16[352,768]{1,0:T(8,128)(2,1)}, bf16[224,768]{1,0:T(8,128)(2,1)}, bf16[4,2,64,768]{3,2,1,0:T(8,128)(2,1)}) custom-call(s32[4]{0:T(128)} %pad_add_fusion.1.coord_ref, s32[4]{0:T(128)} %length_ref.1, bf16[4,64,768]{2,1,0:T(8,128)(2,1)} %hidden_ref.1, bf16[4,64,768]{2,1,0:T(8,128)(2,1)} %grad_ref.1, bf16[192,768]{1,0:T(8,128)(2,1)} %own_q.1, ...), custom_call_target="tpu_custom_call" | custom-call | tf_op jit(solution)/shard_map/pack/pallas_call | solution.py:166
  10.4 4.2 %collective-permute-done = bf16[224,768]{1,0:T(8,128)(2,1)S(1)} collective-permute-done((bf16[224,768]{1,0:T(8,128)(2,1)}, bf16[224,768]{1,0:T(8,128)(2,1)S(1)}, u32[]{:S(2)}, u32[]{:S(2)}) %collective-permute-start) | collective-permute-done | bytes 344096 | tf_op jit(solution)/shard_map/ppermute | solution.py:690
  14.6 11.5 %collective-permute-done.3.p0 = bf16[352,768]{1,0:T(8,128)(2,1)} collective-permute-done((bf16[352,768]{1,0:T(8,128)(2,1)}, bf16[352,768]{1,0:T(8,128)(2,1)}, u32[]{:S(2)}, u32[]{:S(2)}) %collective-permute-start.3) | collective-permute-done | bytes 540704 | tf_op jit(solution)/shard_map/ppermute | solution.py:690
  29.3 3.7 %collective-permute-done.2 = bf16[224,768]{1,0:T(8,128)(2,1)S(1)} collective-permute-done((bf16[224,768]{1,0:T(8,128)(2,1)S(1)}, bf16[224,768]{1,0:T(8,128)(2,1)S(1)}, u32[]{:S(2)}, u32[]{:S(2)}) %collective-permute-start.2) | collective-permute-done | bytes 344096 | tf_op jit(solution)/shard_map/ppermute | solution.py:690
  33.1 3.8 %collective-permute-start.6 = (bf16[3,224,768]{2,1,0:T(8,128)(2,1)S(1)}, bf16[3,224,768]{2,1,0:T(8,128)(2,1)}, u32[]{:S(2)}, u32[]{:S(2)}) collective-permute-start(bf16[3,224,768]{2,1,0:T(8,128)(2,1)S(1)} %pad_maximum_fusion.rest_0_), channel_id=1, source_target_pairs={{0,96},{4,28},{8,104},{12,20},{16,112},{20,12},{24,120},{28,4},{32... | collective-permute-start | bytes 3096584 | tf_op jit(solution)/shard_map/ppermute | solution.py:701
  36.9 4.2 %all-to-all-start = ((bf16[4,2,64,768]{3,2,1,0:T(8,128)(2,1)}), bf16[4,2,64,768]{3,2,1,0:T(8,128)(2,1)S(1)}, u32[]{:S(2)}, u32[]{:S(2)}) async-start(bf16[4,2,64,768]{3,2,1,0:T(8,128)(2,1)} %get-tuple-element.90), calls=%async_computation | async-start | bytes 1572864 | tf_op jit(solution)/shard_map/all_to_all | solution.py:720
  42.1 7.1 %collective-permute-done.6.rest_2_ = bf16[3,224,768]{2,1,0:T(8,128)(2,1)} collective-permute-done((bf16[3,224,768]{2,1,0:T(8,128)(2,1)S(1)}, bf16[3,224,768]{2,1,0:T(8,128)(2,1)}, u32[]{:S(2)}, u32[]{:S(2)}) %collective-permute-start.6) | collective-permute-done | bytes 1032224 | tf_op jit(solution)/shard_map/ppermute | solution.py:701
  54.4 10.6 %attend_forward.1 = (bf16[256,768]{1,0:T(8,128)(2,1)S(1)}, bf16[256,768]{1,0:T(8,128)(2,1)S(1)}, bf16[256,768]{1,0:T(8,128)(2,1)S(1)}, bf16[256,768]{1,0:T(8,128...) custom-call(s32[16]{0:T(128)S(1)} %copy-done.4, ...), custom_call_target="tpu_custom_call" | custom-call | flops 12000000000 | bytes 40000000 | tf_op jit(solution)/shard_map/attend_forward/pallas_call | solution.py:294
  66.3 5.5 %attend_forward_two.1 = (bf16[6,256,256]{2,1,0:T(8,128)(2,1)S(1)}, bf16[256,384]{1,0:T(8,128)(2,1)S(1)}) custom-call(s32[16]{0:T(128)S(1)} %copy-done.4, bf16[256,768]{1,0:T(8,128)(2,1)S(1)} %get-tuple-element.95.q_ref, bf16[256,768]{1,0:T(8,128)(2,1)S(1)} %get-tuple-element.96.k_ref, bf16[256,768]{1,0:T(8,128)(2,1)S(1)} %get-tuple-element.97.v_ref, ...), custom_call_target="tpu_custom_call" | custom-call | flops 8000000000 | bytes 20000000 | tf_op jit(solution)/shard_map/attend_forward_two/pallas_call | solution.py:315
  72.5 16.6 %feed.1 = (bf16[256,768]{1,0:T(8,128)(2,1)S(1)}, bf16[256,768]{1,0:T(8,128)(2,1)S(1)}, f32[256,768]{1,0:T(8,128)S(1)}, bf16[4,4,128,768]{3,2,1,0:T(8,128)(2,1)S(...) custom-call(s32[16]{0:T(128)S(1)} %copy-done.4, ...), custom_call_target="tpu_custom_call" | custom-call | flops 16000000000 | bytes 60000000 | tf_op jit(solution)/shard_map/feed/pallas_call | solution.py:605
  89.7 4.7 %attend_back_one.1 = (bf16[256,384]{1,0:T(8,128)(2,1)S(1)}, bf16[256,384]{1,0:T(8,128)(2,1)S(1)}, bf16[256,384]{1,0:T(8,128)(2,1)S(1)}, bf16[512,384]{1,0:T(8,128)(2,1)S(1)}, bf16[512,384]{1,0:T(8,128)(2,1)S(1)}) custom-call(bf16[256,768]{1,0:T(8,128)(2,1)S(1)} %get-tuple-element.95.q_ref, bf16[256,768]{1,0:T(8,128)(2,1)S(1)} %get-tuple-element.96.k_ref, ...), custom_call_target="tpu_custom_call" | custom-call | flops 8000000000 | bytes 20000000 | tf_op jit(solution)/shard_map/attend_back_one/pallas_call | solution.py:448
  101.3 12.8 %attend_back_two.1 = (bf16[4,2,64,768]{3,2,1,0:T(8,128)(2,1)}, bf16[4,352,768]{2,1,0:T(8,128)(2,1)S(1)}, bf16[4,352,768]{2,1,0:T(8,128)(2,1)S(1)}) custom-call(s32[16]{0:T(128)S(1)} %copy-done.4, bf16[256,768]{1,0:T(8,128)(2,1)S(1)} %get-tuple-element.95.q_ref, bf16[256,768]{1,0:T(8,128)(2,1)S(1)} %get-tuple-element.96.k_ref, ...), custom_call_target="tpu_custom_call" | custom-call | flops 14000000000 | bytes 40000000 | tf_op jit(solution)/shard_map/attend_back_two/pallas_call | solution.py:463
  115.9 3.9 %collective-permute-done.22 = bf16[4,352,768]{2,1,0:T(8,128)(2,1)S(1)} collective-permute-done((bf16[4,352,768]{2,1,0:T(8,128)(2,1)S(1)}, bf16[4,352,768]{2,1,0:T(8,128)(2,1)S(1)}, u32[]{:S(2)}, u32[]{:S(2)}) %collective-permute-start.22) | collective-permute-done | bytes 2162720 | tf_op jit(solution)/shard_map/ppermute | solution.py:705
  126.0 9.0 %collective-permute-done.25 = bf16[4,96,768]{2,1,0:T(8,128)(2,1)S(1)} collective-permute-done((bf16[4,96,768]{2,1,0:T(8,128)(2,1)S(1)}, bf16[4,96,768]{2,1,0:T(8,128)(2,1)S(1)}, u32[]{:S(2)}, u32[]{:S(2)}) %collective-permute-start.25) | collective-permute-done | bytes 589856 | tf_op jit(solution)/shard_map/ppermute | solution.py:701
  139.1 6.2 %collective-permute-done.26 = bf16[352,768]{1,0:T(8,128)(2,1)S(1)} collective-permute-done((bf16[352,768]{1,0:T(8,128)(2,1)S(1)}, bf16[352,768]{1,0:T(8,128)(2,1)S(1)}, u32[]{:S(2)}, u32[]{:S(2)}) %collective-permute-start.26) | collective-permute-done | bytes 540704 | tf_op jit(solution)/shard_map/ppermute | solution.py:690
  147.6 5.6 %collective-permute-done.28 = bf16[2,224,768]{2,1,0:T(8,128)(2,1)S(1)} collective-permute-done((bf16[2,224,768]{2,1,0:T(8,128)(2,1)S(1)}, bf16[2,224,768]{2,1,0:T(8,128)(2,1)S(1)}, u32[]{:S(2)}, u32[]{:S(2)}) %collective-permute-start.28) | collective-permute-done | bytes 688160 | tf_op jit(solution)/shard_map/ppermute | solution.py:690
  153.5 6.3 %collective-permute-done.29 = bf16[224,768]{1,0:T(8,128)(2,1)S(1)} collective-permute-done((bf16[224,768]{1,0:T(8,128)(2,1)S(1)}, bf16[224,768]{1,0:T(8,128)(2,1)S(1)}, u32[]{:S(2)}, u32[]{:S(2)}) %collective-permute-start.29) | collective-permute-done | bytes 344096 | tf_op jit(solution)/shard_map/ppermute | solution.py:690
  162.4 5.1 %collective-permute-done.31 = bf16[224,768]{1,0:T(8,128)(2,1)S(1)} collective-permute-done((bf16[224,768]{1,0:T(8,128)(2,1)S(1)}, bf16[224,768]{1,0:T(8,128)(2,1)S(1)}, u32[]{:S(2)}, u32[]{:S(2)}) %collective-permute-start.31) | collective-permute-done | bytes 344096 | tf_op jit(solution)/shard_map/ppermute | solution.py:701
  171.2 4.6 %collective-permute-done.33 = bf16[224,768]{1,0:T(8,128)(2,1)S(1)} collective-permute-done((bf16[224,768]{1,0:T(8,128)(2,1)S(1)}, bf16[224,768]{1,0:T(8,128)(2,1)S(1)}, u32[]{:S(2)}, u32[]{:S(2)}) %collective-permute-start.33) | collective-permute-done | bytes 344096 | tf_op jit(solution)/shard_map/ppermute | solution.py:701
  180.4 3.8 %all-to-all-start.1 = ((bf16[4,2,64,768]{3,2,1,0:T(8,128)(2,1)}), bf16[4,2,64,768]{3,2,1,0:T(8,128)(2,1)S(1)}, u32[]{:S(2)}, u32[]{:S(2)}) async-start(bf16[4,2,64,768]{3,2,1,0:T(8,128)(2,1)} %get-tuple-element.148), calls=%async_computation.1 | async-start | bytes 1572864 | tf_op jit(solution)/shard_map/all_to_all | solution.py:720
  187.6 5.2 %collective-permute-done.34 = bf16[352,768]{1,0:T(8,128)(2,1)} collective-permute-done((bf16[352,768]{1,0:T(8,128)(2,1)S(1)}, bf16[352,768]{1,0:T(8,128)(2,1)}, u32[]{:S(2)}, u32[]{:S(2)}) %collective-permute-start.34) | collective-permute-done | bytes 540704 | tf_op jit(solution)/shard_map/ppermute | solution.py:701
  196.7 7.1 %collective-permute-start.38 = (bf16[1248,768]{1,0:T(8,128)(2,1)S(1)}, bf16[1248,768]{1,0:T(8,128)(2,1)S(1)}, u32[]{:S(2)}, u32[]{:S(2)}) collective-permute-start(bf16[1248,768]{1,0:T(8,128)(2,1)S(1)} %constant_dynamic-update-slice_fusion.mine), channel_id=1, source_target_pairs={{0,4},{4,0},{1,5},{5,1},{2,6},{6,2},{3,7},{7,3},{8,12},{12,8},{9,1... | collective-permute-start | bytes 5750792 | tf_op jit(solution)/shard_map/ppermute | solution.py:705
  203.8 3.5 %collective-permute-done.38.other = bf16[1248,768]{1,0:T(8,128)(2,1)S(1)} collective-permute-done((bf16[1248,768]{1,0:T(8,128)(2,1)S(1)}, bf16[1248,768]{1,0:T(8,128)(2,1)S(1)}, u32[]{:S(2)}, u32[]{:S(2)}) %collective-permute-start.38) | collective-permute-done | bytes 1916960 | tf_op jit(solution)/shard_map/ppermute | solution.py:705
  207.4 4.5 %finish.1 = (f32[192,768]{1,0:T(8,128)}, f32[192,768]{1,0:T(8,128)}, f32[192,768]{1,0:T(8,128)}, f32[128,768]{1,0:T(8,128)}, f32[768,768]{1,0:T(8,128)}, /*index...) custom-call(s32[16]{0:T(128)S(1)} %copy-done.4, ...), custom_call_target="tpu_custom_call" | custom-call | tf_op jit(solution)/shard_map/finish/pallas_call | solution.py:669
  (112 shorter events, 57.8 us)
Async XLA Ops:
  8.7 17.4 %collective-permute-start.3 = (bf16[352,768]{1,0:T(8,128)(2,1)}, bf16[352,768]{1,0:T(8,128)(2,1)}, u32[]{:S(2)}, u32[]{:S(2)}) collective-permute-start(bf16[352,768]{1,0:T(8,128)(2,1)} %get-tuple-element.92), channel_id=1, source_target_pairs={{0,1},{1,0},{2,3},{3,2},{4,7},{5,6},{6,5},{7,4},{8,9},{9,8},{10,11... | collective-permute-start | bytes 1622024 | tf_op jit(solution)/shard_map/ppermute | solution.py:690
  8.9 24.1 %collective-permute-start.4 = (bf16[352,768]{1,0:T(8,128)(2,1)}, bf16[352,768]{1,0:T(8,128)(2,1)}, u32[]{:S(2)}, u32[]{:S(2)}) collective-permute-start(bf16[352,768]{1,0:T(8,128)(2,1)} %get-tuple-element.92), channel_id=1, source_target_pairs={{0,3},{1,2},{2,1},{3,0},{4,5},{5,4},{6,7},{7,6},{8,11},{9,10},{10,... | collective-permute-start | bytes 1622024 | tf_op jit(solution)/shard_map/ppermute | solution.py:690
  8.9 20.3 %collective-permute-start.1 = (bf16[224,768]{1,0:T(8,128)(2,1)}, bf16[224,768]{1,0:T(8,128)(2,1)S(1)}, u32[]{:S(2)}, u32[]{:S(2)}) collective-permute-start(bf16[224,768]{1,0:T(8,128)(2,1)} %get-tuple-element.91), channel_id=1, source_target_pairs={{0,3},{1,2},{2,1},{3,0},{4,5},{5,4},{6,7},{7,6},{8,11},{9,10},{10,... | collective-permute-start | bytes 1032200 | tf_op jit(solution)/shard_map/ppermute | solution.py:690
  14.6 18.3 %collective-permute-start.2 = (bf16[224,768]{1,0:T(8,128)(2,1)S(1)}, bf16[224,768]{1,0:T(8,128)(2,1)S(1)}, u32[]{:S(2)}, u32[]{:S(2)}) collective-permute-start(bf16[224,768]{1,0:T(8,128)(2,1)S(1)} %collective-permute-done), channel_id=1, source_target_pairs={{0,3},{1,2},{2,1},{3,0},{4,5},{5,4},{6,7},{7,6},{8,11},{9,10},{10,... | collective-permute-start | bytes 1032200 | tf_op jit(solution)/shard_map/ppermute | solution.py:690
  26.1 15.6 %collective-permute-start.7 = (bf16[352,768]{1,0:T(8,128)(2,1)}, bf16[352,768]{1,0:T(8,128)(2,1)}, u32[]{:S(2)}, u32[]{:S(2)}) collective-permute-start(bf16[352,768]{1,0:T(8,128)(2,1)} %collective-permute-done.3.p0), channel_id=1, source_target_pairs={{0,3},{1,2},{2,1},{3,0},{4,5},{5,4},{6,7},{7,6},{8,11},{9,10},{10,... | collective-permute-start | bytes 1622024 | tf_op jit(solution)/shard_map/ppermute | solution.py:690
  33.1 16.1 %collective-permute-start.6 = (bf16[3,224,768]{2,1,0:T(8,128)(2,1)S(1)}, bf16[3,224,768]{2,1,0:T(8,128)(2,1)}, u32[]{:S(2)}, u32[]{:S(2)}) collective-permute-start(bf16[3,224,768]{2,1,0:T(8,128)(2,1)S(1)} %pad_maximum_fusion.rest_0_), channel_id=1, source_target_pairs={{0,96},{4,28},{8,104},{12,20},{16,112},{20,12},{24,120},{28,4},{32... | collective-permute-start | bytes 3096584 | tf_op jit(solution)/shard_map/ppermute | solution.py:701
  36.9 14.1 %collective-permute-start.5 = (bf16[3,224,768]{2,1,0:T(8,128)(2,1)S(1)}, bf16[3,224,768]{2,1,0:T(8,128)(2,1)S(1)}, u32[]{:S(2)}, u32[]{:S(2)}) collective-permute-start(bf16[3,224,768]{2,1,0:T(8,128)(2,1)S(1)} %pad_maximum_fusion.rest_0_), channel_id=1, source_target_pairs={{0,32},{4,12},{8,40},{12,4},{16,48},{20,28},{24,56},{28,20},{32,0}... | collective-permute-start | bytes 3096584 | tf_op jit(solution)/shard_map/ppermute | solution.py:701
  36.9 17.5 %all-to-all-start = ((bf16[4,2,64,768]{3,2,1,0:T(8,128)(2,1)}), bf16[4,2,64,768]{3,2,1,0:T(8,128)(2,1)S(1)}, u32[]{:S(2)}, u32[]{:S(2)}) async-start(bf16[4,2,64,768]{3,2,1,0:T(8,128)(2,1)} %get-tuple-element.90), calls=%async_computation | async-start | bytes 1572864 | tf_op jit(solution)/shard_map/all_to_all | solution.py:720
  41.2 13.2 %collective-permute-start.9 = (bf16[352,768]{1,0:T(8,128)(2,1)}, bf16[352,768]{1,0:T(8,128)(2,1)}, u32[]{:S(2)}, u32[]{:S(2)}) collective-permute-start(bf16[352,768]{1,0:T(8,128)(2,1)} %collective-permute-done.4.p1), channel_id=1, source_target_pairs={{0,4},{4,0},{1,5},{5,1},{2,6},{6,2},{3,7},{7,3},{8,12},{12,8},{9,1... | collective-permute-start | bytes 1622024 | tf_op jit(solution)/shard_map/ppermute | solution.py:705
  41.2 13.2 %collective-permute-start.8 = (bf16[352,768]{1,0:T(8,128)(2,1)}, bf16[352,768]{1,0:T(8,128)(2,1)}, u32[]{:S(2)}, u32[]{:S(2)}) collective-permute-start(bf16[352,768]{1,0:T(8,128)(2,1)} %collective-permute-done.3.p0), channel_id=1, source_target_pairs={{0,4},{4,0},{1,5},{5,1},{2,6},{6,2},{3,7},{7,3},{8,12},{12,8},{9,1... | collective-permute-start | bytes 1622024 | tf_op jit(solution)/shard_map/ppermute | solution.py:705
  41.7 12.7 %collective-permute-start.10 = (bf16[352,768]{1,0:T(8,128)(2,1)}, bf16[352,768]{1,0:T(8,128)(2,1)}, u32[]{:S(2)}, u32[]{:S(2)}) collective-permute-start(bf16[352,768]{1,0:T(8,128)(2,1)} %collective-permute-done.7.p2), channel_id=1, source_target_pairs={{0,4},{4,0},{1,5},{5,1},{2,6},{6,2},{3,7},{7,3},{8,12},{12,8},{9,1... | collective-permute-start | bytes 1622024 | tf_op jit(solution)/shard_map/ppermute | solution.py:705
  51.0 14.0 %collective-permute-start.12 = (bf16[3,96,768]{2,1,0:T(8,128)(2,1)}, bf16[3,96,768]{2,1,0:T(8,128)(2,1)}, u32[]{:S(2)}, u32[]{:S(2)}) collective-permute-start(bf16[3,96,768]{2,1,0:T(8,128)(2,1)} %slice.125), channel_id=1, source_target_pairs={{0,32},{4,12},{8,40},{12,4},{16,48},{20,28},{24,56},{28,20},{32,0}... | collective-permute-start | bytes 1327112 | tf_op jit(solution)/shard_map/ppermute | solution.py:701
  51.9 13.2 %collective-permute-start.11 = (bf16[3,128,768]{2,1,0:T(8,128)(2,1)}, bf16[3,128,768]{2,1,0:T(8,128)(2,1)}, u32[]{:S(2)}, u32[]{:S(2)}) collective-permute-start(bf16[3,128,768]{2,1,0:T(8,128)(2,1)} %slice.124), channel_id=1, source_target_pairs={{0,96},{4,28},{8,104},{12,20},{16,112},{20,12},{24,120},{28,4},{32... | collective-permute-start | bytes 1769480 | tf_op jit(solution)/shard_map/ppermute | solution.py:701
  95.2 19.8 %collective-permute-start.20 = (bf16[2,4,128,768]{3,2,1,0:T(8,128)(2,1)S(1)}, bf16[2,4,128,768]{3,2,1,0:T(8,128)(2,1)S(1)}, u32[]{:S(2)}, u32[]{:S(2)}) collective-permute-start(bf16[2,4,128,768]{3,2,1,0:T(8,128)(2,1)S(1)} %add_convert_fusion), channel_id=1, source_target_pairs={{0,32},{4,12},{8,40},{12,4},{16,48},{20,28},{24,56},{28,20},{32,0}... | collective-permute-start | bytes 4718600 | tf_op jit(solution)/shard_map/ppermute | solution.py:701
  98.5 16.6 %collective-permute-start.21 = (bf16[2,4,96,768]{3,2,1,0:T(8,128)(2,1)S(1)}, bf16[2,4,96,768]{3,2,1,0:T(8,128)(2,1)S(1)}, u32[]{:S(2)}, u32[]{:S(2)}) collective-permute-start(bf16[2,4,96,768]{3,2,1,0:T(8,128)(2,1)S(1)} %add_convert_fusion.1), channel_id=1, source_target_pairs={{0,96},{4,28},{8,104},{12,20},{16,112},{20,12},{24,120},{28,4},{32... | collective-permute-start | bytes 3538952 | tf_op jit(solution)/shard_map/ppermute | solution.py:701
  120.0 15.3 %collective-permute-start.23 = (bf16[2,352,768]{2,1,0:T(8,128)(2,1)S(1)}, bf16[2,352,768]{2,1,0:T(8,128)(2,1)S(1)}, u32[]{:S(2)}, u32[]{:S(2)}) collective-permute-start(bf16[2,352,768]{2,1,0:T(8,128)(2,1)S(1)} %add_convert_fusion.2), channel_id=1, source_target_pairs={{0,1},{1,0},{2,3},{3,2},{4,7},{5,6},{6,5},{7,4},{8,9},{9,8},{10,11... | collective-permute-start | bytes 3244040 | tf_op jit(solution)/shard_map/ppermute | solution.py:690
  123.1 12.1 %collective-permute-start.24 = (bf16[4,128,768]{2,1,0:T(8,128)(2,1)S(1)}, bf16[4,128,768]{2,1,0:T(8,128)(2,1)S(1)}, u32[]{:S(2)}, u32[]{:S(2)}) collective-permute-start(bf16[4,128,768]{2,1,0:T(8,128)(2,1)S(1)} %fusion.3), channel_id=1, source_target_pairs={{0,96},{4,28},{8,104},{12,20},{16,112},{20,12},{24,120},{28,4},{32... | collective-permute-start | bytes 2359304 | tf_op jit(solution)/shard_map/ppermute | solution.py:701
  136.8 16.4 %collective-permute-start.28 = (bf16[2,224,768]{2,1,0:T(8,128)(2,1)S(1)}, bf16[2,224,768]{2,1,0:T(8,128)(2,1)S(1)}, u32[]{:S(2)}, u32[]{:S(2)}) collective-permute-start(bf16[2,224,768]{2,1,0:T(8,128)(2,1)S(1)} %fusion.4), channel_id=1, source_target_pairs={{0,1},{1,0},{2,3},{3,2},{4,7},{5,6},{6,5},{7,4},{8,9},{9,8},{10,11... | collective-permute-start | bytes 2064392 | tf_op jit(solution)/shard_map/ppermute | solution.py:690
  145.5 14.2 %collective-permute-start.27 = (bf16[352,768]{1,0:T(8,128)(2,1)S(1)}, bf16[352,768]{1,0:T(8,128)(2,1)S(1)}, u32[]{:S(2)}, u32[]{:S(2)}) collective-permute-start(bf16[352,768]{1,0:T(8,128)(2,1)S(1)} %fusion.2), channel_id=1, source_target_pairs={{0,8},{4,36},{8,0},{12,44},{16,24},{20,52},{24,16},{28,60},{32,40}... | collective-permute-start | bytes 1622024 | tf_op jit(solution)/shard_map/ppermute | solution.py:701
  178.2 14.6 %collective-permute-start.34 = (bf16[352,768]{1,0:T(8,128)(2,1)S(1)}, bf16[352,768]{1,0:T(8,128)(2,1)}, u32[]{:S(2)}, u32[]{:S(2)}) collective-permute-start(bf16[352,768]{1,0:T(8,128)(2,1)S(1)} %add_convert_fusion.6), channel_id=1, source_target_pairs={{0,96},{4,28},{8,104},{12,20},{16,112},{20,12},{24,120},{28,4},{32... | collective-permute-start | bytes 1622024 | tf_op jit(solution)/shard_map/ppermute | solution.py:701
  180.4 16.2 %all-to-all-start.1 = ((bf16[4,2,64,768]{3,2,1,0:T(8,128)(2,1)}), bf16[4,2,64,768]{3,2,1,0:T(8,128)(2,1)S(1)}, u32[]{:S(2)}, u32[]{:S(2)}) async-start(bf16[4,2,64,768]{3,2,1,0:T(8,128)(2,1)} %get-tuple-element.148), calls=%async_computation.1 | async-start | bytes 1572864 | tf_op jit(solution)/shard_map/all_to_all | solution.py:720
  184.3 12.4 %collective-permute-start.37 = (bf16[224,768]{1,0:T(8,128)(2,1)S(1)}, bf16[224,768]{1,0:T(8,128)(2,1)S(1)}, u32[]{:S(2)}, u32[]{:S(2)}) collective-permute-start(bf16[224,768]{1,0:T(8,128)(2,1)S(1)} %add_convert_fusion.10), channel_id=1, source_target_pairs={{0,96},{4,28},{8,104},{12,20},{16,112},{20,12},{24,120},{28,4},{32... | collective-permute-start | bytes 1032200 | tf_op jit(solution)/shard_map/ppermute | solution.py:701
  184.8 11.5 %collective-permute-start.36 = (bf16[224,768]{1,0:T(8,128)(2,1)S(1)}, bf16[224,768]{1,0:T(8,128)(2,1)S(1)}, u32[]{:S(2)}, u32[]{:S(2)}) collective-permute-start(bf16[224,768]{1,0:T(8,128)(2,1)S(1)} %add_convert_fusion.10), channel_id=1, source_target_pairs={{0,64},{4,20},{8,72},{12,28},{16,80},{20,4},{24,88},{28,12},{32,96... | collective-permute-start | bytes 1032200 | tf_op jit(solution)/shard_map/ppermute | solution.py:701
  196.7 10.7 %collective-permute-start.38 = (bf16[1248,768]{1,0:T(8,128)(2,1)S(1)}, bf16[1248,768]{1,0:T(8,128)(2,1)S(1)}, u32[]{:S(2)}, u32[]{:S(2)}) collective-permute-start(bf16[1248,768]{1,0:T(8,128)(2,1)S(1)} %constant_dynamic-update-slice_fusion.mine), channel_id=1, source_target_pairs={{0,4},{4,0},{1,5},{5,1},{2,6},{6,2},{3,7},{7,3},{8,12},{12,8},{9,1... | collective-permute-start | bytes 5750792 | tf_op jit(solution)/shard_map/ppermute | solution.py:705
  (24 other events, 188.5 us)

commit v4 on v3

--- a/solution.py
+++ b/solution.py
@@ -176,6 +176,28 @@
     )(coords, lengths, hidden, grad_out, *own_first, *own_second, norm_block)
 
 
+def cut_body(near_ref, far_ref, outer_ref, inner_ref, sem):
+    copies = Copies(sem)
+    copies.add(near_ref.at[:, pl.ds(0, QUARTER)], outer_ref)
+    copies.add(far_ref.at[:, pl.ds(QUARTER, HALF)], inner_ref)
+    copies.start()
+    copies.wait()
+
+
+def cut(near, far):
+    shape = jax.ShapeDtypeStruct
+    full, anywhere = pl.BlockSpec(memory_space=pltpu.VMEM), pl.BlockSpec(memory_space=pl.ANY)
+    return pl.pallas_call(
+        cut_body,
+        out_shape=(shape((3, QUARTER, D), LOW), shape((3, HALF, D), LOW)),
+        in_specs=[anywhere] * 2,
+        out_specs=(full, full),
+        scratch_shapes=[pltpu.SemaphoreType.DMA((2,))],
+        compiler_params=pltpu.CompilerParams(vmem_limit_bytes=4 * MIB),
+        name="cut",
+    )(near, far)
+
+
 def load_first(meta_ref, copies, own, pieces, w_ref):
     x, core = meta_ref[X], meta_ref[CORE]
     near, far = x ^ near_of(core), x ^ far_of(core)
@@ -744,7 +766,7 @@
     base_near, base_far = hop_yz(base, 1), hop_yz(base, 3)
     across = hop_x(near, FAR)
     pieces = (near, far, across, swap(near), swap(far), swap(across))
-    part_outer, part_inner = base_near[:, :QUARTER], base_far[:, QUARTER:]
+    part_outer, part_inner = cut(base_near, base_far)
     rows = after(rows, part_outer, part_inner)
     across_outer, across_inner = hop_yz(part_outer, 3), hop_yz(part_inner, 1)
     tok, *saved, relw, probs, ctx = attend_forward(meta, bucket_column, rows, own_halves, pieces)

time: 215 us -> 214 us (level)
  local copies, waits for them, and re-layouts: 3.74 us -> 1.07 us
  waiting for transfers between devices: 88.8 us -> 91 us
    slice x2 -> x0, local copies, waits for them, and re-layouts: 2.66 us -> none  [shards(): part_outer, part_inner = (base_near[:, :QUARTER], base_far[:, QUARTER:])]
  transfers between devices with their start and end apart: 41 -> 41, of which waited for: 24 -> 23; matrix products, arithmetic and copies ran while one was open for 3% -> 2% of each run, Pallas kernels for 16% -> 17%
where the time goes in v4:
time: 214 us; the launch traced here: 210 us
  waiting for transfers between devices  91 us (43%)
  Pallas kernels  59.3 us (28%)
  starting transfers between devices  51.7 us (24%)
  other arithmetic  6.25 us (3%)
    ppermute x10, waiting for transfers between devices, hop_x(): return lax.ppermute(value, ('core', 'shard'), pairs)  42 us
    ppermute x17, waiting for transfers between devices, hop_yz(): return lax.ppermute(value, ('y', 'z', 'core'), pairs)  38.9 us
    ppermute x17, starting transfers between devices, hop_yz(): return lax.ppermute(value, ('y', 'z', 'core'), pairs)  25.3 us
    pallas_call x1, Pallas kernels, feed(): pl.pallas_call(feed_body, out_shape=(shape((ROWS, D), LOW), shape((ROWS,...  16.5 us
    pallas_call x1, Pallas kernels, attend_back_two(): pl.pallas_call(attend_back_two_body, out_shape=(shape((GROUP, 2, PART, D)...  12.8 us
    pallas_call x1, Pallas kernels, attend_forward(): pl.pallas_call(attend_forward_body, out_shape=(*(shape((ROWS, D), LOW),)...  10.7 us
    ppermute x12, waiting for transfers between devices, swap(): return lax.ppermute(value, 'core', [(0, 1), (1, 0)])  10.1 us
    ppermute x10, starting transfers between devices, hop_x(): return lax.ppermute(value, ('core', 'shard'), pairs)  9.25 us
  transfers between devices with their start and end apart: 41, of which 23 were waited for; matrix products, arithmetic and copies ran while one was open for 2% of the time, Pallas kernels for 17%

profile of v4, /device:TPU:17, one launch (start us, length us, event | category | flops | bytes accessed | tf_op | source)
XLA Modules:
  0.0 210.3 jit_solution(12008745824609226894)
XLA Ops:
  10.4 4.2 %collective-permute-done = bf16[224,768]{1,0:T(8,128)(2,1)S(1)} collective-permute-done((bf16[224,768]{1,0:T(8,128)(2,1)}, bf16[224,768]{1,0:T(8,128)(2,1)S(1)}, u32[]{:S(2)}, u32[]{:S(2)}) %collective-permute-start) | collective-permute-done | bytes 344096 | tf_op jit(solution)/shard_map/ppermute | solution.py:712
  14.6 11.5 %collective-permute-done.3.p0 = bf16[352,768]{1,0:T(8,128)(2,1)} collective-permute-done((bf16[352,768]{1,0:T(8,128)(2,1)}, bf16[352,768]{1,0:T(8,128)(2,1)}, u32[]{:S(2)}, u32[]{:S(2)}) %collective-permute-start.3) | collective-permute-done | bytes 540704 | tf_op jit(solution)/shard_map/ppermute | solution.py:712
  29.3 3.7 %collective-permute-done.2 = bf16[224,768]{1,0:T(8,128)(2,1)S(1)} collective-permute-done((bf16[224,768]{1,0:T(8,128)(2,1)S(1)}, bf16[224,768]{1,0:T(8,128)(2,1)S(1)}, u32[]{:S(2)}, u32[]{:S(2)}) %collective-permute-start.2) | collective-permute-done | bytes 344096 | tf_op jit(solution)/shard_map/ppermute | solution.py:712
  33.1 3.8 %collective-permute-start.6 = (bf16[3,224,768]{2,1,0:T(8,128)(2,1)S(1)}, bf16[3,224,768]{2,1,0:T(8,128)(2,1)S(1)}, u32[]{:S(2)}, u32[]{:S(2)}) collective-permute-start(bf16[3,224,768]{2,1,0:T(8,128)(2,1)S(1)} %pad_maximum_fusion.rest_0_), channel_id=1, source_target_pairs={{0,96},{4,28},{8,104},{12,20},{16,112},{20,12},{24,120},{28,4},{32... | collective-permute-start | bytes 3096584 | tf_op jit(solution)/shard_map/ppermute | solution.py:723
  36.9 4.3 %all-to-all-start = ((bf16[4,2,64,768]{3,2,1,0:T(8,128)(2,1)}), bf16[4,2,64,768]{3,2,1,0:T(8,128)(2,1)}, u32[]{:S(2)}, u32[]{:S(2)}) async-start(bf16[4,2,64,768]{3,2,1,0:T(8,128)(2,1)} %get-tuple-element.92), calls=%async_computation | async-start | bytes 1572864 | tf_op jit(solution)/shard_map/all_to_all | solution.py:742
  42.4 7.0 %collective-permute-done.6.far_ref.rest_2_ = bf16[3,224,768]{2,1,0:T(8,128)(2,1)S(1)} collective-permute-done((bf16[3,224,768]{2,1,0:T(8,128)(2,1)S(1)}, bf16[3,224,768]{2,1,0:T(8,128)(2,1)S(1)}, u32[]{:S(2)}, u32[]{:S(2)}) %collective-permute-start.6) | collective-permute-done | bytes 1032224 | tf_op jit(solution)/shard_map/ppermute | solution.py:723
  53.3 10.7 %attend_forward.1 = (bf16[256,768]{1,0:T(8,128)(2,1)S(1)}, bf16[256,768]{1,0:T(8,128)(2,1)S(1)}, bf16[256,768]{1,0:T(8,128)(2,1)S(1)}, bf16[256,768]{1,0:T(8,128...) custom-call(s32[16]{0:T(128)S(1)} %copy-done.4, ...), custom_call_target="tpu_custom_call" | custom-call | flops 12000000000 | bytes 40000000 | tf_op jit(solution)/shard_map/attend_forward/pallas_call | solution.py:316
  65.2 5.5 %attend_forward_two.1 = (bf16[6,256,256]{2,1,0:T(8,128)(2,1)S(1)}, bf16[256,384]{1,0:T(8,128)(2,1)S(1)}) custom-call(s32[16]{0:T(128)S(1)} %copy-done.4, bf16[256,768]{1,0:T(8,128)(2,1)S(1)} %get-tuple-element.99.q_ref, bf16[256,768]{1,0:T(8,128)(2,1)S(1)} %get-tuple-element.100.k_ref, bf16[256,768]{1,0:T(8,128)(2,1)S(1)} %get-tuple-element.101.v_ref, ...), custom_call_target="tpu_custom_call" | custom-call | flops 8000000000 | bytes 20000000 | tf_op jit(solution)/shard_map/attend_forward_two/pallas_call | solution.py:337
  71.2 16.5 %feed.1 = (bf16[256,768]{1,0:T(8,128)(2,1)S(1)}, bf16[256,768]{1,0:T(8,128)(2,1)S(1)}, f32[256,768]{1,0:T(8,128)S(1)}, bf16[4,4,128,768]{3,2,1,0:T(8,128)(2,1)S(...) custom-call(s32[16]{0:T(128)S(1)} %copy-done.4, ...), custom_call_target="tpu_custom_call" | custom-call | flops 16000000000 | bytes 60000000 | tf_op jit(solution)/shard_map/feed/pallas_call | solution.py:627
  88.3 4.7 %attend_back_one.1 = (bf16[256,384]{1,0:T(8,128)(2,1)S(1)}, bf16[256,384]{1,0:T(8,128)(2,1)S(1)}, bf16[256,384]{1,0:T(8,128)(2,1)S(1)}, bf16[512,384]{1,0:T(8,128)(2,1)S(1)}, bf16[512,384]{1,0:T(8,128)(2,1)S(1)}) custom-call(bf16[256,768]{1,0:T(8,128)(2,1)S(1)} %get-tuple-element.99.q_ref, bf16[256,768]{1,0:T(8,128)(2,1)S(1)} %get-tuple-element.100.k_ref, ...), custom_call_target="tpu_custom_call" | custom-call | flops 8000000000 | bytes 20000000 | tf_op jit(solution)/shard_map/attend_back_one/pallas_call | solution.py:470
  97.2 3.7 %collective-permute-start.21 = (bf16[2,4,96,768]{3,2,1,0:T(8,128)(2,1)S(1)}, bf16[2,4,96,768]{3,2,1,0:T(8,128)(2,1)S(1)}, u32[]{:S(2)}, u32[]{:S(2)}) collective-permute-start(bf16[2,4,96,768]{3,2,1,0:T(8,128)(2,1)S(1)} %add_convert_fusion.1), channel_id=1, source_target_pairs={{0,96},{4,28},{8,104},{12,20},{16,112},{20,12},{24,120},{28,4},{32... | collective-permute-start | bytes 3538952 | tf_op jit(solution)/shard_map/ppermute | solution.py:723
  100.9 12.8 %attend_back_two.1 = (bf16[4,2,64,768]{3,2,1,0:T(8,128)(2,1)}, bf16[4,352,768]{2,1,0:T(8,128)(2,1)S(1)}, bf16[4,352,768]{2,1,0:T(8,128)(2,1)S(1)}) custom-call(s32[16]{0:T(128)S(1)} %copy-done.4, bf16[256,768]{1,0:T(8,128)(2,1)S(1)} %get-tuple-element.99.q_ref, bf16[256,768]{1,0:T(8,128)(2,1)S(1)} %get-tuple-element.100.k_ref, ...), custom_call_target="tpu_custom_call" | custom-call | flops 14000000000 | bytes 40000000 | tf_op jit(solution)/shard_map/attend_back_two/pallas_call | solution.py:485
  114.5 4.2 %collective-permute-done.22 = bf16[4,352,768]{2,1,0:T(8,128)(2,1)S(1)} collective-permute-done((bf16[4,352,768]{2,1,0:T(8,128)(2,1)S(1)}, bf16[4,352,768]{2,1,0:T(8,128)(2,1)S(1)}, u32[]{:S(2)}, u32[]{:S(2)}) %collective-permute-start.22) | collective-permute-done | bytes 2162720 | tf_op jit(solution)/shard_map/ppermute | solution.py:727
  125.6 8.7 %collective-permute-done.25 = bf16[4,96,768]{2,1,0:T(8,128)(2,1)S(1)} collective-permute-done((bf16[4,96,768]{2,1,0:T(8,128)(2,1)S(1)}, bf16[4,96,768]{2,1,0:T(8,128)(2,1)S(1)}, u32[]{:S(2)}, u32[]{:S(2)}) %collective-permute-start.25) | collective-permute-done | bytes 589856 | tf_op jit(solution)/shard_map/ppermute | solution.py:723
  137.9 7.5 %collective-permute-done.26 = bf16[352,768]{1,0:T(8,128)(2,1)S(1)} collective-permute-done((bf16[352,768]{1,0:T(8,128)(2,1)S(1)}, bf16[352,768]{1,0:T(8,128)(2,1)S(1)}, u32[]{:S(2)}, u32[]{:S(2)}) %collective-permute-start.26) | collective-permute-done | bytes 540704 | tf_op jit(solution)/shard_map/ppermute | solution.py:712
  146.3 5.6 %collective-permute-done.28 = bf16[2,224,768]{2,1,0:T(8,128)(2,1)S(1)} collective-permute-done((bf16[2,224,768]{2,1,0:T(8,128)(2,1)S(1)}, bf16[2,224,768]{2,1,0:T(8,128)(2,1)S(1)}, u32[]{:S(2)}, u32[]{:S(2)}) %collective-permute-start.28) | collective-permute-done | bytes 688160 | tf_op jit(solution)/shard_map/ppermute | solution.py:712
  152.1 6.4 %collective-permute-done.29 = bf16[224,768]{1,0:T(8,128)(2,1)S(1)} collective-permute-done((bf16[224,768]{1,0:T(8,128)(2,1)S(1)}, bf16[224,768]{1,0:T(8,128)(2,1)S(1)}, u32[]{:S(2)}, u32[]{:S(2)}) %collective-permute-start.29) | collective-permute-done | bytes 344096 | tf_op jit(solution)/shard_map/ppermute | solution.py:712
  161.4 5.1 %collective-permute-done.31 = bf16[224,768]{1,0:T(8,128)(2,1)S(1)} collective-permute-done((bf16[224,768]{1,0:T(8,128)(2,1)S(1)}, bf16[224,768]{1,0:T(8,128)(2,1)S(1)}, u32[]{:S(2)}, u32[]{:S(2)}) %collective-permute-start.31) | collective-permute-done | bytes 344096 | tf_op jit(solution)/shard_map/ppermute | solution.py:723
  170.3 4.9 %collective-permute-done.33 = bf16[224,768]{1,0:T(8,128)(2,1)S(1)} collective-permute-done((bf16[224,768]{1,0:T(8,128)(2,1)S(1)}, bf16[224,768]{1,0:T(8,128)(2,1)S(1)}, u32[]{:S(2)}, u32[]{:S(2)}) %collective-permute-start.33) | collective-permute-done | bytes 344096 | tf_op jit(solution)/shard_map/ppermute | solution.py:723
  179.7 3.7 %all-to-all-start.1 = ((bf16[4,2,64,768]{3,2,1,0:T(8,128)(2,1)}), bf16[4,2,64,768]{3,2,1,0:T(8,128)(2,1)S(1)}, u32[]{:S(2)}, u32[]{:S(2)}) async-start(bf16[4,2,64,768]{3,2,1,0:T(8,128)(2,1)} %get-tuple-element.152), calls=%async_computation.1 | async-start | bytes 1572864 | tf_op jit(solution)/shard_map/all_to_all | solution.py:742
  189.1 6.5 %collective-permute-done.35 = bf16[224,768]{1,0:T(8,128)(2,1)S(1)} collective-permute-done((bf16[224,768]{1,0:T(8,128)(2,1)S(1)}, bf16[224,768]{1,0:T(8,128)(2,1)S(1)}, u32[]{:S(2)}, u32[]{:S(2)}) %collective-permute-start.35) | collective-permute-done | bytes 344096 | tf_op jit(solution)/shard_map/ppermute | solution.py:723
  195.7 6.6 %collective-permute-start.38 = (bf16[1248,768]{1,0:T(8,128)(2,1)S(1)}, bf16[1248,768]{1,0:T(8,128)(2,1)S(1)}, u32[]{:S(2)}, u32[]{:S(2)}) collective-permute-start(bf16[1248,768]{1,0:T(8,128)(2,1)S(1)} %constant_dynamic-update-slice_fusion.mine), channel_id=1, source_target_pairs={{0,4},{4,0},{1,5},{5,1},{2,6},{6,2},{3,7},{7,3},{8,12},{12,8},{9,1... | collective-permute-start | bytes 5750792 | tf_op jit(solution)/shard_map/ppermute | solution.py:727
  202.3 3.5 %collective-permute-done.38.other = bf16[1248,768]{1,0:T(8,128)(2,1)S(1)} collective-permute-done((bf16[1248,768]{1,0:T(8,128)(2,1)S(1)}, bf16[1248,768]{1,0:T(8,128)(2,1)S(1)}, u32[]{:S(2)}, u32[]{:S(2)}) %collective-permute-start.38) | collective-permute-done | bytes 1916960 | tf_op jit(solution)/shard_map/ppermute | solution.py:727
  205.8 4.5 %finish.1 = (f32[192,768]{1,0:T(8,128)}, f32[192,768]{1,0:T(8,128)}, f32[192,768]{1,0:T(8,128)}, f32[128,768]{1,0:T(8,128)}, f32[768,768]{1,0:T(8,128)}, /*index...) custom-call(s32[16]{0:T(128)S(1)} %copy-done.4, ...), custom_call_target="tpu_custom_call" | custom-call | tf_op jit(solution)/shard_map/finish/pallas_call | solution.py:691
  (109 shorter events, 53.5 us)
Async XLA Ops:
  8.7 17.4 %collective-permute-start.3 = (bf16[352,768]{1,0:T(8,128)(2,1)}, bf16[352,768]{1,0:T(8,128)(2,1)}, u32[]{:S(2)}, u32[]{:S(2)}) collective-permute-start(bf16[352,768]{1,0:T(8,128)(2,1)} %get-tuple-element.94), channel_id=1, source_target_pairs={{0,1},{1,0},{2,3},{3,2},{4,7},{5,6},{6,5},{7,4},{8,9},{9,8},{10,11... | collective-permute-start | bytes 1622024 | tf_op jit(solution)/shard_map/ppermute | solution.py:712
  8.9 24.1 %collective-permute-start.4 = (bf16[352,768]{1,0:T(8,128)(2,1)}, bf16[352,768]{1,0:T(8,128)(2,1)}, u32[]{:S(2)}, u32[]{:S(2)}) collective-permute-start(bf16[352,768]{1,0:T(8,128)(2,1)} %get-tuple-element.94), channel_id=1, source_target_pairs={{0,3},{1,2},{2,1},{3,0},{4,5},{5,4},{6,7},{7,6},{8,11},{9,10},{10,... | collective-permute-start | bytes 1622024 | tf_op jit(solution)/shard_map/ppermute | solution.py:712
  8.9 20.3 %collective-permute-start.1 = (bf16[224,768]{1,0:T(8,128)(2,1)}, bf16[224,768]{1,0:T(8,128)(2,1)S(1)}, u32[]{:S(2)}, u32[]{:S(2)}) collective-permute-start(bf16[224,768]{1,0:T(8,128)(2,1)} %get-tuple-element.93), channel_id=1, source_target_pairs={{0,3},{1,2},{2,1},{3,0},{4,5},{5,4},{6,7},{7,6},{8,11},{9,10},{10,... | collective-permute-start | bytes 1032200 | tf_op jit(solution)/shard_map/ppermute | solution.py:712
  14.6 18.3 %collective-permute-start.2 = (bf16[224,768]{1,0:T(8,128)(2,1)S(1)}, bf16[224,768]{1,0:T(8,128)(2,1)S(1)}, u32[]{:S(2)}, u32[]{:S(2)}) collective-permute-start(bf16[224,768]{1,0:T(8,128)(2,1)S(1)} %collective-permute-done), channel_id=1, source_target_pairs={{0,3},{1,2},{2,1},{3,0},{4,5},{5,4},{6,7},{7,6},{8,11},{9,10},{10,... | collective-permute-start | bytes 1032200 | tf_op jit(solution)/shard_map/ppermute | solution.py:712
  26.1 15.7 %collective-permute-start.7 = (bf16[352,768]{1,0:T(8,128)(2,1)}, bf16[352,768]{1,0:T(8,128)(2,1)}, u32[]{:S(2)}, u32[]{:S(2)}) collective-permute-start(bf16[352,768]{1,0:T(8,128)(2,1)} %collective-permute-done.3.p0), channel_id=1, source_target_pairs={{0,3},{1,2},{2,1},{3,0},{4,5},{5,4},{6,7},{7,6},{8,11},{9,10},{10,... | collective-permute-start | bytes 1622024 | tf_op jit(solution)/shard_map/ppermute | solution.py:712
  33.1 16.3 %collective-permute-start.6 = (bf16[3,224,768]{2,1,0:T(8,128)(2,1)S(1)}, bf16[3,224,768]{2,1,0:T(8,128)(2,1)S(1)}, u32[]{:S(2)}, u32[]{:S(2)}) collective-permute-start(bf16[3,224,768]{2,1,0:T(8,128)(2,1)S(1)} %pad_maximum_fusion.rest_0_), channel_id=1, source_target_pairs={{0,96},{4,28},{8,104},{12,20},{16,112},{20,12},{24,120},{28,4},{32... | collective-permute-start | bytes 3096584 | tf_op jit(solution)/shard_map/ppermute | solution.py:723
  36.9 13.9 %collective-permute-start.5 = (bf16[3,224,768]{2,1,0:T(8,128)(2,1)S(1)}, bf16[3,224,768]{2,1,0:T(8,128)(2,1)S(1)}, u32[]{:S(2)}, u32[]{:S(2)}) collective-permute-start(bf16[3,224,768]{2,1,0:T(8,128)(2,1)S(1)} %pad_maximum_fusion.rest_0_), channel_id=1, source_target_pairs={{0,32},{4,12},{8,40},{12,4},{16,48},{20,28},{24,56},{28,20},{32,0}... | collective-permute-start | bytes 3096584 | tf_op jit(solution)/shard_map/ppermute | solution.py:723
  36.9 16.4 %all-to-all-start = ((bf16[4,2,64,768]{3,2,1,0:T(8,128)(2,1)}), bf16[4,2,64,768]{3,2,1,0:T(8,128)(2,1)}, u32[]{:S(2)}, u32[]{:S(2)}) async-start(bf16[4,2,64,768]{3,2,1,0:T(8,128)(2,1)} %get-tuple-element.92), calls=%async_computation | async-start | bytes 1572864 | tf_op jit(solution)/shard_map/all_to_all | solution.py:742
  41.3 12.0 %collective-permute-start.9 = (bf16[352,768]{1,0:T(8,128)(2,1)}, bf16[352,768]{1,0:T(8,128)(2,1)}, u32[]{:S(2)}, u32[]{:S(2)}) collective-permute-start(bf16[352,768]{1,0:T(8,128)(2,1)} %collective-permute-done.4.p1), channel_id=1, source_target_pairs={{0,4},{4,0},{1,5},{5,1},{2,6},{6,2},{3,7},{7,3},{8,12},{12,8},{9,1... | collective-permute-start | bytes 1622024 | tf_op jit(solution)/shard_map/ppermute | solution.py:727
  41.4 11.9 %collective-permute-start.8 = (bf16[352,768]{1,0:T(8,128)(2,1)}, bf16[352,768]{1,0:T(8,128)(2,1)}, u32[]{:S(2)}, u32[]{:S(2)}) collective-permute-start(bf16[352,768]{1,0:T(8,128)(2,1)} %collective-permute-done.3.p0), channel_id=1, source_target_pairs={{0,4},{4,0},{1,5},{5,1},{2,6},{6,2},{3,7},{7,3},{8,12},{12,8},{9,1... | collective-permute-start | bytes 1622024 | tf_op jit(solution)/shard_map/ppermute | solution.py:727
  41.9 11.4 %collective-permute-start.10 = (bf16[352,768]{1,0:T(8,128)(2,1)}, bf16[352,768]{1,0:T(8,128)(2,1)}, u32[]{:S(2)}, u32[]{:S(2)}) collective-permute-start(bf16[352,768]{1,0:T(8,128)(2,1)} %collective-permute-done.7.p2), channel_id=1, source_target_pairs={{0,4},{4,0},{1,5},{5,1},{2,6},{6,2},{3,7},{7,3},{8,12},{12,8},{9,1... | collective-permute-start | bytes 1622024 | tf_op jit(solution)/shard_map/ppermute | solution.py:727
  51.9 12.1 %collective-permute-start.12 = (bf16[3,96,768]{2,1,0:T(8,128)(2,1)}, bf16[3,96,768]{2,1,0:T(8,128)(2,1)}, u32[]{:S(2)}, u32[]{:S(2)}) collective-permute-start(bf16[3,96,768]{2,1,0:T(8,128)(2,1)} %get-tuple-element.97), channel_id=1, source_target_pairs={{0,32},{4,12},{8,40},{12,4},{16,48},{20,28},{24,56},{28,20},{32,0}... | collective-permute-start | bytes 1327112 | tf_op jit(solution)/shard_map/ppermute | solution.py:723
  52.0 12.0 %collective-permute-start.11 = (bf16[3,128,768]{2,1,0:T(8,128)(2,1)}, bf16[3,128,768]{2,1,0:T(8,128)(2,1)}, u32[]{:S(2)}, u32[]{:S(2)}) collective-permute-start(bf16[3,128,768]{2,1,0:T(8,128)(2,1)} %get-tuple-element.96), channel_id=1, source_target_pairs={{0,96},{4,28},{8,104},{12,20},{16,112},{20,12},{24,120},{28,4},{32... | collective-permute-start | bytes 1769480 | tf_op jit(solution)/shard_map/ppermute | solution.py:723
  93.9 20.6 %collective-permute-start.20 = (bf16[2,4,128,768]{3,2,1,0:T(8,128)(2,1)S(1)}, bf16[2,4,128,768]{3,2,1,0:T(8,128)(2,1)S(1)}, u32[]{:S(2)}, u32[]{:S(2)}) collective-permute-start(bf16[2,4,128,768]{3,2,1,0:T(8,128)(2,1)S(1)} %add_convert_fusion), channel_id=1, source_target_pairs={{0,32},{4,12},{8,40},{12,4},{16,48},{20,28},{24,56},{28,20},{32,0}... | collective-permute-start | bytes 4718600 | tf_op jit(solution)/shard_map/ppermute | solution.py:723
  97.2 17.3 %collective-permute-start.21 = (bf16[2,4,96,768]{3,2,1,0:T(8,128)(2,1)S(1)}, bf16[2,4,96,768]{3,2,1,0:T(8,128)(2,1)S(1)}, u32[]{:S(2)}, u32[]{:S(2)}) collective-permute-start(bf16[2,4,96,768]{3,2,1,0:T(8,128)(2,1)S(1)} %add_convert_fusion.1), channel_id=1, source_target_pairs={{0,96},{4,28},{8,104},{12,20},{16,112},{20,12},{24,120},{28,4},{32... | collective-permute-start | bytes 3538952 | tf_op jit(solution)/shard_map/ppermute | solution.py:723
  119.0 15.7 %collective-permute-start.23 = (bf16[2,352,768]{2,1,0:T(8,128)(2,1)S(1)}, bf16[2,352,768]{2,1,0:T(8,128)(2,1)S(1)}, u32[]{:S(2)}, u32[]{:S(2)}) collective-permute-start(bf16[2,352,768]{2,1,0:T(8,128)(2,1)S(1)} %add_convert_fusion.2), channel_id=1, source_target_pairs={{0,1},{1,0},{2,3},{3,2},{4,7},{5,6},{6,5},{7,4},{8,9},{9,8},{10,11... | collective-permute-start | bytes 3244040 | tf_op jit(solution)/shard_map/ppermute | solution.py:712
  121.9 12.8 %collective-permute-start.24 = (bf16[4,128,768]{2,1,0:T(8,128)(2,1)S(1)}, bf16[4,128,768]{2,1,0:T(8,128)(2,1)S(1)}, u32[]{:S(2)}, u32[]{:S(2)}) collective-permute-start(bf16[4,128,768]{2,1,0:T(8,128)(2,1)S(1)} %fusion.3), channel_id=1, source_target_pairs={{0,96},{4,28},{8,104},{12,20},{16,112},{20,12},{24,120},{28,4},{32... | collective-permute-start | bytes 2359304 | tf_op jit(solution)/shard_map/ppermute | solution.py:723
  134.9 10.5 %collective-permute-start.26 = (bf16[352,768]{1,0:T(8,128)(2,1)S(1)}, bf16[352,768]{1,0:T(8,128)(2,1)S(1)}, u32[]{:S(2)}, u32[]{:S(2)}) collective-permute-start(bf16[352,768]{1,0:T(8,128)(2,1)S(1)} %fusion.7), channel_id=1, source_target_pairs={{0,3},{1,2},{2,1},{3,0},{4,5},{5,4},{6,7},{7,6},{8,11},{9,10},{10,... | collective-permute-start | bytes 1622024 | tf_op jit(solution)/shard_map/ppermute | solution.py:712
  135.7 16.2 %collective-permute-start.28 = (bf16[2,224,768]{2,1,0:T(8,128)(2,1)S(1)}, bf16[2,224,768]{2,1,0:T(8,128)(2,1)S(1)}, u32[]{:S(2)}, u32[]{:S(2)}) collective-permute-start(bf16[2,224,768]{2,1,0:T(8,128)(2,1)S(1)} %fusion.4), channel_id=1, source_target_pairs={{0,1},{1,0},{2,3},{3,2},{4,7},{5,6},{6,5},{7,4},{8,9},{9,8},{10,11... | collective-permute-start | bytes 2064392 | tf_op jit(solution)/shard_map/ppermute | solution.py:712
  145.7 12.8 %collective-permute-start.27 = (bf16[352,768]{1,0:T(8,128)(2,1)S(1)}, bf16[352,768]{1,0:T(8,128)(2,1)S(1)}, u32[]{:S(2)}, u32[]{:S(2)}) collective-permute-start(bf16[352,768]{1,0:T(8,128)(2,1)S(1)} %fusion.2), channel_id=1, source_target_pairs={{0,8},{4,36},{8,0},{12,44},{16,24},{20,52},{24,16},{28,60},{32,40}... | collective-permute-start | bytes 1622024 | tf_op jit(solution)/shard_map/ppermute | solution.py:723
  179.7 15.9 %all-to-all-start.1 = ((bf16[4,2,64,768]{3,2,1,0:T(8,128)(2,1)}), bf16[4,2,64,768]{3,2,1,0:T(8,128)(2,1)S(1)}, u32[]{:S(2)}, u32[]{:S(2)}) async-start(bf16[4,2,64,768]{3,2,1,0:T(8,128)(2,1)} %get-tuple-element.152), calls=%async_computation.1 | async-start | bytes 1572864 | tf_op jit(solution)/shard_map/all_to_all | solution.py:742
  183.6 12.1 %collective-permute-start.37 = (bf16[224,768]{1,0:T(8,128)(2,1)S(1)}, bf16[224,768]{1,0:T(8,128)(2,1)S(1)}, u32[]{:S(2)}, u32[]{:S(2)}) collective-permute-start(bf16[224,768]{1,0:T(8,128)(2,1)S(1)} %add_convert_fusion.10), channel_id=1, source_target_pairs={{0,96},{4,28},{8,104},{12,20},{16,112},{20,12},{24,120},{28,4},{32... | collective-permute-start | bytes 1032200 | tf_op jit(solution)/shard_map/ppermute | solution.py:723
  184.4 11.2 %collective-permute-start.36 = (bf16[224,768]{1,0:T(8,128)(2,1)S(1)}, bf16[224,768]{1,0:T(8,128)(2,1)S(1)}, u32[]{:S(2)}, u32[]{:S(2)}) collective-permute-start(bf16[224,768]{1,0:T(8,128)(2,1)S(1)} %add_convert_fusion.10), channel_id=1, source_target_pairs={{0,64},{4,20},{8,72},{12,28},{16,80},{20,4},{24,88},{28,12},{32,96... | collective-permute-start | bytes 1032200 | tf_op jit(solution)/shard_map/ppermute | solution.py:723
  185.0 10.6 %collective-permute-start.35 = (bf16[224,768]{1,0:T(8,128)(2,1)S(1)}, bf16[224,768]{1,0:T(8,128)(2,1)S(1)}, u32[]{:S(2)}, u32[]{:S(2)}) collective-permute-start(bf16[224,768]{1,0:T(8,128)(2,1)S(1)} %add_convert_fusion.10), channel_id=1, source_target_pairs={{0,32},{4,12},{8,40},{12,4},{16,48},{20,28},{24,56},{28,20},{32,0}... | collective-permute-start | bytes 1032200 | tf_op jit(solution)/shard_map/ppermute | solution.py:723
  (23 other events, 175.0 us)
